TPU v7x, 128 devices: a whole 4x4x4 slice. The times are simulated.
128 devices in a mesh: req: 4 (over z), blk: 32 (over y, x, core).
Axes of the slice: x: 4, y: 4, z: 4, core: 2. Of those that a mesh axis runs over, the one named last changes fastest.
Arguments:
- tree_input: bfloat16 [6144, 1280], P(('req', 'blk')), may hold values from -6 to 6
- cache: bfloat16 [4, 2, 65536, 1280], P('req', None, 'blk'), may hold values from -1200 to 1200, as said below
- page_table: int32 [4, 512], P('req'), may hold values from 0 to 511, each once within a row
- lengths: int32 [4, 32], P('req'), may hold values from 1 to 32768, 57344 in all within a row
- parents: int32 [128, 48], P(('req', 'blk')), may hold values from 0 to 29, as said below
- accept_leaf: int32 [4, 32], P('req'), may hold values from 0 to 47
- w_qkv: bfloat16 [1280, 3840], P(None, 'blk'), may hold values from -0.15625 to 0.15625
- w_out: bfloat16 [1280, 1280], P(None, 'blk'), may hold values from -0.15625 to 0.15625
- w_up: bfloat16 [1280, 1280], P(None, 'blk'), may hold values from -0.15625 to 0.15625
- w_down: bfloat16 [1280, 1280], P('blk'), may hold values from -0.15625 to 0.15625
- w_draft: bfloat16 [4, 1280, 1280], P(None, None, 'blk'), may hold values from -0.15625 to 0.15625
- w_patch: bfloat16 [1280, 1280], P(None, 'req'), may hold values from -0.15625 to 0.15625
Outputs:
- layer_out: bfloat16 [6144, 1280], P(('req', 'blk'))
- drafts: bfloat16 [4, 6144, 1280], P(None, ('req', 'blk'))
- cache_new: bfloat16 [4, 2, 65536, 1280], P('req', None, 'blk')
Inputs may be any that keep to these rules, and one draw needn't show every extreme that they name: `cache`: keys of the pool may hold a few rows of far larger size. `parents`: node 0 is its own parent. The nodes form 5 levels of sizes 1, 4, 10, 15, 18 in index order, and every other node's parent lies in the level before its own. `page_table`: row g holds the pool pages of group g; request r's pages are the npages_r entries after those of requests before it (see the steps), and page p is held by index p // 16 of blk.
All inputs are finite; a program needn't handle non-finite values.
Results may differ from a plain program's by a relative error of at most 0.018.
The roundings to bfloat16 on the way count: a program that leaves them out, or rounds other values in their place, can miss the bound.
Values may be sent and summed in bfloat16 or wider, within the bound.
A program may use at most 192 MiB of HBM per device.

v0:
```python
import math

import jax
import jax.numpy as jnp
from jax import lax
from jax.sharding import PartitionSpec as P

H = 16
HD = 80
TREE = 48
DEPTH = 5
PAGE = 128


EPS = 1e-06
NEG = -1e30
LEVEL_START = (0, 1, 5, 15, 30, 48)


def rms_rows(values):
    wide = values.astype(jnp.float32)
    return (wide * lax.rsqrt(jnp.mean(wide * wide, axis=-1, keepdims=True) + EPS)).astype(
        jnp.bfloat16
    )


def ancestors(parent_rows):
    nodes = jnp.arange(TREE, dtype=jnp.int32)
    current = jnp.broadcast_to(nodes, parent_rows.shape)
    marks = current[:, :, None] == nodes[None, None, :]
    for level in range(DEPTH - 1):
        current = jnp.take_along_axis(parent_rows, current, axis=1)
        marks = marks | (current[:, :, None] == nodes[None, None, :])
    return marks


def row_blocks(values, mapper):
    return mapper(lax.all_gather(values, "blk", axis=0, tiled=True), jnp.int32(0))


def column_blocks(values):
    return lax.all_to_all(values, "blk", split_axis=0, concat_axis=1, tiled=True)


def on_device(
    tree_input,
    cache,
    page_table,
    lengths,
    parents,
    accept_leaf,
    w_qkv,
    w_out,
    w_up,
    w_down,
    w_draft,
    w_patch,
):
    blocks = lax.axis_size("blk")
    myself = lax.axis_index("blk")
    tree_rows = tree_input.shape[0]
    width = tree_input.shape[1]
    requests = lengths.shape[1]
    pool_pages = cache.shape[2] // PAGE
    scale = 1.0 / math.sqrt(HD)
    normed = rms_rows(tree_input)

    def project_qkv(piece, start):
        return jnp.dot(piece, w_qkv, preferred_element_type=jnp.float32).astype(jnp.bfloat16)

    projected_part = row_blocks(normed, project_qkv)
    projected = column_blocks(projected_part)
    key_own = projected[:, width : 2 * width]
    value_own = projected[:, 2 * width :]
    query_all = lax.all_gather(projected[:, :width], "blk", axis=0, tiled=True)
    page_row = page_table[0]
    length_row = lengths[0]
    leaf_row = accept_leaf[0]
    total_pages = page_row.shape[0]
    npages = (length_row + DEPTH + PAGE - 1) // PAGE
    page_ends = jnp.cumsum(npages)
    offsets = page_ends - npages
    local_ids = myself * pool_pages + jnp.arange(pool_pages, dtype=jnp.int32)
    located = page_row[None, :] == local_ids[:, None]
    where_at = jnp.sum(
        jnp.where(located, jnp.arange(total_pages, dtype=jnp.int32)[None, :], 0), axis=1
    )
    owner = jnp.sum((page_ends[None, :] <= where_at[:, None]).astype(jnp.int32), axis=1)
    owner_hot = owner[:, None] == jnp.arange(requests, dtype=jnp.int32)[None, :]
    safe_owner = jnp.minimum(owner, requests - 1)
    page_len = jnp.sum(jnp.where(owner_hot, length_row[None, :], 0), axis=1)
    page_offset = jnp.sum(jnp.where(owner_hot, offsets[None, :], 0), axis=1)
    positions = (where_at - page_offset)[:, None] * PAGE + jnp.arange(PAGE, dtype=jnp.int32)[
        None, :
    ]
    valid = positions < page_len[:, None]
    query4 = query_all.reshape(requests, tree_rows, H, HD)
    query_page = jnp.take(query4, safe_owner, axis=0)
    keys = cache[0, 0].reshape(pool_pages, PAGE, H, HD)
    values = cache[0, 1].reshape(pool_pages, PAGE, H, HD)
    scores = (
        jnp.einsum("pqhd,pthd->pqht", query_page, keys, preferred_element_type=jnp.float32) * scale
    )
    masked = jnp.where(valid[:, None, None, :], scores, NEG)
    page_max = jnp.max(masked, axis=-1)
    request_max = jnp.max(jnp.where(owner_hot.T[:, :, None, None], page_max[None], NEG), axis=1)
    page_top = jnp.take(request_max, safe_owner, axis=0)
    weights = jnp.where(valid[:, None, None, :], jnp.exp(masked - page_top[..., None]), 0.0)
    page_den = jnp.sum(weights, axis=-1)
    page_num = jnp.einsum(
        "pqht,pthd->pqhd", weights.astype(jnp.bfloat16), values, preferred_element_type=jnp.float32
    )
    hot = owner_hot.astype(jnp.float32)
    den_part = jnp.einsum("pr,pqh->rqh", hot, page_den, precision=lax.Precision.HIGHEST)
    num_part = jnp.einsum("pr,pqhd->rqhd", hot, page_num, precision=lax.Precision.HIGHEST).reshape(
        requests, tree_rows, width
    )
    max_all = lax.pmax(request_max, "blk")
    factor = jnp.exp(request_max - max_all)
    den_scaled = den_part * factor
    num_scaled = (num_part.reshape(requests, tree_rows, H, HD) * factor[..., None]).reshape(
        requests, tree_rows, width
    )
    den_own, num_own = (
        lax.psum_scatter(den_scaled, "blk", scatter_dimension=0, tiled=True),
        lax.psum_scatter(num_scaled, "blk", scatter_dimension=0, tiled=True),
    )
    cache_top = lax.dynamic_slice_in_dim(max_all, myself, 1, 0)[0]
    cache_den = den_own[0]
    cache_num = num_own[0]
    marks = ancestors(parents)[0]
    query_own = lax.dynamic_slice_in_dim(query_all, myself * tree_rows, tree_rows, 0).reshape(
        tree_rows, H, HD
    )
    key_tree = key_own.reshape(tree_rows, H, HD)
    value_tree = value_own.reshape(tree_rows, H, HD)
    tree_scores = (
        jnp.einsum("qhd,khd->qhk", query_own, key_tree, preferred_element_type=jnp.float32) * scale
    )
    tree_masked = jnp.where(marks[:, None, :], tree_scores, NEG)
    row_top = jnp.maximum(cache_top, jnp.max(tree_masked, axis=-1))
    tree_weights = jnp.where(marks[:, None, :], jnp.exp(tree_masked - row_top[..., None]), 0.0)
    carried = jnp.exp(cache_top - row_top)
    denom = cache_den * carried + jnp.sum(tree_weights, axis=-1)
    numer = cache_num.reshape(tree_rows, H, HD) * carried[..., None] + jnp.einsum(
        "qhk,khd->qhd",
        tree_weights.astype(jnp.bfloat16),
        value_tree,
        preferred_element_type=jnp.float32,
    )
    attended = (numer / denom[..., None]).reshape(tree_rows, width).astype(jnp.bfloat16)

    def project_out(piece, start):
        return jnp.dot(piece, w_out, preferred_element_type=jnp.float32).astype(jnp.bfloat16)

    proj = column_blocks(row_blocks(attended, project_out))
    mid = (tree_input.astype(jnp.float32) + proj.astype(jnp.float32)).astype(jnp.bfloat16)

    def project_up(piece, start):
        return jax.nn.gelu(jnp.dot(piece, w_up, preferred_element_type=jnp.float32)).astype(
            jnp.bfloat16
        )

    hidden_all = row_blocks(rms_rows(mid), project_up)
    feedforward = lax.psum_scatter(
        jnp.dot(hidden_all, w_down, preferred_element_type=jnp.float32),
        "blk",
        scatter_dimension=0,
        tiled=True,
    )
    layer_out = (mid.astype(jnp.float32) + feedforward).astype(jnp.bfloat16)
    head_count = w_draft.shape[0]
    head_cols = w_draft.shape[2]

    def project_draft(piece, start):
        grown = jnp.einsum("nd,kdc->nkc", piece, w_draft, preferred_element_type=jnp.float32)
        return (
            jax.nn.silu(grown).astype(jnp.bfloat16).reshape(piece.shape[0], head_count * head_cols)
        )

    branch = column_blocks(row_blocks(rms_rows(layer_out), project_draft))
    branch = (
        branch.reshape(tree_rows, blocks, head_count, head_cols)
        .transpose(2, 0, 1, 3)
        .reshape(head_count, tree_rows, width)
    )
    drafted = (layer_out.astype(jnp.float32)[None] + branch.astype(jnp.float32)).astype(
        jnp.bfloat16
    )
    drafts = jnp.einsum(
        "krd,do->kro",
        drafted,
        lax.all_gather(w_patch, "req", axis=1, tiled=True),
        preferred_element_type=jnp.float32,
    ).astype(jnp.bfloat16)
    my_leaf = lax.dynamic_slice_in_dim(leaf_row, myself, 1, 0)
    chosen = jnp.take(marks, my_leaf, axis=0)[0]
    ranks = jnp.cumsum(chosen.astype(jnp.int32)) - 1
    picker = chosen[None, :] & (ranks[None, :] == jnp.arange(DEPTH, dtype=jnp.int32)[:, None])
    both_rows = jnp.concatenate([key_own, value_own], axis=1)
    send_rows = jnp.dot(
        picker.astype(jnp.bfloat16), both_rows, preferred_element_type=jnp.float32
    ).astype(jnp.bfloat16)
    received = lax.all_gather(send_rows, "blk", axis=0, tiled=True)
    level_marks = jnp.asarray(LEVEL_START[1:-1], jnp.int32)
    accepted_count = 1 + jnp.sum(
        (leaf_row[:, None] >= level_marks[None, :]).astype(jnp.int32), axis=1
    )
    steps_ahead = jnp.arange(DEPTH, dtype=jnp.int32)
    written = length_row[:, None] + steps_ahead[None, :]
    page_index = jnp.take(
        page_row, jnp.clip(offsets[:, None] + written // PAGE, 0, total_pages - 1)
    )
    keeper = (steps_ahead[None, :] < accepted_count[:, None]) & (page_index // pool_pages == myself)
    target = jnp.where(
        keeper, page_index % pool_pages * PAGE + written % PAGE, pool_pages * PAGE
    ).reshape(-1)
    new_keys = cache[0, 0].at[target].set(received[:, :width], mode="drop")
    new_values = cache[0, 1].at[target].set(received[:, width:], mode="drop")
    cache_new = jnp.stack([new_keys, new_values])[None]
    return (layer_out, drafts, cache_new)


def solution(mesh):
    in_specs = (
        P(("req", "blk"), None),
        P("req", None, "blk", None),
        P("req", None),
        P("req", None),
        P(("req", "blk"), None),
        P("req", None),
        P(None, "blk"),
        P(None, "blk"),
        P(None, "blk"),
        P("blk", None),
        P(None, None, "blk"),
        P(None, "req"),
    )
    out_specs = (
        P(("req", "blk"), None),
        P(None, ("req", "blk"), None),
        P("req", None, "blk", None),
    )
    return jax.shard_map(
        on_device, mesh=mesh, in_specs=in_specs, out_specs=out_specs, check_vma=False
    )
```

profile of v0, /device:TPU:2, one launch (start us, length us, event | category | flops | bytes accessed | tf_op | source)
XLA Modules:
  0.0 739.0 jit_solution(1722064064987440074)
XLA Ops:
  10.0 48.5 %all-gather.8.cloned.1.call-done = bf16[1536,1280]{1,0:T(8,128)(2,1)} async-done(((bf16[48,1280]{1,0:T(8,128)(2,1)}), bf16[1536,1280]{1,0:T(8,128)(2,1)}) %all-gather.8.cloned.1.call-update) | async-done | bytes 3932176 | tf_op jit(solution)/shard_map/all_gather | solution.py:38
  62.3 14.8 %all_to_all.45 = bf16[32,48,120]{2,1,0:T(8,128)(2,1)S(1)} all-to-all(bf16[32,48,120]{2,1,0:T(8,128)(2,1)S(1)} %bitcast.182), channel_id=1, replica_groups=mesh['req'=4,'blk'=32] {'blk'}, dimensions={0} | all-to-all | bytes 737280 | tf_op jit(solution)/shard_map/all_to_all | solution.py:42
  79.3 10.6 %slice_bitcast_fusion.1 = (bf16[2048,1280]{1,0:T(8,128)(2,1)}, bf16[2048,1280]{1,0:T(8,128)(2,1)}, bf16[1,1,2048,1280]{3,2,1,0:T(8,128)(2,1)}, bf16[1,1,2048,1280]{3,2,1,0:T(8,128)(2,1)}) fusion(bf16[1,2,2048,1280]{3,2,1,0:T(8,128)(2,1)} %param.16), kind=kLoop, calls=%fused_computation.218 | loop fusion | bytes 31457280 | tf_op jit(solution)/shard_map/squeeze | solution.py:218
  89.9 15.7 %reshape.1047 = bf16[16,128,16,80]{3,2,1,0:T(8,128)(2,1)} reshape(bf16[1,1,2048,1280]{3,2,1,0:T(8,128)(2,1)} %get-tuple-element.30) | data formatting | bytes 10485760 | tf_op jit(solution)/shard_map/reshape;squeeze | solution.py:99
  105.6 15.8 %reshape.1048 = bf16[16,128,16,80]{3,2,1,0:T(8,128)(2,1)} reshape(bf16[1,1,2048,1280]{3,2,1,0:T(8,128)(2,1)} %get-tuple-element.29) | data formatting | bytes 10485760 | tf_op jit(solution)/shard_map/reshape;squeeze | solution.py:100
  122.6 12.1 %reshape.896 = bf16[32,48,16,80]{3,2,1,0:T(8,128)(2,1)} reshape(bf16[1536,1280]{1,0:T(8,128)(2,1)} %all-gather.10.cloned.1.call-done) | data formatting | bytes 7864320 | tf_op jit(solution)/shard_map/reshape | solution.py:97
  142.3 10.6 %bitcast_reduce_fusion = (f32[16,48,16]{1,2,0:T(8,128)S(1)}, f32[16,16,48,128]{3,2,1,0:T(8,128)}) fusion(pred[16,128]{1,0:T(8,128)(4,1)S(1)} %add_compare_fusion, bf16[16,128,16,80]{3,2,1,0:T(8,128)(2,1)} %reshape.1047, bf16[16,48,16,80]{3,2,1,0:T(8,128)(2,1)S(1)} %broadcast_select_fusion), kind=kOutput, calls=%fused_computation.15 | convolution fusion | flops 256364544 | bytes 13551616 | tf_op jit(solution)/shard_map/pqhd,pthd->pqht/dot_general | solution.py:102
  155.6 9.4 %fusion.23 = f32[16,48,16,80]{3,1,2,0:T(8,128)} fusion(bf16[16,128,16,80]{3,2,1,0:T(8,128)(2,1)} %reshape.1048, f32[16,16,48,128]{3,2,1,0:T(8,128)} %get-tuple-element.38, f32[16,48,16]{1,2,0:T(8,128)S(1)} %broadcast_select_fusion.1, pred[16,128]{1,0:T(8,128)(4,1)S(1)} %add_compare_fusion), kind=kOutput, calls=%fused_computation.37 | convolution fusion | flops 259522560 | bytes 15517696 | tf_op jit(solution)/shard_map/pqht,pthd->pqhd/dot_general | solution.py:110
  168.7 87.2 %all-reduce.2.cloned.1.call-done = f32[32,48,16]{1,0,2:T(8,128)} async-done(((f32[32,48,16]{1,0,2:T(8,128)}), f32[32,48,16]{1,0,2:T(8,128)}) %all-reduce.2.cloned.1.call-update) | async-done | bytes 98320 | tf_op jit(solution)/shard_map/pmax | solution.py:118
  258.5 13.2 %broadcast_multiply_fusion = f32[32,48,16,80]{3,0,2,1:T(8,128)} fusion(f32[32,48,16]{0,2,1:T(8,128)S(1)} %copy.110, f32[16,48,16,80]{3,1,2,0:T(8,128)} %fusion.23, s32[16]{0:T(128)S(1)} %convert_reduce_fusion), kind=kOutput, calls=%fused_computation.20 | convolution fusion | flops 379453952 | bytes 11894848 | tf_op jit(solution)/shard_map/pr,pqhd->rqhd/dot_general | solution.py:115
  271.7 16.4 %copy.111 = f32[32,48,16,80]{3,2,1,0:T(8,128)} copy(f32[32,48,16,80]{3,0,2,1:T(8,128)} %broadcast_multiply_fusion) | data formatting | bytes 15728640 | tf_op jit(solution)/shard_map/mul | solution.py:121
  288.1 12.8 %reshape.897 = f32[32,48,1280]{2,1,0:T(8,128)} reshape(f32[32,48,16,80]{3,2,1,0:T(8,128)} %copy.111) | data formatting | bytes 15728640 | tf_op jit(solution)/shard_map/reshape | solution.py:121
  308.0 28.5 %reduce-scatter.6.cloned.1.call-done = f32[1,48,16]{1,2,0:T(8,128)} async-done(((f32[32,48,16]{1,2,0:T(8,128)}), f32[1,48,16]{1,2,0:T(8,128)}) %reduce-scatter.6.cloned.1.call-update) | async-done | bytes 3088 | tf_op jit(solution)/shard_map/reduce_scatter | solution.py:125
  337.2 92.8 %reduce-scatter.4.cloned.1.call-done = f32[1,48,1280]{2,1,0:T(8,128)} async-done(((f32[32,48,1280]{2,1,0:T(8,128)}), f32[1,48,1280]{2,1,0:T(8,128)}) %reduce-scatter.4.cloned.1.call-update) | async-done | bytes 245776 | tf_op jit(solution)/shard_map/reduce_scatter | solution.py:126
  432.6 45.3 %all-gather.12.cloned.1.call-done = bf16[1536,1280]{1,0:T(8,128)(2,1)} async-done(((bf16[48,1280]{1,0:T(8,128)(2,1)}), bf16[1536,1280]{1,0:T(8,128)(2,1)}) %all-gather.12.cloned.1.call-update) | async-done | bytes 3932176 | tf_op jit(solution)/shard_map/all_gather | solution.py:38
  482.1 12.3 %all_to_all.46 = bf16[32,2,960]{2,1,0:T(2,128)(2,1)S(1)} all-to-all(bf16[32,2,960]{2,1,0:T(2,128)(2,1)S(1)} %reshape.1056), channel_id=1, replica_groups=mesh['req'=4,'blk'=32] {'blk'}, dimensions={0} | all-to-all | bytes 245760 | tf_op jit(solution)/shard_map/all_to_all | solution.py:42
  496.1 44.1 %all-gather.14.cloned.1.call-done = bf16[1536,1280]{1,0:T(8,128)(2,1)} async-done(((bf16[48,1280]{1,0:T(8,128)(2,1)}), bf16[1536,1280]{1,0:T(8,128)(2,1)}) %all-gather.14.cloned.1.call-update) | async-done | bytes 3932176 | tf_op jit(solution)/shard_map/all_gather | solution.py:38
  540.3 7.8 %fusion.66 = f32[1536,1280]{1,0:T(8,128)} fusion(bf16[40,1280]{1,0:T(8,128)(2,1)S(1)} %copy-done.7, bf16[1536,1280]{1,0:T(8,128)(2,1)} %all-gather.14.cloned.1.call-done, bf16[1280,40]{0,1:T(8,128)(2,1)S(1)} %copy-done.8), kind=kOutput, calls=%fused_computation.93 | convolution fusion | flops 315125760 | bytes 12001280 | tf_op jit(solution)/shard_map/dot_general | solution.py:166
  548.1 89.4 %reduce-scatter.8.cloned.1.call-done = f32[48,1280]{1,0:T(8,128)} async-done(((f32[1536,1280]{1,0:T(8,128)}), f32[48,1280]{1,0:T(8,128)}) %reduce-scatter.8.cloned.1.call-update) | async-done | bytes 245776 | tf_op jit(solution)/shard_map/reduce_scatter | solution.py:165
  645.7 24.1 %all-gather = bf16[32,5,2560]{2,1,0:T(8,128)(2,1)S(1)} all-gather(bf16[1,5,2560]{2,1,0:T(8,128)(2,1)S(1)} %fusion.12), channel_id=1, replica_groups=mesh['req'=4,'blk'=32] {'blk'}, dimensions={0}, use_global_device_ids=true | all-gather | bytes 844800 | tf_op jit(solution)/shard_map/all_gather | solution.py:204
  670.2 7.2 scatter_custom_fusion
  677.4 7.4 scatter_custom_fusion.1
  692.9 6.2 all-to-all-start.2
  699.1 9.1 %maximum_bitcast_fusion = bf16[1,2,2048,1280]{3,2,1,0:T(8,128)(2,1)} fusion(bf16[1,2048,1280]{2,1,0:T(8,128)(2,1)} %bitcast.177, bf16[1,2048,1280]{2,1,0:T(8,128)(2,1)} %bitcast.178), kind=kLoop, calls=%fused_computation.9 | loop fusion | flops 5242880 | bytes 20971520 | tf_op jit(solution)/shard_map/broadcast_in_dim | solution.py:220
  (164 shorter events, 81.1 us)
Async XLA Ops:
  7.2 678.7 %copy-start = (bf16[4,1280,40]{1,2,0:T(8,128)(2,1)S(1)}, bf16[4,1280,40]{1,2,0:T(8,128)(2,1)}, u32[]{:S(2)}) copy-start(bf16[4,1280,40]{1,2,0:T(8,128)(2,1)} %param.25) | copy-start | bytes 1228804
  7.2 51.4 %all-gather.8.cloned.1.call-start = ((), (), s32[]{:S(2)}) async-start(), calls=%async_computation.6 | async-start | bytes 4055040 | tf_op jit(solution)/shard_map/all_gather | solution.py:38
  8.3 70.7 %copy-start.9 = (s32[1,32]{1,0:T(1,128)S(1)}, s32[1,32]{1,0:T(1,128)}, u32[]{:S(2)}) copy-start(s32[1,32]{1,0:T(1,128)} %param.18) | copy-start | bytes 388
  10.0 112.6 %all-gather.10.cloned.1.call-start = ((), (), s32[]{:S(2)}) async-start(), calls=%async_computation.7 | async-start | bytes 4055040 | tf_op jit(solution)/shard_map/all_gather | solution.py:75
  78.4 177.4 %all-reduce.2.cloned.1.call-start = ((), (), s32[]{:S(2)}) async-start(), calls=%async_computation.8 | async-start | bytes 524288 | tf_op jit(solution)/shard_map/pmax | solution.py:118
  105.6 15.8 %copy-start.1 = (s32[1,512]{1,0:T(1,128)S(1)}, s32[1,512]{1,0:T(1,128)}, u32[]{:S(2)}) copy-start(s32[1,512]{1,0:T(1,128)} %param.17) | copy-start | bytes 6148
  155.2 9.8 %slice-start = ((s8[6291456]{0:T(1024)(128)(4,1)}), s8[2097152]{0:T(1024)(128)(4,1)S(1)}, s32[]{:S(2)}) async-start(s8[6291456]{0:T(1024)(128)(4,1)} %bitcast.175), calls=%async_computation.16 | async-start | bytes 4194304
  155.3 181.1 %reduce-scatter.6.cloned.1.call-start = ((), (), s32[]{:S(2)}) async-start(), calls=%async_computation.10 | async-start | bytes 270336 | tf_op jit(solution)/shard_map/reduce_scatter | solution.py:125
  155.6 9.5 %slice-start.1 = ((s8[6291456]{0:T(1024)(128)(4,1)}), s8[4194304]{0:T(1024)(128)(4,1)S(1)}, s32[]{:S(2)}) async-start(s8[6291456]{0:T(1024)(128)(4,1)} %bitcast.175), calls=%async_computation.17 | async-start | bytes 8388608
  258.5 171.5 %reduce-scatter.4.cloned.1.call-start = ((), (), s32[]{:S(2)}) async-start(), calls=%async_computation.9 | async-start | bytes 8110080 | tf_op jit(solution)/shard_map/reduce_scatter | solution.py:126
  300.9 4.0 copy-start.5
  300.9 177.0 %copy-start.6 = (bf16[1280,40]{0,1:T(8,128)(2,1)S(1)}, bf16[1280,40]{0,1:T(8,128)(2,1)}, u32[]{:S(2)}) copy-start(bf16[1280,40]{0,1:T(8,128)(2,1)} %param.22) | copy-start | bytes 307204
  300.9 177.0 %all-gather.12.cloned.1.call-start = ((), (), s32[]{:S(2)}) async-start(), calls=%async_computation.11 | async-start | bytes 4055040 | tf_op jit(solution)/shard_map/all_gather | solution.py:38
  431.5 63.6 %copy-start.3 = (bf16[48,1280]{1,0:T(8,128)(2,1)S(1)}, bf16[48,1280]{1,0:T(8,128)(2,1)}, u32[]{:S(2)}) copy-start(bf16[48,1280]{1,0:T(8,128)(2,1)} %param.15) | copy-start | bytes 368644
  432.5 107.8 %copy-start.7 = (bf16[40,1280]{1,0:T(8,128)(2,1)S(1)}, bf16[40,1280]{1,0:T(8,128)(2,1)}, u32[]{:S(2)}) copy-start(bf16[40,1280]{1,0:T(8,128)(2,1)} %param.24) | copy-start | bytes 307204
  432.5 107.8 %copy-start.8 = (bf16[1280,40]{0,1:T(8,128)(2,1)S(1)}, bf16[1280,40]{0,1:T(8,128)(2,1)}, u32[]{:S(2)}) copy-start(bf16[1280,40]{0,1:T(8,128)(2,1)} %param.23) | copy-start | bytes 307204
  432.5 107.8 %all-gather.14.cloned.1.call-start = ((), (), s32[]{:S(2)}) async-start(), calls=%async_computation.12 | async-start | bytes 4055040 | tf_op jit(solution)/shard_map/all_gather | solution.py:38
  496.1 141.4 %reduce-scatter.8.cloned.1.call-start = ((), (), s32[]{:S(2)}) async-start(), calls=%async_computation.13 | async-start | bytes 8110080 | tf_op jit(solution)/shard_map/reduce_scatter | solution.py:165
  548.0 91.9 %copy-start.10 = (s32[1,32]{1,0:T(1,128)S(1)}, s32[1,32]{1,0:T(1,128)}, u32[]{:S(2)}) copy-start(s32[1,32]{1,0:T(1,128)} %param.20) | copy-start | bytes 388
  548.1 137.8 %all-gather.16.cloned.1.call-start = ((), (), s32[]{:S(2)}) async-start(), calls=%async_computation.14 | async-start | bytes 4055040 | tf_op jit(solution)/shard_map/all_gather | solution.py:38
  638.5 6.1 copy-start.4
  639.4 88.6 %all-gather.18.cloned.1.call-start = ((), (), s32[]{:S(2)}) async-start(), calls=%async_computation.15 | async-start | bytes 4096000 | tf_op jit(solution)/shard_map/all_gather | solution.py:193
  642.9 2.0 copy-start.11
  692.9 19.3 %all-to-all-start.2 = ((bf16[32,48,160]{2,1,0:T(8,128)(2,1)}), bf16[32,48,160]{2,1,0:T(8,128)(2,1)S(1)}, u32[]{:S(2)}, u32[]{:S(2)}) async-start(bf16[32,48,160]{2,1,0:T(8,128)(2,1)} %copy.123), calls=%async_computation.5 | async-start | bytes 1572864 | tf_op jit(solution)/shard_map/all_to_all | solution.py:42
  (1 other events, 0.7 us)
Sparse Core Ops, SparseCore 0:
  10.8 47.6 all-gather.7
  78.6 44.0 all-gather.9
  155.5 100.3 all-reduce.1
  259.7 76.6 reduce-scatter.5
  340.7 89.1 reduce-scatter.3
  432.9 44.9 all-gather.11
  496.2 44.0 all-gather.13
  548.2 89.2 reduce-scatter.7
  640.3 45.5 all-gather.15
  687.4 40.5 all-gather.17
where the time goes:
time: 744 us; the launch traced here: 739 us
  waiting for transfers between devices  447 us (60%)
  local copies, waits for them, and re-layouts  135 us (18%)
  matrix products  56.4 us (8%)
  blocking collectives  51.2 us (7%)
  other arithmetic  25.4 us (3%)
  between operations  16.9 us (2%)
  starting transfers between devices  7.48 us (1%)
    all_gather x4, waiting for transfers between devices, row_blocks(): lax.all_gather(values, 'blk', axis=0, tiled=True)  139 us
    reduce_scatter x1, waiting for transfers between devices, on_device(): lax.psum_scatter(num_scaled, 'blk', scatter_dimension=0, tiled=True)  92.8 us
    reduce_scatter x1, waiting for transfers between devices, on_device(): lax.psum_scatter(jnp.dot(hidden_all, w_down, preferred_element_type=jnp.f...  89.4 us
    pmax x1, waiting for transfers between devices, on_device(): max_all = lax.pmax(request_max, 'blk')  87.2 us
    reduce_scatter x1, waiting for transfers between devices, on_device(): lax.psum_scatter(den_scaled, 'blk', scatter_dimension=0, tiled=True)  28.5 us
    all_to_all x2, blocking collectives, column_blocks(): lax.all_to_all(values, 'blk', split_axis=0, concat_axis=1, tiled=True)  27.1 us
    all_gather x1, blocking collectives, on_device(): received = lax.all_gather(send_rows, 'blk', axis=0, tiled=True)  24.1 us
    mul x1, local copies, waits for them, and re-layouts, on_device(): num_part.reshape(requests, tree_rows, H, HD) * factor[..., None]  16.4 us
  transfers between devices with their start and end apart: 11, of which 11 were waited for; matrix products, arithmetic and copies ran while one was open for 20% of the time, Pallas kernels for 0%

commit v1 on v0

v1 whole, which is shorter than its diff:
```python
import math

import jax
import jax.numpy as jnp
from jax import lax
from jax.experimental import pallas as pl
from jax.experimental.pallas import tpu as pltpu
from jax.sharding import PartitionSpec as P

H = 16
HD = 80
TREE = 48
DEPTH = 5
PAGE = 128
BLK = 32
WIDTH = H * HD

EPS = 1e-06
LOWEST = -8388608.0
LEVEL_START = (0, 1, 5, 15, 30, 48)
MESH = pl.DeviceIdType.MESH
ROWSLOT = ((0, 0), (-1, 0), (1, 0), (2, 0))


def rms_rows(values):
    wide = values.astype(jnp.float32)
    return (wide * lax.rsqrt(jnp.mean(wide * wide, axis=-1, keepdims=True) + EPS)).astype(
        jnp.bfloat16
    )


def dot_t(left, right):
    return lax.dot_general(
        left, right, (((1,), (1,)), ((), ())), preferred_element_type=jnp.float32
    )


class Spot:
    def __init__(self):
        self.me = lax.axis_index("blk")
        self.core = self.me % 2
        x = (self.me // 2) % 4
        y = self.me // 8
        self.one = x + self.core * (y - x)
        self.two = y + self.core * (x - y)
        self.sibling = self.me + 1 - 2 * self.core

    def at(self, a, b):
        return self.core + 2 * self.chip(a, b)

    def chip(self, a, b):
        one = (self.one + a + 4) % 4
        two = (self.two + b + 4) % 4
        return (1 + 3 * self.core) * one + (4 - 3 * self.core) * two


def greet_plane(spot):
    barrier = pltpu.get_barrier_semaphore()
    for who in (spot.at(1, 0), spot.at(-1, 0), spot.at(0, 1), spot.at(0, -1), spot.sibling):
        pl.semaphore_signal(barrier, inc=1, device_id={"blk": who}, device_id_type=MESH)
    pl.semaphore_wait(barrier, 5)


def numbered(names):
    return {name: i for i, name in enumerate(names)}


GATHER = numbered(
    ["L", "R", "OA", "OB"]
    + [f"{kind}{k}" for k in range(4) for kind in ("D", "U", "PA", "PB")]
    + [f"S{k}" for k in range(16)]
)


def sender(sent, ssem, rsem, events):
    def put(event, src, dst, who):
        copy = pltpu.make_async_remote_copy(
            src_ref=src,
            dst_ref=dst,
            send_sem=ssem(events[event]),
            recv_sem=rsem(events[event]),
            device_id={"blk": who},
            device_id_type=MESH,
        )
        copy.start()
        sent[event] = copy

    return put


def gather_steps(spot, shard, view, ssem, rsem, lsem, cut):
    sent = {}
    send = sender(sent, ssem, rsem, GATHER)

    def put(event, src, slot, who, half=None):
        dst = view(slot)
        if half is not None:
            src, dst = cut(src, half), cut(dst, half)
        send(event, src, dst, who)

    right, left = spot.at(1, 0), spot.at(-1, 0)
    up, down = spot.at(0, 1), spot.at(0, -1)
    local = pltpu.make_async_copy(shard, view(spot.me), lsem)
    local.start()
    put("L", shard, spot.me, right)
    put("R", shard, spot.me, left)
    put("D0", shard, spot.me, up)
    put("U0", shard, spot.me, down)
    put("S0", shard, spot.me, spot.sibling)
    yield
    for k, event in ((1, "L"), (2, "R")):
        slot = spot.at(*ROWSLOT[k])
        sent[event].wait_recv()
        if k == 1:
            put("OA", view(slot), slot, right, 0)
        else:
            put("OB", view(slot), slot, left, 1)
        put(f"D{k}", view(slot), slot, up)
        put(f"U{k}", view(slot), slot, down)
        put(f"S{k}", view(slot), slot, spot.sibling)
        yield

    def column(k):
        a = ROWSLOT[k][0]
        slot = spot.at(a, -1)
        sent[f"D{k}"].wait_recv()
        put(f"PA{k}", view(slot), slot, up, 0)
        put(f"S{4 + k}", view(slot), slot, spot.sibling)
        slot = spot.at(a, 1)
        sent[f"U{k}"].wait_recv()
        put(f"PB{k}", view(slot), slot, down, 1)
        put(f"S{8 + k}", view(slot), slot, spot.sibling)

    column(0)
    yield
    sent["OA"].wait_recv()
    sent["OB"].wait_recv()
    slot = spot.at(2, 0)
    put("D3", view(slot), slot, up)
    put("U3", view(slot), slot, down)
    put("S3", view(slot), slot, spot.sibling)
    yield
    for k in (1, 2, 3):
        column(k)
        yield
    for k in range(4):
        slot = spot.at(ROWSLOT[k][0], 2)
        sent[f"PA{k}"].wait_recv()
        sent[f"PB{k}"].wait_recv()
        put(f"S{12 + k}", view(slot), slot, spot.sibling)
        yield
    for k in range(16):
        sent[f"S{k}"].wait_recv()
    local.wait()
    for event in GATHER:
        sent[event].wait_send()


def run_all(steps):
    steps = list(steps)
    while steps:
        alive = []
        for step in steps:
            try:
                next(step)
                alive.append(step)
            except StopIteration:
                pass
        steps = alive


def row_halves(rows):
    first = ((rows // 2) + 7) // 8 * 8

    def cut(ref, half):
        return ref.at[pl.ds(0, first)] if half == 0 else ref.at[pl.ds(first, rows - first)]

    return cut


def gather_all(spot, ins, outs, ssem, rsem, lsem):
    count = len(GATHER)
    return [
        gather_steps(
            spot,
            ins[i],
            lambda slot, i=i: outs[i].at[slot],
            lambda e, i=i: ssem.at[i * count + e],
            lambda e, i=i: rsem.at[i * count + e],
            lsem.at[i],
            row_halves(ins[i].shape[0]),
        )
        for i in range(len(ins))
    ]


def gather_sems(arrays):
    return [
        pltpu.SemaphoreType.DMA((arrays * len(GATHER),)),
        pltpu.SemaphoreType.DMA((arrays * len(GATHER),)),
        pltpu.SemaphoreType.DMA((arrays,)),
    ]


ANY = pl.BlockSpec(memory_space=pl.ANY)
VMEM = pl.BlockSpec(memory_space=pltpu.VMEM)


def all_gather(shards, collective_id, name):
    count = len(shards)

    def kernel(*refs):
        spot = Spot()
        greet_plane(spot)
        run_all(gather_all(spot, refs[:count], refs[count : 2 * count], *refs[2 * count :]))

    return pl.pallas_call(
        kernel,
        out_shape=[jax.ShapeDtypeStruct((BLK,) + s.shape, s.dtype) for s in shards],
        in_specs=[ANY] * count,
        out_specs=[ANY] * count,
        scratch_shapes=gather_sems(count),
        compiler_params=pltpu.CompilerParams(collective_id=collective_id, has_side_effects=True),
        name=name,
    )(*shards)


def window(w):
    return 128 * (5 * (w // 4) + w % 4), 32 * (w % 4)


def attend_kernel(
    tables, query_ref, cache_ref, proj_ref, marks_ref, num_ref, stats_ref, new_ref, acc, tops, dens
):
    step = pl.program_id(0)
    pages = pl.num_programs(0) - 1
    owner = tables[0, step]
    start = tables[1, step]
    length = tables[2, step]
    count = tables[3, step]
    factor = math.log2(math.e) / math.sqrt(HD)

    @pl.when(step == 0)
    def _():
        tops[...] = jnp.full_like(tops, LOWEST)
        dens[...] = jnp.zeros_like(dens)

        @pl.loop(0, BLK)
        def _(r):
            acc[r] = jnp.zeros(acc.shape[1:], acc.dtype)

    lanes = lax.broadcasted_iota(jnp.int32, (TREE, 128), 1)
    columns = lax.broadcasted_iota(jnp.int32, (TREE, 256), 1)

    def merge(query, key_at, value_at, seen):
        tops_old = tops[owner]
        dens_old = dens[owner]
        tops_new, dens_new = tops_old, dens_old
        for w in range(8):
            first, begin = window(w)
            here = [
                (columns >= begin + HD * i) & (columns < begin + HD * (i + 1)) for i in range(2)
            ]
            picked = query(first)
            stacked = jnp.concatenate(
                [picked * here[i].astype(jnp.float32).astype(jnp.bfloat16) for i in range(2)],
                axis=0,
            )
            scores = dot_t(stacked, key_at(first)) * factor
            weights = []
            scales = []
            for i in range(2):
                head = 2 * w + i
                part = jnp.where(seen, scores[i * TREE : (i + 1) * TREE], LOWEST)
                before = tops_old[:, head : head + 1]
                top = jnp.maximum(before, jnp.ceil(jnp.max(part, axis=1, keepdims=True)))
                weight = jnp.where(seen, jnp.exp2(part - top), 0.0)
                scale = jnp.exp2(before - top)
                total = dens_old[:, head : head + 1] * scale + jnp.sum(
                    weight, axis=1, keepdims=True
                )
                tops_new = jnp.where(lanes == head, top, tops_new)
                dens_new = jnp.where(lanes == head, total, dens_new)
                weights.append(weight.astype(jnp.bfloat16))
                scales.append(scale)
            added = jnp.dot(
                jnp.concatenate(weights, axis=0),
                value_at(first),
                preferred_element_type=jnp.float32,
            )
            window_scale = jnp.where(here[0], scales[0], jnp.where(here[1], scales[1], 1.0))
            window_sum = jnp.where(
                here[0], added[:TREE], jnp.where(here[1], added[TREE:], 0.0)
            )
            old = acc[owner, :, pl.ds(first, 256)]
            acc[owner, :, pl.ds(first, 256)] = old * window_scale + window_sum
        tops[owner] = tops_new
        dens[owner] = dens_new

    @pl.when(step < pages)
    def _():
        seen = lax.broadcasted_iota(jnp.int32, (TREE, PAGE), 1) + start < length
        merge(
            lambda first: query_ref[0, pl.ds(0, TREE), pl.ds(first, 256)],
            lambda first: cache_ref[0, 0, :, pl.ds(first, 256)],
            lambda first: cache_ref[0, 1, :, pl.ds(first, 256)],
            seen,
        )
        row0 = length - start
        touched = (row0 < PAGE) & (row0 + count > 0)

        @pl.when(jnp.logical_not(touched))
        def _():
            new_ref[...] = cache_ref[...]

        @pl.when(touched)
        def _():
            ahead = lax.broadcasted_iota(jnp.int32, (PAGE, 8), 0) - row0
            nth = lax.broadcasted_iota(jnp.int32, (PAGE, 8), 1)
            hot = ((ahead == nth) & (nth < count)).astype(jnp.float32).astype(jnp.bfloat16)
            rows = lax.broadcasted_iota(jnp.int32, (PAGE, WIDTH), 0) - row0
            hit = (rows >= 0) & (rows < count)
            for i in range(2):
                fresh = jnp.dot(
                    hot,
                    query_ref[0, pl.ds(TREE + 8 * i, 8), :],
                    preferred_element_type=jnp.float32,
                )
                kept = cache_ref[0, i].astype(jnp.float32)
                new_ref[0, i] = jnp.where(hit, fresh, kept).astype(jnp.bfloat16)

    @pl.when(step == pages)
    def _():
        merge(
            lambda first: query_ref[0, pl.ds(0, TREE), pl.ds(first, 256)],
            lambda first: proj_ref[:, pl.ds(WIDTH + first, 256)],
            lambda first: proj_ref[:, pl.ds(2 * WIDTH + first, 256)],
            marks_ref[...] > 0.5,
        )

        @pl.loop(0, BLK)
        def _(r):
            num_ref[r] = acc[r].astype(jnp.bfloat16)
            stats_ref[r] = jnp.where(lanes < 64, tops[r], pltpu.roll(dens[r], 64, 1))


def attend(tables, gathered, cache, projected, marks):
    pages = cache.shape[2] // PAGE
    rows = gathered.shape[1]
    page_block = pl.BlockSpec(
        (1, 2, PAGE, WIDTH), lambda p, t: (0, 0, jnp.minimum(p, pages - 1), 0)
    )
    whole3 = lambda p, t: (0, 0, 0)
    return pl.pallas_call(
        attend_kernel,
        out_shape=[
            jax.ShapeDtypeStruct((BLK, TREE, WIDTH), jnp.bfloat16),
            jax.ShapeDtypeStruct((BLK, TREE, 128), jnp.float32),
            jax.ShapeDtypeStruct(cache.shape, cache.dtype),
        ],
        grid_spec=pltpu.PrefetchScalarGridSpec(
            num_scalar_prefetch=1,
            grid=(pages + 1,),
            in_specs=[
                pl.BlockSpec((1, rows, WIDTH), lambda p, t: (t[4, p], 0, 0)),
                page_block,
                pl.BlockSpec((TREE, 3 * WIDTH), lambda p, t: (0, 0)),
                pl.BlockSpec((TREE, TREE), lambda p, t: (0, 0)),
            ],
            out_specs=[
                pl.BlockSpec((BLK, TREE, WIDTH), whole3),
                pl.BlockSpec((BLK, TREE, 128), whole3),
                page_block,
            ],
            scratch_shapes=[
                pltpu.VMEM((BLK, TREE, WIDTH), jnp.float32),
                pltpu.VMEM((BLK, TREE, 128), jnp.float32),
                pltpu.VMEM((BLK, TREE, 128), jnp.float32),
            ],
        ),
        compiler_params=pltpu.CompilerParams(vmem_limit_bytes=48 * 1024 * 1024),
        name="attend",
    )(tables, gathered, cache, projected, marks)


PAIR_ORDER = (
    [(2, b) for b in range(4)]
    + [(1, 2), (1, 3), (-1, 0), (-1, 1)]
    + [(1, 0), (1, 1), (-1, 2), (-1, 3)]
    + [(0, b) for b in range(4)]
)
REDUCE = numbered(
    [f"{kind}{i}{s}" for kind, n in (("P", 16), ("T", 4), ("L", 4), ("R", 4)) for i in range(n) for s in "ns"]
    + [f"{kind}{s}" for kind in ("t0", "t1", "l", "r") for s in "ns"]
)


def split_stats(stats):
    return stats, pltpu.roll(stats, 64, 1)


def combine(parts, spread):
    stats = [split_stats(s) for _, s in parts]
    lanes = lax.broadcasted_iota(jnp.int32, stats[0][0].shape, 1)
    top = stats[0][0]
    for s, _ in stats[1:]:
        top = jnp.maximum(top, s)
    total = None
    num = None
    for (n, _), (s, d) in zip(parts, stats):
        scale = jnp.where(lanes < H, jnp.exp2(jnp.minimum(s - top, 0.0)), 0.0)
        wide = jnp.dot(scale.astype(jnp.bfloat16), spread, preferred_element_type=jnp.float32)
        d = d * scale
        n = n.astype(jnp.float32) * wide
        total = d if total is None else total + d
        num = n if num is None else num + n
    return num, top, total


def join_stats(top, total):
    lanes = lax.broadcasted_iota(jnp.int32, top.shape, 1)
    return jnp.where(lanes < H, top, pltpu.roll(jnp.where(lanes < H, total, 0.0), 64, 1))


def reduce_steps(spot, num, stats, out, spread, bufs, ssem, rsem):
    pair_n, pair_s, work_n, work_s, thru_n, thru_s, left_n, left_s, right_n, right_s = bufs[:10]
    fin_n, fin_s, two_n, two_s = bufs[10:]
    sent = {}
    send = sender(sent, ssem, rsem, REDUCE)

    def put(event, src_n, src_s, dst_n, dst_s, who):
        send(event + "n", src_n, dst_n, who)
        send(event + "s", src_s, dst_s, who)

    def took(event):
        sent[event + "n"].wait_recv()
        sent[event + "s"].wait_recv()

    right, left = spot.at(1, 0), spot.at(-1, 0)
    up, down = spot.at(0, 1), spot.at(0, -1)
    other = (1 - spot.core) * 16
    mine = spot.core * 16
    for i, (a, b) in enumerate(PAIR_ORDER):
        c = other + spot.chip(b, a)
        put(f"P{i}", num.at[c], stats.at[c], pair_n.at[i], pair_s.at[i], spot.sibling)
    yield

    def store(dst_n, dst_s, parts):
        n, top, total = combine(parts, spread())
        dst_n[...] = n.astype(jnp.bfloat16)
        dst_s[...] = join_stats(top, total)

    place = {pair: i for i, pair in enumerate(PAIR_ORDER)}
    for i, (a, b) in enumerate(PAIR_ORDER):
        took(f"P{i}")
        c = mine + spot.chip(a, b)
        store(
            work_n.at[i], work_s.at[i], [(num[c], stats[c]), (pair_n[i], pair_s[i])]
        )
        if a == 2:
            put(
                f"T{b}", work_n.at[i], work_s.at[i], thru_n.at[b], thru_s.at[b],
                right if b < 2 else left,
            )
        elif (a == 1 and b >= 2):
            put(f"L{b}", work_n.at[i], work_s.at[i], left_n.at[b], left_s.at[b], right)
        elif (a == -1 and b < 2):
            put(f"R{b}", work_n.at[i], work_s.at[i], right_n.at[b], right_s.at[b], left)
        yield
    for b in range(4):
        took(f"T{b}")
        a = 1 if b < 2 else -1
        i = place[(a, b)]
        store(
            work_n.at[i], work_s.at[i], [(work_n[i], work_s[i]), (thru_n[b], thru_s[b])]
        )
        if a == 1:
            put(f"L{b}", work_n.at[i], work_s.at[i], left_n.at[b], left_s.at[b], right)
        else:
            put(f"R{b}", work_n.at[i], work_s.at[i], right_n.at[b], right_s.at[b], left)
        yield
    cuts = (pl.ds(0, 32), pl.ds(32, 16))
    for b in (2, 1, 3, 0):
        took(f"L{b}")
        took(f"R{b}")
        i = place[(0, b)]
        store(
            fin_n.at[b],
            fin_s.at[b],
            [(work_n[i], work_s[i]), (left_n[b], left_s[b]), (right_n[b], right_s[b])],
        )
        if b == 2:
            for half, who in ((0, up), (1, down)):
                put(
                    f"t{half}",
                    fin_n.at[2, cuts[half]],
                    fin_s.at[2, cuts[half]],
                    two_n.at[0, cuts[half]],
                    two_s.at[0, cuts[half]],
                    who,
                )
        yield
    for half, b in ((0, 1), (1, 3)):
        took(f"t{half}")
        rows = cuts[half]
        store(
            fin_n.at[b, rows],
            fin_s.at[b, rows],
            [(fin_n[b, rows], fin_s[b, rows]), (two_n[0, rows], two_s[0, rows])],
        )
        if b == 1:
            put("l", fin_n.at[1], fin_s.at[1], two_n.at[1], two_s.at[1], up)
        else:
            put("r", fin_n.at[3], fin_s.at[3], two_n.at[2], two_s.at[2], down)
        yield
    took("l")
    took("r")
    n, top, total = combine(
        [(fin_n[0], fin_s[0]), (two_n[1], two_s[1]), (two_n[2], two_s[2])], spread()
    )
    lanes = lax.broadcasted_iota(jnp.int32, total.shape, 1)
    inverse = jnp.where(lanes < H, 1.0 / jnp.where(lanes < H, total, 1.0), 0.0)
    wide = jnp.dot(
        inverse,
        spread().astype(jnp.float32),
        preferred_element_type=jnp.float32,
        precision=lax.Precision.HIGHEST,
    )
    out[...] = (n * wide).astype(jnp.bfloat16)
    for event in REDUCE:
        sent[event].wait_send()


def reduce_and_gather(num, stats, spread, shards, collective_id):
    count = len(shards)

    def kernel(num_ref, stats_ref, spread_ref, *refs):
        ins = refs[:count]
        out = refs[count]
        outs = refs[count + 1 : 2 * count + 1]
        scratch = refs[2 * count + 1 :]
        spot = Spot()
        greet_plane(spot)
        ssem, rsem = scratch[:2]
        steps = [
            reduce_steps(
                spot,
                num_ref,
                stats_ref,
                out,
                lambda: spread_ref[...],
                scratch[5:],
                lambda e: ssem.at[e],
                lambda e: rsem.at[e],
            )
        ]
        run_all(steps + gather_all(spot, ins, outs, *scratch[2:5]))

    def block(n):
        return [
            pltpu.VMEM((n, TREE, WIDTH), jnp.bfloat16),
            pltpu.VMEM((n, TREE, 128), jnp.float32),
        ]

    return pl.pallas_call(
        kernel,
        out_shape=[jax.ShapeDtypeStruct((TREE, WIDTH), jnp.bfloat16)]
        + [jax.ShapeDtypeStruct((BLK,) + s.shape, s.dtype) for s in shards],
        in_specs=[VMEM, VMEM, VMEM] + [ANY] * count,
        out_specs=[VMEM] + [ANY] * count,
        scratch_shapes=[
            pltpu.SemaphoreType.DMA((len(REDUCE),)),
            pltpu.SemaphoreType.DMA((len(REDUCE),)),
        ]
        + gather_sems(count)
        + block(16)
        + block(16)
        + block(4)
        + block(4)
        + block(4)
        + block(4)
        + block(3),
        compiler_params=pltpu.CompilerParams(
            collective_id=collective_id,
            has_side_effects=True,
            vmem_limit_bytes=48 * 1024 * 1024,
        ),
        name="reduce_and_gather",
    )(num, stats, spread, *shards)


def greet_column(at):
    barrier = pltpu.get_barrier_semaphore()
    for d in (1, 2, 3):
        pl.semaphore_signal(
            barrier, inc=1, device_id={"req": (at + d) % 4}, device_id_type=MESH
        )
    pl.semaphore_wait(barrier, 3)


def column_kernel(exchange):
    def kernel(block, out, ssem, rsem, lsem):
        at = lax.axis_index("req")
        greet_column(at)
        copies = []
        for d in (2, 1, 3):
            to = (at + d) % 4
            copy = pltpu.make_async_remote_copy(
                src_ref=block.at[to] if exchange else block,
                dst_ref=out.at[at],
                send_sem=ssem.at[d - 1],
                recv_sem=rsem.at[d - 1],
                device_id={"req": to},
                device_id_type=MESH,
            )
            copy.start()
            copies.append(copy)
        local = pltpu.make_async_copy(block.at[at] if exchange else block, out.at[at], lsem)
        local.start()
        local.wait()
        for copy in copies:
            copy.wait()

    return kernel


def over_column(block, exchange, collective_id, name):
    shape = block.shape if exchange else (4,) + block.shape
    return pl.pallas_call(
        column_kernel(exchange),
        out_shape=jax.ShapeDtypeStruct(shape, block.dtype),
        in_specs=[VMEM],
        out_specs=VMEM,
        scratch_shapes=[
            pltpu.SemaphoreType.DMA((3,)),
            pltpu.SemaphoreType.DMA((3,)),
            pltpu.SemaphoreType.DMA,
        ],
        compiler_params=pltpu.CompilerParams(
            collective_id=collective_id, has_side_effects=True
        ),
        name=name,
    )(block)


def ancestors(parent_row):
    nodes = jnp.arange(TREE, dtype=jnp.int32)
    step = (parent_row[:, None] == nodes[None, :]).astype(jnp.float32)
    current = jnp.eye(TREE, dtype=jnp.float32)
    marks = current
    for _ in range(DEPTH - 1):
        current = jnp.dot(current, step)
        marks = jnp.maximum(marks, current)
    return marks


def on_device(
    tree_input,
    cache,
    page_table,
    lengths,
    parents,
    accept_leaf,
    w_qkv,
    w_out,
    w_up,
    w_down,
    w_draft,
    w_patch,
):
    myself = lax.axis_index("blk")
    width = WIDTH
    pool_pages = cache.shape[2] // PAGE
    patch = lax.all_gather(w_patch.T, "req", axis=0, tiled=True)
    normed = rms_rows(tree_input)
    (qkv,) = all_gather([w_qkv.T], 1, "gather_qkv")
    projected = dot_t(normed, qkv.reshape(3 * width, width)).astype(jnp.bfloat16)

    page_row = page_table[0]
    length_row = lengths[0]
    leaf_row = accept_leaf[0]
    requests = length_row.shape[0]
    total_pages = page_row.shape[0]
    npages = (length_row + DEPTH + PAGE - 1) // PAGE
    before = jnp.arange(requests)[:, None] >= jnp.arange(requests)[None, :]
    page_ends = jnp.sum(jnp.where(before, npages[None, :], 0), axis=1)
    offsets = page_ends - npages
    local_ids = myself * pool_pages + jnp.arange(pool_pages, dtype=jnp.int32)
    located = page_row[None, :] == local_ids[:, None]
    where_at = jnp.sum(
        jnp.where(located, jnp.arange(total_pages, dtype=jnp.int32)[None, :], 0), axis=1
    )
    owner = jnp.sum((page_ends[None, :] <= where_at[:, None]).astype(jnp.int32), axis=1)
    owner_hot = owner[:, None] == jnp.arange(requests, dtype=jnp.int32)[None, :]
    safe_owner = jnp.minimum(owner, requests - 1)
    level_marks = jnp.asarray(LEVEL_START[1:-1], jnp.int32)
    accepted = 1 + jnp.sum((leaf_row[:, None] >= level_marks[None, :]).astype(jnp.int32), axis=1)

    def of_owner(row):
        return jnp.sum(jnp.where(owner_hot, row[None, :], 0), axis=1)

    def with_tree(row, last):
        return jnp.concatenate([row, jnp.reshape(jnp.asarray(last, jnp.int32), (1,))])

    owners = with_tree(safe_owner, myself)
    tables = jnp.stack(
        [
            owners % 2 * 16 + owners // 2,
            with_tree((where_at - of_owner(offsets)) * PAGE, 0),
            with_tree(of_owner(length_row), 0),
            with_tree(of_owner(accepted), 0),
            owners,
        ]
    )
    marks = ancestors(parents[0])
    my_leaf = jnp.sum(jnp.where(jnp.arange(requests) == myself, leaf_row, 0))
    nodes = jnp.arange(TREE, dtype=jnp.int32)
    chosen = jnp.sum(jnp.where(nodes[:, None] == my_leaf, marks, 0.0), axis=0)
    ranks = jnp.sum(jnp.where(nodes[:, None] <= nodes[None, :], chosen[:, None], 0.0), axis=0) - 1
    picker = jnp.where(
        (chosen[None, :] > 0.5) & (ranks[None, :] == jnp.arange(8, dtype=jnp.float32)[:, None]),
        1.0,
        0.0,
    ).astype(jnp.bfloat16)
    send_rows = jnp.dot(
        picker, projected[:, width:], preferred_element_type=jnp.float32
    ).astype(jnp.bfloat16)
    (gathered,) = all_gather(
        [jnp.concatenate([projected[:, :width], send_rows[:, :width], send_rows[:, width:]])],
        2,
        "gather_query",
    )
    num, stats, cache_new = attend(tables, gathered, cache, projected, marks)
    spread = (
        jnp.arange(128, dtype=jnp.int32)[:, None]
        == jnp.arange(width, dtype=jnp.int32)[None, :] // HD
    ).astype(jnp.bfloat16)
    draft_mine = lax.dynamic_index_in_dim(
        w_draft.transpose(0, 2, 1), lax.axis_index("req"), 0, keepdims=False
    )
    attended, full_out, full_up, full_down, full_draft = reduce_and_gather(
        num, stats, spread, [w_out.T, w_up.T, w_down, draft_mine], 3
    )
    full_out, full_up, full_down, full_draft = (
        w.reshape(width, width) for w in (full_out, full_up, full_down, full_draft)
    )
    proj = dot_t(attended, full_out).astype(jnp.bfloat16)
    mid = (tree_input.astype(jnp.float32) + proj.astype(jnp.float32)).astype(jnp.bfloat16)
    hidden = jax.nn.gelu(dot_t(rms_rows(mid), full_up)).astype(jnp.bfloat16)
    feedforward = jnp.dot(hidden, full_down, preferred_element_type=jnp.float32)
    layer_out = (mid.astype(jnp.float32) + feedforward).astype(jnp.bfloat16)
    rows = over_column(layer_out, False, 4, "gather_rows").reshape(4 * TREE, width)
    branch = jax.nn.silu(dot_t(rms_rows(rows), full_draft)).astype(jnp.bfloat16)
    drafted = (rows.astype(jnp.float32) + branch.astype(jnp.float32)).astype(jnp.bfloat16)
    head = dot_t(drafted, patch).astype(jnp.bfloat16)
    drafts = over_column(head.reshape(4, TREE, width), True, 5, "return_rows")
    return (layer_out, drafts, cache_new)


def solution(mesh):
    in_specs = (
        P(("req", "blk"), None),
        P("req", None, "blk", None),
        P("req", None),
        P("req", None),
        P(("req", "blk"), None),
        P("req", None),
        P(None, "blk"),
        P(None, "blk"),
        P(None, "blk"),
        P("blk", None),
        P(None, None, "blk"),
        P(None, "req"),
    )
    out_specs = (
        P(("req", "blk"), None),
        P(None, ("req", "blk"), None),
        P("req", None, "blk", None),
    )
    return jax.shard_map(
        on_device, mesh=mesh, in_specs=in_specs, out_specs=out_specs, check_vma=False
    )
```

time: 744 us -> 259 us (0.35)
  waiting for transfers between devices: 447 us -> 0.7 us
  Pallas kernels: 0 us -> 209 us
  local copies, waits for them, and re-layouts: 135 us -> 3.93 us
  blocking collectives: 51.2 us -> 0 us
  matrix products: 56.4 us -> 24.1 us
  other arithmetic: 25.4 us -> 6.41 us
  starting transfers between devices: 7.48 us -> 0.04 us
    reduce_scatter x3 -> x0, waiting for transfers between devices: 211 us -> none  [the longest x1 92.8 us: on_device(): lax.psum_scatter(num_scaled, 'blk', scatter_dimension=0, tiled=True)]
    pallas_call x0 -> x6, Pallas kernels: none -> 209 us  [the longest x1 69.5 us: reduce_and_gather(): pl.pallas_call(kernel, out_shape=[jax.ShapeDtypeStruct((TREE, WIDTH), jnp...]
    all_gather x6 -> x1, waiting for transfers between devices: 144 us -> 0.02 us  [on_device(): patch = lax.all_gather(w_patch.T, 'req', axis=0, tiled=True)]
    pmax x1 -> x0, waiting for transfers between devices: 87.2 us -> none  [on_device(): max_all = lax.pmax(request_max, 'blk')]
    another operation x3 -> x1, local copies, waits for them, and re-layouts: 32.6 us -> 0.02 us  [on_device(): jnp.stack([owners % 2 * 16 + owners // 2, with_tree((where_at - of_owner(...]
    dot_general x11 -> x10, matrix products: 52.9 us -> 24.1 us  [the longest x4 15.2 us: dot_t(): lax.dot_general(left, right, (((1,), (1,)), ((), ())), preferred_element_...]
    all_to_all x2 -> x0, blocking collectives: 27.1 us -> none  [column_blocks(): lax.all_to_all(values, 'blk', split_axis=0, concat_axis=1, tiled=True)]
    reshape x5 -> x0, local copies, waits for them, and re-layouts: 25.7 us -> none  [the longest x1 12.8 us: on_device(): (num_part.reshape(requests, tree_rows, H, HD) * factor[..., None]).reshap...]
  transfers between devices with their start and end apart: 11 -> 1, of which waited for: 11 -> 0; matrix products, arithmetic and copies ran while one was open for 20% -> 10% of each run, Pallas kernels for 0% -> 77%
where the time goes in v1:
time: 259 us
  Pallas kernels  209 us (81%)
  matrix products  24.1 us (9%)
  between operations  14.3 us (6%)
  other arithmetic  6.41 us (2%)
  local copies, waits for them, and re-layouts  3.93 us (2%)
    pallas_call x1, Pallas kernels, reduce_and_gather(): pl.pallas_call(kernel, out_shape=[jax.ShapeDtypeStruct((TREE, WIDTH), jnp...  69.5 us
    pallas_call x1, Pallas kernels, attend(): pl.pallas_call(attend_kernel, out_shape=[jax.ShapeDtypeStruct((BLK, TREE,...  59.4 us
    pallas_call x2, Pallas kernels, all_gather(): pl.pallas_call(kernel, out_shape=[jax.ShapeDtypeStruct((BLK,) + s.shape,...  58.1 us
    pallas_call x2, Pallas kernels, over_column(): pl.pallas_call(column_kernel(exchange), out_shape=jax.ShapeDtypeStruct(sh...  22.1 us
    dot_general x4, matrix products, dot_t(): lax.dot_general(left, right, (((1,), (1,)), ((), ())), preferred_element_...  15.2 us
    dot_general x1, matrix products, on_device(): feedforward = jnp.dot(hidden, full_down, preferred_element_type=jnp.float32)  5.34 us
  transfers between devices with their start and end apart: 1, of which 0 were waited for; matrix products, arithmetic and copies ran while one was open for 10% of the time, Pallas kernels for 77%

profile of v1, /device:TPU:2, one launch (start us, length us, event | category | flops | bytes accessed | tf_op | source)
XLA Modules:
  0.0 258.6 jit_solution(7487122018899488484)
XLA Ops:
  7.2 0.7 all-gather.2.cloned.1.call-update
  7.9 0.8 fusion.29
  8.8 0.8 fusion.28
  9.6 0.9 fusion.27
  10.5 1.3 fusion.47
  11.8 0.6 iota_compare_fusion.12
  12.4 0.9 select_reduce_fusion.2
  13.4 34.7 %gather_qkv.1 = bf16[32,120,1280]{2,1,0:T(8,128)(2,1)} custom-call(bf16[120,1280]{1,0:T(8,128)(2,1)} %bitcast.65), custom_call_target="tpu_custom_call" | custom-call | tf_op jit(solution)/shard_map/gather_qkv/pallas_call | solution.py:217
  48.3 6.8 %convolution_convert_fusion.proj_ref = bf16[48,3840]{1,0:T(8,128)(2,1)S(1)} fusion(bf16[3840,1280]{1,0:T(8,128)(2,1)} %bitcast.59, bf16[48,1280]{1,0:T(8,128)(2,1)S(1)} %copy-done.5, f32[48]{0:T(128)S(1)} %add_rsqrt_fusion.2), kind=kOutput, calls=%fused_computation | convolution fusion | flops 472227840 | bytes 10322112 | tf_op jit(solution)/shard_map/dot_general | solution.py:33
  55.4 0.7 pad_maximum_fusion.refs_0_
  56.1 23.4 %gather_query.1.query_ref = bf16[32,64,1280]{2,1,0:T(8,128)(2,1)} custom-call(bf16[64,1280]{1,0:T(8,128)(2,1)} %pad_maximum_fusion.refs_0_), custom_call_target="tpu_custom_call" | custom-call | tf_op jit(solution)/shard_map/gather_query/pallas_call | solution.py:217
  80.1 0.2 select_reduce_fusion.4
  80.6 59.4 %attend.1 = (bf16[32,48,1280]{2,1,0:T(8,128)(2,1)S(1)}, f32[32,48,128]{2,1,0:T(8,128)S(1)}, bf16[1,2,2048,1280]{3,2,1,0:T(8,128)(2,1)}) custom-call(s32[5,17]{1,0:T(8,128)S(1)} %stack.20.tables, bf16[32,64,1280]{2,1,0:T(8,128)(2,1)} %gather_query.1.query_ref, bf16[1,2,2048,1280]{3,2,1,0:T(8,128)(2,1)} %cache_ref.1, ...), custom_call_target="tpu_custom_call" | custom-call | tf_op jit(solution)/shard_map/attend/pallas_call | solution.py:354
  140.0 2.0 copy-done.1
  142.1 69.5 %reduce_and_gather.1 = (bf16[48,1280]{1,0:T(8,128)(2,1)S(1)}, bf16[32,40,1280]{2,1,0:T(8,128)(2,1)S(1)}, bf16[32,40,1280]{2,1,0:T(8,128)(2,1)}, bf16[32,40,1280]{2,1,0:T(8,128)(2,1)}, bf16[32,40,1280]{2,1,0:T(8,128)(2,1)}) custom-call(bf16[32,48,1280]{2,1,0:T(8,128)(2,1)} %copy-done.1, f32[32,48,128]{2,1,0:T(8,128)S(1)} %get-tuple-element.12.stats_ref, ...), custom_call_target="tpu_custom_call" | custom-call | tf_op jit(solution)/shard_map/reduce_and_gather/pallas_call | solution.py:565
  211.6 1.2 multiply_reduce_fusion.1
  212.8 5.3 %fusion.block = bf16[48,1280]{1,0:T(8,128)(2,1)} fusion(f32[48,1280]{1,0:T(8,128)S(1)} %get-tuple-element.29, bf16[1280,1280]{1,0:T(8,128)(2,1)} %bitcast.61, bf16[1280,1280]{1,0:T(8,128)(2,1)} %bitcast.60, f32[48]{0:T(128)S(1)} %add_rsqrt_fusion.1), kind=kOutput, calls=%fused_computation.4 | convolution fusion | flops 315371520 | bytes 6922432 | tf_op jit(solution)/shard_map/dot_general | solution.py:750
  218.1 11.6 %gather_rows.1 = bf16[4,48,1280]{2,1,0:T(8,128)(2,1)} custom-call(bf16[48,1280]{1,0:T(8,128)(2,1)} %fusion.block), custom_call_target="tpu_custom_call" | custom-call | tf_op jit(solution)/shard_map/gather_rows/pallas_call | solution.py:629
  229.8 1.2 multiply_reduce_fusion
  231.0 1.2 multiply_convert_fusion.1
  232.2 3.3 %fusion.5 = bf16[192,1280]{1,0:T(8,128)(2,1)S(1)} fusion(bf16[4,48,1280]{2,1,0:T(8,128)(2,1)} %gather_rows.1, bf16[192,1280]{1,0:T(8,128)(2,1)S(1)} %bitcast.64, bf16[1280,1280]{1,0:T(8,128)(2,1)} %bitcast.68), kind=kOutput, calls=%fused_computation.12 | convolution fusion | flops 631357440 | bytes 4751360 | tf_op jit(solution)/shard_map/dot_general | solution.py:33
  235.5 3.9 %convolution_convert_fusion.2 = bf16[192,1280]{1,0:T(8,128)(2,1)} fusion(bf16[192,1280]{1,0:T(8,128)(2,1)S(1)} %fusion.5, bf16[1280,1280]{1,0:T(8,128)(2,1)} %all-gather.2.cloned.1.call-done), kind=kOutput, calls=%fused_computation.2 | convolution fusion | flops 629391360 | bytes 4259840 | tf_op jit(solution)/shard_map/dot_general | solution.py:33
  239.4 10.5 %return_rows.1 = bf16[4,48,1280]{2,1,0:T(8,128)(2,1)} custom-call(bf16[4,48,1280]{2,1,0:T(8,128)(2,1)} %bitcast.62), custom_call_target="tpu_custom_call" | custom-call | tf_op jit(solution)/shard_map/return_rows/pallas_call | solution.py:629
  249.9 1.8 copy.17
  (48 shorter events, 1.5 us)
Async XLA Ops:
  7.2 134.8 %copy-start = (bf16[4,1280,40]{1,2,0:T(8,128)(2,1)S(1)}, bf16[4,1280,40]{1,2,0:T(8,128)(2,1)}, u32[]{:S(2)}) copy-start(bf16[4,1280,40]{1,2,0:T(8,128)(2,1)} %param.23) | copy-start | bytes 1228804
  7.2 228.3 %all-gather.2.cloned.1.call-start = ((), (), s32[]{:S(2)}) async-start(), calls=%async_computation | async-start | bytes 4096000 | tf_op jit(solution)/shard_map/all_gather | solution.py:674
  13.4 34.8 %copy-start.5 = (bf16[48,1280]{1,0:T(8,128)(2,1)S(1)}, bf16[48,1280]{1,0:T(8,128)(2,1)}, u32[]{:S(2)}) copy-start(bf16[48,1280]{1,0:T(8,128)(2,1)} %param.13) | copy-start | bytes 368644
  48.3 7.0 %copy-start.7 = (s32[1,32]{1,0:T(1,128)S(1)}, s32[1,32]{1,0:T(1,128)}, u32[]{:S(2)}) copy-start(s32[1,32]{1,0:T(1,128)} %param.16) | copy-start | bytes 388
  55.1 24.4 %copy-start.6 = (s32[1,512]{1,0:T(1,128)S(1)}, s32[1,512]{1,0:T(1,128)}, u32[]{:S(2)}) copy-start(s32[1,512]{1,0:T(1,128)} %param.15) | copy-start | bytes 6148
  55.2 24.9 %copy-start.8 = (s32[1,32]{1,0:T(1,128)S(1)}, s32[1,32]{1,0:T(1,128)}, u32[]{:S(2)}) copy-start(s32[1,32]{1,0:T(1,128)} %param.18) | copy-start | bytes 388
  55.2 24.9 %copy-start.9 = (s32[4]{0:T(128)S(1)}, s32[4]{0:T(128)}, u32[]{:S(2)}) copy-start(s32[4]{0:T(128)} %constant.106.clone) | copy-start | bytes 52
  80.5 61.5 %copy-start.2 = (bf16[1280,40]{0,1:T(8,128)(2,1)S(1)}, bf16[1280,40]{0,1:T(8,128)(2,1)}, u32[]{:S(2)}) copy-start(bf16[1280,40]{0,1:T(8,128)(2,1)} %param.20) | copy-start | bytes 307204
  80.6 61.5 %copy-start.3 = (bf16[1280,40]{0,1:T(8,128)(2,1)S(1)}, bf16[1280,40]{0,1:T(8,128)(2,1)}, u32[]{:S(2)}) copy-start(bf16[1280,40]{0,1:T(8,128)(2,1)} %param.21) | copy-start | bytes 307204
  80.6 61.5 %copy-start.4 = (bf16[40,1280]{1,0:T(8,128)(2,1)S(1)}, bf16[40,1280]{1,0:T(8,128)(2,1)}, u32[]{:S(2)}) copy-start(bf16[40,1280]{1,0:T(8,128)(2,1)} %refs_2_.1) | copy-start | bytes 307204
  140.0 2.0 copy-start.1
Sparse Core Ops, SparseCore 0:
  9.7 43.2 all-gather.1

commit v2 on v1

--- a/solution.py
+++ b/solution.py
@@ -54,11 +54,17 @@
         return (1 + 3 * self.core) * one + (4 - 3 * self.core) * two
 
 
-def greet_plane(spot):
+def greet_plane(spot, column=False):
     barrier = pltpu.get_barrier_semaphore()
     for who in (spot.at(1, 0), spot.at(-1, 0), spot.at(0, 1), spot.at(0, -1), spot.sibling):
         pl.semaphore_signal(barrier, inc=1, device_id={"blk": who}, device_id_type=MESH)
-    pl.semaphore_wait(barrier, 5)
+    if column:
+        at = lax.axis_index("req")
+        for d in (1, 2, 3):
+            pl.semaphore_signal(
+                barrier, inc=1, device_id={"req": (at + d) % 4}, device_id_type=MESH
+            )
+    pl.semaphore_wait(barrier, 8 if column else 5)
 
 
 def numbered(names):
@@ -202,27 +208,81 @@
     ]
 
 
+def column_steps(spot, shard, out, ssem, rsem, lsem):
+    at = lax.axis_index("req")
+    half = shard.shape[0] // 2
+    rows = pl.ds(pl.multiple_of(spot.core * half, 8), half)
+    local = pltpu.make_async_copy(shard, out.at[at], lsem)
+    local.start()
+    copies = []
+    for i, d in enumerate((2, 1, 3)):
+        copy = pltpu.make_async_remote_copy(
+            src_ref=shard.at[rows],
+            dst_ref=out.at[at, rows],
+            send_sem=ssem.at[i],
+            recv_sem=rsem.at[i],
+            device_id={"req": (at + d) % 4},
+            device_id_type=MESH,
+        )
+        copy.start()
+        copies.append(copy)
+    for _ in range(3):
+        yield
+    for i, d in ((1, 1), (2, 3), (0, 2)):
+        copies[i].wait_recv()
+        slot = (at - d + 4) % 4
+        copy = pltpu.make_async_remote_copy(
+            src_ref=out.at[slot, rows],
+            dst_ref=out.at[slot, rows],
+            send_sem=ssem.at[3 + i],
+            recv_sem=rsem.at[3 + i],
+            device_id={"blk": spot.sibling},
+            device_id_type=MESH,
+        )
+        copy.start()
+        copies.append(copy)
+        yield
+    local.wait()
+    for copy in copies[3:]:
+        copy.wait_recv()
+    for copy in copies:
+        copy.wait_send()
+
+
 ANY = pl.BlockSpec(memory_space=pl.ANY)
 VMEM = pl.BlockSpec(memory_space=pltpu.VMEM)
 
 
-def all_gather(shards, collective_id, name):
+def all_gather(shards, column, collective_id, name):
     count = len(shards)
+    both = shards + column
 
     def kernel(*refs):
+        ins = refs[: len(both)]
+        outs = refs[len(both) : 2 * len(both)]
+        scratch = refs[2 * len(both) :]
         spot = Spot()
-        greet_plane(spot)
-        run_all(gather_all(spot, refs[:count], refs[count : 2 * count], *refs[2 * count :]))
+        greet_plane(spot, bool(column))
+        steps = gather_all(spot, ins[:count], outs[:count], *scratch[:3])
+        if column:
+            steps.append(column_steps(spot, ins[count], outs[count], *scratch[3:]))
+        run_all(steps)
 
     return pl.pallas_call(
         kernel,
-        out_shape=[jax.ShapeDtypeStruct((BLK,) + s.shape, s.dtype) for s in shards],
-        in_specs=[ANY] * count,
-        out_specs=[ANY] * count,
-        scratch_shapes=gather_sems(count),
+        out_shape=[jax.ShapeDtypeStruct((BLK,) + s.shape, s.dtype) for s in shards]
+        + [jax.ShapeDtypeStruct((4,) + s.shape, s.dtype) for s in column],
+        in_specs=[ANY] * len(both),
+        out_specs=[ANY] * len(both),
+        scratch_shapes=gather_sems(count)
+        + [
+            pltpu.SemaphoreType.DMA((6,)),
+            pltpu.SemaphoreType.DMA((6,)),
+            pltpu.SemaphoreType.DMA,
+        ][: 3 * len(column)],
         compiler_params=pltpu.CompilerParams(collective_id=collective_id, has_side_effects=True),
         name=name,
-    )(*shards)
+    )(*both)
 
 
 def window(w):
@@ -230,81 +290,81 @@
 
 
 def attend_kernel(
-    tables, query_ref, cache_ref, proj_ref, marks_ref, num_ref, stats_ref, new_ref, acc, tops, dens
+    tables, query_ref, cache_ref, proj_ref, marks_ref, num_ref, stats_ref, new_ref,
+    masked, scores, weights, tops, dens, scales, acc,
 ):
     step = pl.program_id(0)
-    pages = pl.num_programs(0) - 1
-    owner = tables[0, step]
+    slot = tables[0, step]
     start = tables[1, step]
     length = tables[2, step]
     count = tables[3, step]
+    fresh = tables[6, step] > 0
+    final = tables[7, step] > 0
+    tree = tables[8, step] > 0
     factor = math.log2(math.e) / math.sqrt(HD)
+    lanes = lax.broadcasted_iota(jnp.int32, (TREE, 128), 1)
+    columns = lax.broadcasted_iota(jnp.int32, (TREE, 256), 1)
+    pair = 2 * TREE
+
+    def inside(w, i):
+        begin = window(w)[1] + HD * i
+        return (columns >= begin) & (columns < begin + HD)
 
     @pl.when(step == 0)
+    def _():
+        @pl.loop(0, BLK)
+        def _(r):
+            num_ref[r] = jnp.zeros(num_ref.shape[1:], num_ref.dtype)
+            stats_ref[r] = jnp.where(lanes < 64, LOWEST, 0.0)
+
+    @pl.when(fresh)
     def _():
         tops[...] = jnp.full_like(tops, LOWEST)
         dens[...] = jnp.zeros_like(dens)
-
-        @pl.loop(0, BLK)
-        def _(r):
-            acc[r] = jnp.zeros(acc.shape[1:], acc.dtype)
-
-    lanes = lax.broadcasted_iota(jnp.int32, (TREE, 128), 1)
-    columns = lax.broadcasted_iota(jnp.int32, (TREE, 256), 1)
-
-    def merge(query, key_at, value_at, seen):
-        tops_old = tops[owner]
-        dens_old = dens[owner]
-        tops_new, dens_new = tops_old, dens_old
+        acc[...] = jnp.zeros_like(acc)
         for w in range(8):
-            first, begin = window(w)
-            here = [
-                (columns >= begin + HD * i) & (columns < begin + HD * (i + 1)) for i in range(2)
-            ]
-            picked = query(first)
-            stacked = jnp.concatenate(
-                [picked * here[i].astype(jnp.float32).astype(jnp.bfloat16) for i in range(2)],
-                axis=0,
+            picked = query_ref[0, pl.ds(0, TREE), pl.ds(window(w)[0], 256)]
+            for i in range(2):
+                one = inside(w, i).astype(jnp.float32).astype(jnp.bfloat16)
+                masked[w, pl.ds(TREE * i, TREE)] = picked * one
+
+    def merge(key_at, value_at, seen, keys):
+        for w in range(8):
+            scores[pl.ds(pair * w, pair), pl.ds(0, keys)] = dot_t(
+                masked[w], key_at(window(w)[0])
             )
-            scores = dot_t(stacked, key_at(first)) * factor
-            weights = []
-            scales = []
-            for i in range(2):
-                head = 2 * w + i
-                part = jnp.where(seen, scores[i * TREE : (i + 1) * TREE], LOWEST)
-                before = tops_old[:, head : head + 1]
-                top = jnp.maximum(before, jnp.ceil(jnp.max(part, axis=1, keepdims=True)))
-                weight = jnp.where(seen, jnp.exp2(part - top), 0.0)
-                scale = jnp.exp2(before - top)
-                total = dens_old[:, head : head + 1] * scale + jnp.sum(
-                    weight, axis=1, keepdims=True
-                )
-                tops_new = jnp.where(lanes == head, top, tops_new)
-                dens_new = jnp.where(lanes == head, total, dens_new)
-                weights.append(weight.astype(jnp.bfloat16))
-                scales.append(scale)
+        for part in range(4):
+            rows = pl.ds(2 * pair * part, 2 * pair)
+            shown = jnp.concatenate([seen] * 4, axis=0) if seen.shape[0] > 1 else seen
+            part_scores = jnp.where(shown, scores[rows, pl.ds(0, keys)] * factor, LOWEST)
+            before = tops[rows, :]
+            top = jnp.maximum(
+                before, jnp.ceil(jnp.max(part_scores, axis=1, keepdims=True))
+            )
+            weight = jnp.where(shown, jnp.exp2(part_scores - top[:, :keys]), 0.0)
+            scale = jnp.exp2(before - top)
+            tops[rows, :] = top
+            scales[rows, :] = scale
+            dens[rows, :] = dens[rows, :] * scale + jnp.sum(weight, axis=1, keepdims=True)
+            weights[rows, pl.ds(0, keys)] = weight.astype(jnp.bfloat16)
+        for w in range(8):
+            rows = pl.ds(pair * w, pair)
             added = jnp.dot(
-                jnp.concatenate(weights, axis=0),
-                value_at(first),
+                weights[rows, pl.ds(0, keys)],
+                value_at(window(w)[0]),
                 preferred_element_type=jnp.float32,
             )
-            window_scale = jnp.where(here[0], scales[0], jnp.where(here[1], scales[1], 1.0))
-            window_sum = jnp.where(
-                here[0], added[:TREE], jnp.where(here[1], added[TREE:], 0.0)
-            )
-            old = acc[owner, :, pl.ds(first, 256)]
-            acc[owner, :, pl.ds(first, 256)] = old * window_scale + window_sum
-        tops[owner] = tops_new
-        dens[owner] = dens_new
-
-    @pl.when(step < pages)
+            scale = scales[rows, :]
+            acc[w] = acc[w] * jnp.concatenate([scale, scale], axis=1) + added
+
+    @pl.when(jnp.logical_not(tree))
     def _():
-        seen = lax.broadcasted_iota(jnp.int32, (TREE, PAGE), 1) + start < length
+        seen = lax.broadcasted_iota(jnp.int32, (1, PAGE), 1) + start < length
         merge(
-            lambda first: query_ref[0, pl.ds(0, TREE), pl.ds(first, 256)],
             lambda first: cache_ref[0, 0, :, pl.ds(first, 256)],
             lambda first: cache_ref[0, 1, :, pl.ds(first, 256)],
             seen,
+            PAGE,
         )
         row0 = length - start
         touched = (row0 < PAGE) & (row0 + count > 0)
@@ -321,36 +381,53 @@
             rows = lax.broadcasted_iota(jnp.int32, (PAGE, WIDTH), 0) - row0
             hit = (rows >= 0) & (rows < count)
             for i in range(2):
-                fresh = jnp.dot(
+                taken = jnp.dot(
                     hot,
                     query_ref[0, pl.ds(TREE + 8 * i, 8), :],
                     preferred_element_type=jnp.float32,
                 )
                 kept = cache_ref[0, i].astype(jnp.float32)
-                new_ref[0, i] = jnp.where(hit, fresh, kept).astype(jnp.bfloat16)
-
-    @pl.when(step == pages)
+                new_ref[0, i] = jnp.where(hit, taken, kept).astype(jnp.bfloat16)
+
+    @pl.when(tree)
     def _():
         merge(
-            lambda first: query_ref[0, pl.ds(0, TREE), pl.ds(first, 256)],
             lambda first: proj_ref[:, pl.ds(WIDTH + first, 256)],
             lambda first: proj_ref[:, pl.ds(2 * WIDTH + first, 256)],
             marks_ref[...] > 0.5,
-        )
-
-        @pl.loop(0, BLK)
-        def _(r):
-            num_ref[r] = acc[r].astype(jnp.bfloat16)
-            stats_ref[r] = jnp.where(lanes < 64, tops[r], pltpu.roll(dens[r], 64, 1))
+            TREE,
+        )
+
+    @pl.when(final)
+    def _():
+        carried = None
+        for w in range(8):
+            picked = jnp.where(
+                inside(w, 0),
+                acc[w, pl.ds(0, TREE), :],
+                jnp.where(inside(w, 1), acc[w, pl.ds(TREE, TREE), :], 0.0),
+            )
+            head = picked[:, :128]
+            if w % 4:
+                head = head + carried
+            carried = picked[:, 128:]
+            num_ref[slot, :, pl.ds(window(w)[0], 128)] = head.astype(jnp.bfloat16)
+            if w % 4 == 3:
+                num_ref[slot, :, pl.ds(window(w)[0] + 128, 128)] = carried.astype(jnp.bfloat16)
+        stats = jnp.full((TREE, 128), LOWEST, jnp.float32)
+        for head in range(H):
+            rows = pl.ds(TREE * head, TREE)
+            stats = jnp.where(lanes == head, tops[rows, :], stats)
+            stats = jnp.where(lanes == 64 + head, dens[rows, :], stats)
+        stats_ref[slot] = stats
 
 
 def attend(tables, gathered, cache, projected, marks):
-    pages = cache.shape[2] // PAGE
+    steps = tables.shape[1]
     rows = gathered.shape[1]
-    page_block = pl.BlockSpec(
-        (1, 2, PAGE, WIDTH), lambda p, t: (0, 0, jnp.minimum(p, pages - 1), 0)
-    )
+    page_block = pl.BlockSpec((1, 2, PAGE, WIDTH), lambda p, t: (0, 0, t[5, p], 0))
     whole3 = lambda p, t: (0, 0, 0)
+    lines = 2 * TREE * 8
     return pl.pallas_call(
         attend_kernel,
         out_shape=[
@@ -360,7 +437,7 @@
         ],
         grid_spec=pltpu.PrefetchScalarGridSpec(
             num_scalar_prefetch=1,
-            grid=(pages + 1,),
+            grid=(steps,),
             in_specs=[
                 pl.BlockSpec((1, rows, WIDTH), lambda p, t: (t[4, p], 0, 0)),
                 page_block,
@@ -373,9 +450,13 @@
                 page_block,
             ],
             scratch_shapes=[
-                pltpu.VMEM((BLK, TREE, WIDTH), jnp.float32),
-                pltpu.VMEM((BLK, TREE, 128), jnp.float32),
-                pltpu.VMEM((BLK, TREE, 128), jnp.float32),
+                pltpu.VMEM((8, 2 * TREE, 256), jnp.bfloat16),
+                pltpu.VMEM((lines, 128), jnp.float32),
+                pltpu.VMEM((lines, 128), jnp.bfloat16),
+                pltpu.VMEM((lines, 128), jnp.float32),
+                pltpu.VMEM((lines, 128), jnp.float32),
+                pltpu.VMEM((lines, 128), jnp.float32),
+                pltpu.VMEM((8, 2 * TREE, 256), jnp.float32),
             ],
         ),
         compiler_params=pltpu.CompilerParams(vmem_limit_bytes=48 * 1024 * 1024),
@@ -572,7 +653,7 @@
             pltpu.SemaphoreType.DMA((len(REDUCE),)),
             pltpu.SemaphoreType.DMA((len(REDUCE),)),
         ]
-        + gather_sems(count)
+        + (gather_sems(count) if count else [pltpu.SemaphoreType.DMA] * 3)
         + block(16)
         + block(16)
         + block(4)
@@ -671,9 +752,16 @@
     myself = lax.axis_index("blk")
     width = WIDTH
     pool_pages = cache.shape[2] // PAGE
-    patch = lax.all_gather(w_patch.T, "req", axis=0, tiled=True)
     normed = rms_rows(tree_input)
-    (qkv,) = all_gather([w_qkv.T], 1, "gather_qkv")
+    draft_mine = lax.dynamic_index_in_dim(
+        w_draft.transpose(0, 2, 1), lax.axis_index("req"), 0, keepdims=False
+    )
+    qkv, full_out, full_up, full_down, full_draft, patch = all_gather(
+        [w_qkv.T, w_out.T, w_up.T, w_down, draft_mine], [w_patch.T], 1, "gather_weights"
+    )
+    full_out, full_up, full_down, full_draft, patch = (
+        w.reshape(width, width) for w in (full_out, full_up, full_down, full_draft, patch)
+    )
     projected = dot_t(normed, qkv.reshape(3 * width, width)).astype(jnp.bfloat16)
 
     page_row = page_table[0]
@@ -699,17 +787,38 @@
     def of_owner(row):
         return jnp.sum(jnp.where(owner_hot, row[None, :], 0), axis=1)
 
+    my_end = jnp.sum(jnp.where(jnp.arange(requests) == myself, page_ends, 0))
+
     def with_tree(row, last):
         return jnp.concatenate([row, jnp.reshape(jnp.asarray(last, jnp.int32), (1,))])
 
+    spots = with_tree(2 * where_at, 2 * my_end - 1)
+    rank = jnp.sum((spots[None, :] < spots[:, None]).astype(jnp.int32), axis=1)
+    sorted_hot = rank[None, :] == jnp.arange(pool_pages + 1, dtype=jnp.int32)[:, None]
     owners = with_tree(safe_owner, myself)
-    tables = jnp.stack(
+    page_ids = with_tree(jnp.arange(pool_pages, dtype=jnp.int32), -1)
+    unsorted = jnp.stack(
         [
             owners % 2 * 16 + owners // 2,
             with_tree((where_at - of_owner(offsets)) * PAGE, 0),
             with_tree(of_owner(length_row), 0),
             with_tree(of_owner(accepted), 0),
             owners,
+            page_ids,
+        ]
+    )
+    table = jnp.sum(jnp.where(sorted_hot[None], unsorted[:, None, :], 0), axis=2)
+    owners, page_ids = table[4], table[5]
+    changes = (owners[1:] != owners[:-1]).astype(jnp.int32)
+    one = jnp.ones((1,), jnp.int32)
+    beside = jnp.concatenate([page_ids[1:2], page_ids[:-1]])
+    tables = jnp.concatenate(
+        [
+            table[:5],
+            jnp.where(page_ids < 0, beside, page_ids)[None],
+            jnp.concatenate([one, changes])[None],
+            jnp.concatenate([changes, one])[None],
+            (page_ids < 0).astype(jnp.int32)[None],
         ]
     )
     marks = ancestors(parents[0])
@@ -727,6 +836,7 @@
     ).astype(jnp.bfloat16)
     (gathered,) = all_gather(
         [jnp.concatenate([projected[:, :width], send_rows[:, :width], send_rows[:, width:]])],
+        [],
         2,
         "gather_query",
     )
@@ -735,15 +845,7 @@
         jnp.arange(128, dtype=jnp.int32)[:, None]
         == jnp.arange(width, dtype=jnp.int32)[None, :] // HD
     ).astype(jnp.bfloat16)
-    draft_mine = lax.dynamic_index_in_dim(
-        w_draft.transpose(0, 2, 1), lax.axis_index("req"), 0, keepdims=False
-    )
-    attended, full_out, full_up, full_down, full_draft = reduce_and_gather(
-        num, stats, spread, [w_out.T, w_up.T, w_down, draft_mine], 3
-    )
-    full_out, full_up, full_down, full_draft = (
-        w.reshape(width, width) for w in (full_out, full_up, full_down, full_draft)
-    )
+    (attended,) = reduce_and_gather(num, stats, spread, [], 3)
     proj = dot_t(attended, full_out).astype(jnp.bfloat16)
     mid = (tree_input.astype(jnp.float32) + proj.astype(jnp.float32)).astype(jnp.bfloat16)
     hidden = jax.nn.gelu(dot_t(rms_rows(mid), full_up)).astype(jnp.bfloat16)

time: 259 us -> 201 us (0.78)
  Pallas kernels: 209 us -> 163 us
  between operations: 14.3 us -> 1.6 us
  other arithmetic: 6.41 us -> 9.68 us
    pallas_call x1, Pallas kernels: 69.5 us -> 25.6 us  [reduce_and_gather(): pl.pallas_call(kernel, out_shape=[jax.ShapeDtypeStruct((TREE, WIDTH), jnp...]
    pallas_call x2, Pallas kernels: 58.1 us -> 96.5 us  [all_gather(): pl.pallas_call(kernel, out_shape=[jax.ShapeDtypeStruct((BLK,) + s.shape,...]
    pallas_call x1, Pallas kernels: 59.4 us -> 21.1 us  [attend(): pl.pallas_call(attend_kernel, out_shape=[jax.ShapeDtypeStruct((BLK, TREE,...]
  transfers between devices with their start and end apart: 1 -> 0, of which waited for: 0 -> 0; matrix products, arithmetic and copies ran while one was open for 10% -> 0% of each run, Pallas kernels for 77% -> 0%
where the time goes in v2:
time: 201 us; the launch traced here: 200 us
  Pallas kernels  163 us (81%)
  matrix products  22.5 us (11%)
  other arithmetic  9.68 us (5%)
  local copies, waits for them, and re-layouts  3.56 us (2%)
    pallas_call x2, Pallas kernels, all_gather(): pl.pallas_call(kernel, out_shape=[jax.ShapeDtypeStruct((BLK,) + s.shape,...  96.5 us
    pallas_call x1, Pallas kernels, reduce_and_gather(): pl.pallas_call(kernel, out_shape=[jax.ShapeDtypeStruct((TREE, WIDTH), jnp...  25.6 us
    pallas_call x1, Pallas kernels, attend(): pl.pallas_call(attend_kernel, out_shape=[jax.ShapeDtypeStruct((BLK, TREE,...  21.1 us
    pallas_call x2, Pallas kernels, over_column(): pl.pallas_call(column_kernel(exchange), out_shape=jax.ShapeDtypeStruct(sh...  19.9 us
    dot_general x4, matrix products, dot_t(): lax.dot_general(left, right, (((1,), (1,)), ((), ())), preferred_element_...  13.6 us
    dot_general x1, matrix products, on_device(): feedforward = jnp.dot(hidden, full_down, preferred_element_type=jnp.float32)  5.34 us

profile of v2, /device:TPU:2, one launch (start us, length us, event | category | flops | bytes accessed | tf_op | source)
XLA Modules:
  0.0 200.5 jit_solution(241748194436685380)
XLA Ops:
  0.6 0.9 fusion.29
  1.5 0.8 fusion.28
  2.4 0.9 fusion.27
  3.2 0.7 fusion.70
  4.0 1.4 fusion.45
  6.1 0.9 select_reduce_fusion.3
  7.1 0.7 dynamic-slice_bitcast_fusion.refs_4_
  7.7 72.8 %gather_weights.1 = (bf16[32,120,1280]{2,1,0:T(8,128)(2,1)}, bf16[32,40,1280]{2,1,0:T(8,128)(2,1)}, bf16[32,40,1280]{2,1,0:T(8,128)(2,1)}, bf16[32,40,1280]{2,1,...) custom-call(bf16[120,1280]{1,0:T(8,128)(2,1)} %bitcast.73, bf16[40,1280]{1,0:T(8,128)(2,1)} %bitcast.74, ...), custom_call_target="tpu_custom_call" | custom-call | tf_op jit(solution)/shard_map/gather_weights/pallas_call | solution.py:271
  80.5 1.0 fusion.7
  81.6 6.9 %convolution_convert_fusion.proj_ref = bf16[48,3840]{1,0:T(8,128)(2,1)S(1)} fusion(bf16[3840,1280]{1,0:T(8,128)(2,1)} %bitcast.64, bf16[48,1280]{1,0:T(8,128)(2,1)} %param.13, f32[48]{0:T(128)S(1)} %add_rsqrt_fusion.2), kind=kOutput, calls=%fused_computation | convolution fusion | flops 472227840 | bytes 10322112 | tf_op jit(solution)/shard_map/dot_general | solution.py:33
  88.7 0.7 pad_maximum_fusion.refs_0_
  89.4 23.7 %gather_query.1.query_ref = bf16[32,64,1280]{2,1,0:T(8,128)(2,1)} custom-call(bf16[64,1280]{1,0:T(8,128)(2,1)} %pad_maximum_fusion.refs_0_), custom_call_target="tpu_custom_call" | custom-call | tf_op jit(solution)/shard_map/gather_query/pallas_call | solution.py:271
  116.5 0.7 compare_select_fusion
  117.4 21.1 %attend.1 = (bf16[32,48,1280]{2,1,0:T(8,128)(2,1)S(1)}, f32[32,48,128]{2,1,0:T(8,128)S(1)}, bf16[1,2,2048,1280]{3,2,1,0:T(8,128)(2,1)}) custom-call(s32[9,17]{1,0:T(8,128)S(1)} %concatenate.80.tables, bf16[32,64,1280]{2,1,0:T(8,128)(2,1)} %gather_query.1.query_ref, bf16[1,2,2048,1280]{3,2,1,0:T(8,128)(2,1)} %cache_ref.1, ...), custom_call_target="tpu_custom_call" | custom-call | tf_op jit(solution)/shard_map/attend/pallas_call | solution.py:431
  138.6 25.6 %reduce_and_gather.1 = bf16[48,1280]{1,0:T(8,128)(2,1)S(1)} custom-call(bf16[32,48,1280]{2,1,0:T(8,128)(2,1)S(1)} %get-tuple-element.13.num_ref, f32[32,48,128]{2,1,0:T(8,128)S(1)} %get-tuple-element.14.stats_ref, bf16[128,1280]{1,0:T(8,128)(2,1)S(1)} %fusion.6.spread_ref), custom_call_target="tpu_custom_call" | custom-call | tf_op jit(solution)/shard_map/reduce_and_gather/pallas_call | solution.py:646
  164.2 1.2 multiply_reduce_fusion.1
  165.4 5.3 %fusion.block = bf16[48,1280]{1,0:T(8,128)(2,1)} fusion(f32[48,1280]{1,0:T(8,128)S(1)} %get-tuple-element.37, bf16[1280,1280]{1,0:T(8,128)(2,1)} %bitcast.66, bf16[1280,1280]{1,0:T(8,128)(2,1)} %bitcast.65, f32[48]{0:T(128)S(1)} %add_rsqrt_fusion.1), kind=kOutput, calls=%fused_computation.4 | convolution fusion | flops 315371520 | bytes 6922432 | tf_op jit(solution)/shard_map/dot_general | solution.py:852
  170.8 9.7 %gather_rows.1 = bf16[4,48,1280]{2,1,0:T(8,128)(2,1)} custom-call(bf16[48,1280]{1,0:T(8,128)(2,1)} %fusion.block), custom_call_target="tpu_custom_call" | custom-call | tf_op jit(solution)/shard_map/gather_rows/pallas_call | solution.py:710
  180.5 1.2 multiply_reduce_fusion
  181.7 1.2 multiply_convert_fusion.1
  182.9 3.4 %fusion.5 = bf16[192,1280]{1,0:T(8,128)(2,1)S(1)} fusion(bf16[4,48,1280]{2,1,0:T(8,128)(2,1)} %gather_rows.1, bf16[192,1280]{1,0:T(8,128)(2,1)S(1)} %bitcast.71, bf16[1280,1280]{1,0:T(8,128)(2,1)} %bitcast.79), kind=kOutput, calls=%fused_computation.12 | convolution fusion | flops 631357440 | bytes 4751360 | tf_op jit(solution)/shard_map/dot_general | solution.py:33
  186.4 2.0 %convolution_convert_fusion.2 = bf16[192,1280]{1,0:T(8,128)(2,1)} fusion(bf16[192,1280]{1,0:T(8,128)(2,1)S(1)} %fusion.5, bf16[1280,1280]{1,0:T(8,128)(2,1)S(1)} %bitcast.67), kind=kOutput, calls=%fused_computation.2 | convolution fusion | flops 629391360 | bytes 4259840 | tf_op jit(solution)/shard_map/dot_general | solution.py:33
  188.4 10.2 %return_rows.1 = bf16[4,48,1280]{2,1,0:T(8,128)(2,1)} custom-call(bf16[4,48,1280]{2,1,0:T(8,128)(2,1)} %bitcast.69), custom_call_target="tpu_custom_call" | custom-call | tf_op jit(solution)/shard_map/return_rows/pallas_call | solution.py:710
  198.6 1.8 copy.29
  (57 shorter events, 4.0 us)
Async XLA Ops:
  0.6 6.4 %copy-start = (bf16[4,1280,40]{1,2,0:T(8,128)(2,1)S(1)}, bf16[4,1280,40]{1,2,0:T(8,128)(2,1)}, u32[]{:S(2)}) copy-start(bf16[4,1280,40]{1,2,0:T(8,128)(2,1)} %param.23) | copy-start | bytes 1228804
  88.5 24.6 %copy-start.4 = (s32[1,512]{1,0:T(1,128)S(1)}, s32[1,512]{1,0:T(1,128)}, u32[]{:S(2)}) copy-start(s32[1,512]{1,0:T(1,128)} %param.15) | copy-start | bytes 6148
  88.5 25.0 %copy-start.7 = (s32[1,32]{1,0:T(1,128)S(1)}, s32[1,32]{1,0:T(1,128)}, u32[]{:S(2)}) copy-start(s32[1,32]{1,0:T(1,128)} %param.16) | copy-start | bytes 388
  88.5 25.0 %copy-start.6 = (s32[1,32]{1,0:T(1,128)S(1)}, s32[1,32]{1,0:T(1,128)}, u32[]{:S(2)}) copy-start(s32[1,32]{1,0:T(1,128)} %param.18) | copy-start | bytes 388
  88.5 25.0 %copy-start.8 = (s32[4]{0:T(128)S(1)}, s32[4]{0:T(128)}, u32[]{:S(2)}) copy-start(s32[4]{0:T(128)} %constant.116.clone) | copy-start | bytes 52
  88.6 25.5 %copy-start.5 = (s32[1,17]{1,0:T(1,128)S(1)}, s32[1,17]{1,0:T(1,128)}, u32[]{:S(2)}) copy-start(s32[1,17]{1,0:T(1,128)} %constant.102.clone.1) | copy-start | bytes 208
  138.5 25.6 %copy-start.2 = (bf16[32,40,1280]{2,1,0:T(8,128)(2,1)S(1)}, bf16[32,40,1280]{2,1,0:T(8,128)(2,1)}, u32[]{:S(2)}) copy-start(bf16[32,40,1280]{2,1,0:T(8,128)(2,1)} %get-tuple-element.15) | copy-start | bytes 9830404
  138.5 25.7 %copy-start.3 = (bf16[48,1280]{1,0:T(8,128)(2,1)S(1)}, bf16[48,1280]{1,0:T(8,128)(2,1)}, u32[]{:S(2)}) copy-start(bf16[48,1280]{1,0:T(8,128)(2,1)} %param.13) | copy-start | bytes 368644
  182.9 3.5 %copy-start.1 = (bf16[4,320,1280]{2,1,0:T(8,128)(2,1)S(1)}, bf16[4,320,1280]{2,1,0:T(8,128)(2,1)}, u32[]{:S(2)}) copy-start(bf16[4,320,1280]{2,1,0:T(8,128)(2,1)} %get-tuple-element.19) | copy-start | bytes 9830404

commit v3 on v1

--- a/solution.py
+++ b/solution.py
@@ -54,11 +54,17 @@
         return (1 + 3 * self.core) * one + (4 - 3 * self.core) * two
 
 
-def greet_plane(spot):
+def greet_plane(spot, column=False):
     barrier = pltpu.get_barrier_semaphore()
     for who in (spot.at(1, 0), spot.at(-1, 0), spot.at(0, 1), spot.at(0, -1), spot.sibling):
         pl.semaphore_signal(barrier, inc=1, device_id={"blk": who}, device_id_type=MESH)
-    pl.semaphore_wait(barrier, 5)
+    if column:
+        at = lax.axis_index("req")
+        for d in (1, 3):
+            pl.semaphore_signal(
+                barrier, inc=1, device_id={"req": (at + d) % 4}, device_id_type=MESH
+            )
+    pl.semaphore_wait(barrier, 7 if column else 5)
 
 
 def numbered(names):
@@ -202,6 +208,56 @@
     ]
 
 
+COLUMN = numbered(["L", "R", "OA", "OB", "S1", "S2", "S3"])
+
+
+def column_steps(spot, shard, out, ssem, rsem, lsem):
+    at = lax.axis_index("req")
+    above, below = (at + 1) % 4, (at + 3) % 4
+    half = shard.shape[0] // 2
+    base = spot.core * half
+    rows = pl.ds(pl.multiple_of(base, 8), half)
+    parts = [pl.ds(pl.multiple_of(base + i * (half // 2), 8), half // 2) for i in range(2)]
+    sent = {}
+
+    def put(event, src, slot, part, device):
+        copy = pltpu.make_async_remote_copy(
+            src_ref=src,
+            dst_ref=out.at[slot, part],
+            send_sem=ssem.at[COLUMN[event]],
+            recv_sem=rsem.at[COLUMN[event]],
+            device_id=device,
+            device_id_type=MESH,
+        )
+        copy.start()
+        sent[event] = copy
+
+    local = pltpu.make_async_copy(shard, out.at[at], lsem)
+    local.start()
+    put("L", shard.at[rows], at, rows, {"req": above})
+    put("R", shard.at[rows], at, rows, {"req": below})
+    for _ in range(2):
+        yield
+    sent["L"].wait_recv()
+    put("OA", out.at[below, parts[0]], below, parts[0], {"req": above})
+    put("S1", out.at[below, rows], below, rows, {"blk": spot.sibling})
+    sent["R"].wait_recv()
+    put("OB", out.at[above, parts[1]], above, parts[1], {"req": below})
+    put("S2", out.at[above, rows], above, rows, {"blk": spot.sibling})
+    for _ in range(3):
+        yield
+    sent["OA"].wait_recv()
+    sent["OB"].wait_recv()
+    far = (at + 2) % 4
+    put("S3", out.at[far, rows], far, rows, {"blk": spot.sibling})
+    yield
+    local.wait()
+    for event in ("S1", "S2", "S3"):
+        sent[event].wait_recv()
+    for event in COLUMN:
+        sent[event].wait_send()
+
+
 ANY = pl.BlockSpec(memory_space=pl.ANY)
 VMEM = pl.BlockSpec(memory_space=pltpu.VMEM)
 
@@ -217,7 +273,7 @@
     return pl.pallas_call(
         kernel,
         out_shape=[jax.ShapeDtypeStruct((BLK,) + s.shape, s.dtype) for s in shards],
-        in_specs=[ANY] * count,
+        in_specs=[VMEM] * count,
         out_specs=[ANY] * count,
         scratch_shapes=gather_sems(count),
         compiler_params=pltpu.CompilerParams(collective_id=collective_id, has_side_effects=True),
@@ -225,162 +281,336 @@
     )(*shards)
 
 
+def iota(shape, dim):
+    return lax.broadcasted_iota(jnp.int32, shape, dim)
+
+
+def to_column(row):
+    n = row.shape[1]
+    return jnp.sum(jnp.where(iota((n, n), 0) == iota((n, n), 1), row, 0), axis=1, keepdims=True)
+
+
+def to_row(column):
+    n = column.shape[0]
+    return jnp.sum(jnp.where(iota((n, n), 0) == iota((n, n), 1), column, 0), axis=0, keepdims=True)
+
+
+def tree_marks(parent_row, leaf):
+    square = (TREE, TREE)
+    climb = (to_column(parent_row) == iota(square, 1)).astype(jnp.float32)
+    current = (iota(square, 0) == iota(square, 1)).astype(jnp.float32)
+    marks = current
+    for _ in range(DEPTH - 1):
+        current = jnp.dot(current, climb, preferred_element_type=jnp.float32)
+        marks = jnp.maximum(marks, current)
+    chosen = jnp.sum(jnp.where(iota(square, 0) == leaf, marks, 0.0), axis=0, keepdims=True)
+    upto = jnp.where(iota(square, 0) <= iota(square, 1), to_column(chosen), 0.0)
+    nth = (jnp.sum(upto, axis=0, keepdims=True) - 1.0).astype(jnp.int32)
+    picker = (chosen > 0.5) & (nth == iota((16, TREE), 0))
+    return marks, picker.astype(jnp.float32)
+
+
+def page_tables(page_row, length_row, leaf_row, myself, pool_pages):
+    requests = length_row.shape[1]
+    npages = (length_row + (DEPTH + PAGE - 1)) // PAGE
+    square = (requests, requests)
+    ends = jnp.sum(
+        jnp.where(iota(square, 0) <= iota(square, 1), to_column(npages), 0), axis=0, keepdims=True
+    )
+    offsets = ends - npages
+    my_end = jnp.sum(jnp.where(iota((1, requests), 1) == myself, ends, 0), axis=1, keepdims=True)
+    accepted = 1 + sum((leaf_row >= first).astype(jnp.int32) for first in LEVEL_START[1:-1])
+    lines = 24
+    line = iota((lines, 1), 0)
+    slots = page_row.shape[1]
+    located = page_row == myself * pool_pages + iota((lines, slots), 0)
+    where_at = jnp.sum(jnp.where(located, iota((lines, slots), 1), 0), axis=1, keepdims=True)
+    owner = jnp.sum((ends <= where_at).astype(jnp.int32), axis=1, keepdims=True)
+    hot = owner == iota((lines, requests), 1)
+
+    def of_owner(row):
+        return jnp.sum(jnp.where(hot, row, 0), axis=1, keepdims=True)
+
+    is_tree = line == pool_pages
+    spare = line > pool_pages
+    owner_or_me = jnp.where(is_tree, myself, jnp.minimum(owner, requests - 1))
+    place = owner_or_me % 2 * (requests // 2) + owner_or_me // 2
+    start = jnp.where(is_tree, 0, (where_at - of_owner(offsets)) * PAGE)
+    length = jnp.where(is_tree, 0, of_owner(length_row))
+    count = jnp.where(is_tree, 0, of_owner(accepted))
+    spots = jnp.where(is_tree, 2 * my_end - 1, jnp.where(spare, 4 * slots + line, 2 * where_at))
+    rank = jnp.sum((to_row(spots) < spots).astype(jnp.int32), axis=1, keepdims=True)
+    wide = (lines, 128)
+
+    def in_order(column):
+        return jnp.sum(jnp.where(rank == iota(wide, 1), column, 0), axis=0, keepdims=True)
+
+    def as_it_lies(column):
+        return jnp.sum(jnp.where(line == iota(wide, 1), column, 0), axis=0, keepdims=True)
+
+    columns = [place, start, length, count, owner_or_me, line]
+    rows = [in_order(column) for column in columns]
+    lane = iota((1, 128), 1)
+    fresh = ((rows[4] != pltpu.roll(rows[4], 1, 1)) | (lane == 0)).astype(jnp.int32)
+    last = jnp.max(
+        jnp.where((place == iota(wide, 1)) & jnp.logical_not(spare), rank, -1),
+        axis=0,
+        keepdims=True,
+    )
+    last = jnp.where(last < 0, pool_pages + 1, last)
+    rows += [fresh, fresh, in_order(is_tree.astype(jnp.int32)), last]
+    return rows, [as_it_lies(column) for column in (owner_or_me, start, length, count)]
+
+
+def prepare(shard, patch, tree_input, page_row, length_row, leaf_row, parent_row, pool_pages):
+    def kernel(
+        shard_ref, patch_ref, x_ref, page_ref, length_ref, leaf_ref, parent_ref,
+        full_ref, full_patch_ref, normed_ref, steps_ref, pages_ref, marks_ref, picker_ref,
+        *scratch,
+    ):
+        spot = Spot()
+        greet_plane(spot, True)
+        steps = gather_all(spot, [shard_ref], [full_ref], *scratch[:3])
+        steps.append(column_steps(spot, patch_ref, full_patch_ref, *scratch[3:]))
+        for one in steps:
+            next(one)
+        normed_ref[...] = rms_rows(x_ref[...])
+        leaf = jnp.sum(
+            jnp.where(iota(leaf_ref.shape, 1) == spot.me, leaf_ref[...], 0), axis=1, keepdims=True
+        )
+        marks_ref[...], picker = tree_marks(parent_ref[...], leaf)
+        picker_ref[...] = picker.astype(jnp.bfloat16)
+        in_order, as_they_lie = page_tables(
+            page_ref[...], length_ref[...], leaf_ref[...], spot.me, pool_pages
+        )
+        for k, row in enumerate(in_order):
+            steps_ref[pl.ds(k, 1), :] = row
+        for k, row in enumerate(as_they_lie):
+            pages_ref[pl.ds(k, 1), :] = row
+        run_all(steps)
+
+    return pl.pallas_call(
+        kernel,
+        out_shape=[
+            jax.ShapeDtypeStruct((BLK,) + shard.shape, shard.dtype),
+            jax.ShapeDtypeStruct((4,) + patch.shape, patch.dtype),
+            jax.ShapeDtypeStruct(tree_input.shape, jnp.bfloat16),
+            jax.ShapeDtypeStruct((10, 128), jnp.int32),
+            jax.ShapeDtypeStruct((4, 128), jnp.int32),
+            jax.ShapeDtypeStruct((TREE, TREE), jnp.float32),
+            jax.ShapeDtypeStruct((16, TREE), jnp.bfloat16),
+        ],
+        in_specs=[VMEM] * 7,
+        out_specs=[ANY, ANY] + [VMEM] * 5,
+        scratch_shapes=gather_sems(1)
+        + [
+            pltpu.SemaphoreType.DMA((len(COLUMN),)),
+            pltpu.SemaphoreType.DMA((len(COLUMN),)),
+            pltpu.SemaphoreType.DMA,
+        ],
+        compiler_params=pltpu.CompilerParams(collective_id=1, has_side_effects=True),
+        name="prepare",
+    )(shard, patch, tree_input, page_row, length_row, leaf_row, parent_row)
+
+
 def window(w):
     return 128 * (5 * (w // 4) + w % 4), 32 * (w % 4)
 
 
-def attend_kernel(
-    tables, query_ref, cache_ref, proj_ref, marks_ref, num_ref, stats_ref, new_ref, acc, tops, dens
-):
-    step = pl.program_id(0)
-    pages = pl.num_programs(0) - 1
-    owner = tables[0, step]
-    start = tables[1, step]
-    length = tables[2, step]
-    count = tables[3, step]
-    factor = math.log2(math.e) / math.sqrt(HD)
-
-    @pl.when(step == 0)
-    def _():
-        tops[...] = jnp.full_like(tops, LOWEST)
-        dens[...] = jnp.zeros_like(dens)
-
-        @pl.loop(0, BLK)
-        def _(r):
-            acc[r] = jnp.zeros(acc.shape[1:], acc.dtype)
-
-    lanes = lax.broadcasted_iota(jnp.int32, (TREE, 128), 1)
-    columns = lax.broadcasted_iota(jnp.int32, (TREE, 256), 1)
-
-    def merge(query, key_at, value_at, seen):
-        tops_old = tops[owner]
-        dens_old = dens[owner]
-        tops_new, dens_new = tops_old, dens_old
-        for w in range(8):
-            first, begin = window(w)
-            here = [
-                (columns >= begin + HD * i) & (columns < begin + HD * (i + 1)) for i in range(2)
-            ]
-            picked = query(first)
-            stacked = jnp.concatenate(
-                [picked * here[i].astype(jnp.float32).astype(jnp.bfloat16) for i in range(2)],
-                axis=0,
-            )
-            scores = dot_t(stacked, key_at(first)) * factor
-            weights = []
-            scales = []
-            for i in range(2):
-                head = 2 * w + i
-                part = jnp.where(seen, scores[i * TREE : (i + 1) * TREE], LOWEST)
-                before = tops_old[:, head : head + 1]
-                top = jnp.maximum(before, jnp.ceil(jnp.max(part, axis=1, keepdims=True)))
-                weight = jnp.where(seen, jnp.exp2(part - top), 0.0)
-                scale = jnp.exp2(before - top)
-                total = dens_old[:, head : head + 1] * scale + jnp.sum(
-                    weight, axis=1, keepdims=True
-                )
-                tops_new = jnp.where(lanes == head, top, tops_new)
-                dens_new = jnp.where(lanes == head, total, dens_new)
-                weights.append(weight.astype(jnp.bfloat16))
-                scales.append(scale)
-            added = jnp.dot(
-                jnp.concatenate(weights, axis=0),
-                value_at(first),
-                preferred_element_type=jnp.float32,
-            )
-            window_scale = jnp.where(here[0], scales[0], jnp.where(here[1], scales[1], 1.0))
-            window_sum = jnp.where(
-                here[0], added[:TREE], jnp.where(here[1], added[TREE:], 0.0)
-            )
-            old = acc[owner, :, pl.ds(first, 256)]
-            acc[owner, :, pl.ds(first, 256)] = old * window_scale + window_sum
-        tops[owner] = tops_new
-        dens[owner] = dens_new
-
-    @pl.when(step < pages)
-    def _():
-        seen = lax.broadcasted_iota(jnp.int32, (TREE, PAGE), 1) + start < length
-        merge(
-            lambda first: query_ref[0, pl.ds(0, TREE), pl.ds(first, 256)],
-            lambda first: cache_ref[0, 0, :, pl.ds(first, 256)],
-            lambda first: cache_ref[0, 1, :, pl.ds(first, 256)],
-            seen,
-        )
-        row0 = length - start
-        touched = (row0 < PAGE) & (row0 + count > 0)
-
-        @pl.when(jnp.logical_not(touched))
+def append_kernel(tables, rows_ref, cache_ref, new_ref, kept, rows, load, save, more):
+    pages = kept.shape[0]
+
+    def page_of(ref, p, i):
+        return ref.at[0, i, pl.ds(p * PAGE, PAGE)]
+
+    def loads(p):
+        return [
+            pltpu.make_async_copy(page_of(cache_ref, p, i), kept.at[p, i], load.at[2 * p + i])
+            for i in range(2)
+        ]
+
+    def saves(p):
+        return [
+            pltpu.make_async_copy(kept.at[p, i], page_of(new_ref, p, i), save.at[2 * p + i])
+            for i in range(2)
+        ]
+
+    for p in range(pages):
+        for copy in loads(p):
+            copy.start()
+    for p in range(pages):
+        for copy in loads(p):
+            copy.wait()
+        row0 = tables[2, p] - tables[1, p]
+        count = tables[3, p]
+
+        @pl.when((row0 < PAGE) & (row0 + count > 0))
         def _():
-            new_ref[...] = cache_ref[...]
-
-        @pl.when(touched)
-        def _():
+            fetch = pltpu.make_async_copy(rows_ref.at[tables[0, p], pl.ds(TREE, 16)], rows, more)
+            fetch.start()
+            fetch.wait()
             ahead = lax.broadcasted_iota(jnp.int32, (PAGE, 8), 0) - row0
             nth = lax.broadcasted_iota(jnp.int32, (PAGE, 8), 1)
             hot = ((ahead == nth) & (nth < count)).astype(jnp.float32).astype(jnp.bfloat16)
-            rows = lax.broadcasted_iota(jnp.int32, (PAGE, WIDTH), 0) - row0
-            hit = (rows >= 0) & (rows < count)
+            index = lax.broadcasted_iota(jnp.int32, (PAGE, WIDTH), 0) - row0
+            hit = (index >= 0) & (index < count)
             for i in range(2):
-                fresh = jnp.dot(
-                    hot,
-                    query_ref[0, pl.ds(TREE + 8 * i, 8), :],
-                    preferred_element_type=jnp.float32,
+                taken = jnp.dot(
+                    hot, rows[pl.ds(8 * i, 8), :], preferred_element_type=jnp.float32
                 )
-                kept = cache_ref[0, i].astype(jnp.float32)
-                new_ref[0, i] = jnp.where(hit, fresh, kept).astype(jnp.bfloat16)
-
-    @pl.when(step == pages)
-    def _():
-        merge(
-            lambda first: query_ref[0, pl.ds(0, TREE), pl.ds(first, 256)],
-            lambda first: proj_ref[:, pl.ds(WIDTH + first, 256)],
-            lambda first: proj_ref[:, pl.ds(2 * WIDTH + first, 256)],
-            marks_ref[...] > 0.5,
-        )
-
-        @pl.loop(0, BLK)
-        def _(r):
-            num_ref[r] = acc[r].astype(jnp.bfloat16)
-            stats_ref[r] = jnp.where(lanes < 64, tops[r], pltpu.roll(dens[r], 64, 1))
-
-
-def attend(tables, gathered, cache, projected, marks):
+                old = kept[p, i].astype(jnp.float32)
+                kept[p, i] = jnp.where(hit, taken, old).astype(jnp.bfloat16)
+
+        for copy in saves(p):
+            copy.start()
+    for p in range(pages):
+        for copy in saves(p):
+            copy.wait()
+
+
+def append(tables, gathered, cache):
     pages = cache.shape[2] // PAGE
-    rows = gathered.shape[1]
-    page_block = pl.BlockSpec(
-        (1, 2, PAGE, WIDTH), lambda p, t: (0, 0, jnp.minimum(p, pages - 1), 0)
-    )
-    whole3 = lambda p, t: (0, 0, 0)
     return pl.pallas_call(
-        attend_kernel,
-        out_shape=[
-            jax.ShapeDtypeStruct((BLK, TREE, WIDTH), jnp.bfloat16),
-            jax.ShapeDtypeStruct((BLK, TREE, 128), jnp.float32),
-            jax.ShapeDtypeStruct(cache.shape, cache.dtype),
+        append_kernel,
+        out_shape=jax.ShapeDtypeStruct(cache.shape, cache.dtype),
+        in_specs=[pl.BlockSpec(memory_space=pltpu.SMEM), ANY, ANY],
+        out_specs=ANY,
+        scratch_shapes=[
+            pltpu.VMEM((pages, 2, PAGE, WIDTH), jnp.bfloat16),
+            pltpu.VMEM((16, WIDTH), jnp.bfloat16),
+            pltpu.SemaphoreType.DMA((2 * pages,)),
+            pltpu.SemaphoreType.DMA((2 * pages,)),
+            pltpu.SemaphoreType.DMA,
         ],
-        grid_spec=pltpu.PrefetchScalarGridSpec(
-            num_scalar_prefetch=1,
-            grid=(pages + 1,),
-            in_specs=[
-                pl.BlockSpec((1, rows, WIDTH), lambda p, t: (t[4, p], 0, 0)),
-                page_block,
-                pl.BlockSpec((TREE, 3 * WIDTH), lambda p, t: (0, 0)),
-                pl.BlockSpec((TREE, TREE), lambda p, t: (0, 0)),
-            ],
-            out_specs=[
-                pl.BlockSpec((BLK, TREE, WIDTH), whole3),
-                pl.BlockSpec((BLK, TREE, 128), whole3),
-                page_block,
-            ],
-            scratch_shapes=[
-                pltpu.VMEM((BLK, TREE, WIDTH), jnp.float32),
-                pltpu.VMEM((BLK, TREE, 128), jnp.float32),
-                pltpu.VMEM((BLK, TREE, 128), jnp.float32),
-            ],
-        ),
-        compiler_params=pltpu.CompilerParams(vmem_limit_bytes=48 * 1024 * 1024),
-        name="attend",
-    )(tables, gathered, cache, projected, marks)
+        compiler_params=pltpu.CompilerParams(vmem_limit_bytes=32 * 1024 * 1024),
+        name="append",
+    )(tables, gathered, cache)
+
+
+PAIR = 2 * TREE
+LINES = 8 * PAIR
+
+
+def attend_scratch(pages):
+    return [
+        pltpu.VMEM((2, pages + 1, PAGE, WIDTH), jnp.bfloat16),
+        pltpu.VMEM((BLK, TREE + 16, WIDTH), jnp.bfloat16),
+        pltpu.SemaphoreType.DMA((2 * pages + 1,)),
+        pltpu.VMEM((8, PAIR, 256), jnp.bfloat16),
+        pltpu.VMEM((8, PAIR, 256), jnp.bfloat16),
+        pltpu.VMEM((TREE, PAGE), jnp.float32),
+        pltpu.VMEM((LINES, 128), jnp.float32),
+        pltpu.VMEM((LINES, 128), jnp.bfloat16),
+        pltpu.VMEM((LINES, 128), jnp.float32),
+        pltpu.VMEM((LINES, 128), jnp.float32),
+        pltpu.VMEM((LINES, 128), jnp.float32),
+        pltpu.VMEM((8, PAIR, 256), jnp.float32),
+        pltpu.VMEM((pages + 2, TREE, WIDTH), jnp.bfloat16),
+        pltpu.VMEM((pages + 2, TREE, 128), jnp.float32),
+    ]
+
+
+def attend_steps(tables, query_ref, cache_ref, proj_ref, marks_ref, bufs, pause):
+    (kept, query, load, ones, masked, marks, scores, weights, tops, dens, scales, acc, sums, stats) = bufs
+    pages = cache_ref.shape[2] // PAGE
+    factor = math.log2(math.e) / math.sqrt(HD)
+    lanes = lax.broadcasted_iota(jnp.int32, (TREE, 128), 1)
+    columns = lax.broadcasted_iota(jnp.int32, (TREE, 256), 1)
+    copies = [
+        pltpu.make_async_copy(
+            cache_ref.at[0, i, pl.ds(p * PAGE, PAGE)], kept.at[i, p], load.at[i * pages + p]
+        )
+        for i in range(2)
+        for p in range(pages)
+    ]
+    copies.append(pltpu.make_async_copy(query_ref, query, load.at[2 * pages]))
+    for copy in copies:
+        copy.start()
+    yield
+
+    def inside(w, i):
+        begin = window(w)[1] + HD * i
+        return (columns >= begin) & (columns < begin + HD)
+
+    for w in range(8):
+        for i in range(2):
+            ones[w, pl.ds(TREE * i, TREE)] = (
+                inside(w, i).astype(jnp.float32).astype(jnp.bfloat16)
+            )
+    for i in range(2):
+        kept[i, pages, pl.ds(0, TREE)] = proj_ref[:, pl.ds((1 + i) * WIDTH, WIDTH)]
+        kept[i, pages, pl.ds(TREE, PAGE - TREE)] = jnp.zeros((PAGE - TREE, WIDTH), jnp.bfloat16)
+    marks[...] = jnp.zeros_like(marks)
+    marks[:, pl.ds(0, TREE)] = marks_ref[...]
+    tops[...] = jnp.full_like(tops, LOWEST)
+    dens[...] = jnp.zeros_like(dens)
+    acc[...] = jnp.zeros_like(acc)
+    sums[pages + 1] = jnp.zeros((TREE, WIDTH), jnp.bfloat16)
+    stats[pages + 1] = jnp.where(lanes < 64, LOWEST, 0.0)
+    for copy in copies:
+        copy.wait()
+
+    def step(j, carry):
+        start, length, owner = tables[1, j], tables[2, j], tables[4, j]
+        page, fresh, tree = tables[5, j], tables[6, j] > 0, tables[8, j] > 0
+        for w in range(8):
+            picked = query[owner, pl.ds(0, TREE), pl.ds(window(w)[0], 256)]
+            for i in range(2):
+                half = pl.ds(TREE * i, TREE)
+                masked[w, half] = picked * ones[w, half]
+        for w in range(8):
+            scores[pl.ds(PAIR * w, PAIR), :] = dot_t(
+                masked[w], kept[0, page, :, pl.ds(window(w)[0], 256)]
+            )
+        near = (lanes + start < length).astype(jnp.float32)
+        seen = jnp.where(tree, marks[...], near)
+        shown = jnp.concatenate([seen] * 4, axis=0) > 0.5
+        for part in range(4):
+            rows = pl.ds(2 * PAIR * part, 2 * PAIR)
+            part_scores = jnp.where(shown, scores[rows, :] * factor, LOWEST)
+            before = jnp.where(fresh, LOWEST, tops[rows, :])
+            top = jnp.maximum(before, jnp.ceil(jnp.max(part_scores, axis=1, keepdims=True)))
+            weight = jnp.where(shown, jnp.exp2(part_scores - top), 0.0)
+            scale = jnp.where(fresh, 0.0, jnp.exp2(before - top))
+            tops[rows, :] = top
+            scales[rows, :] = scale
+            dens[rows, :] = dens[rows, :] * scale + jnp.sum(weight, axis=1, keepdims=True)
+            weights[rows, :] = weight.astype(jnp.bfloat16)
+        carried = None
+        for w in range(8):
+            rows = pl.ds(PAIR * w, PAIR)
+            added = jnp.dot(
+                weights[rows, :],
+                kept[1, page, :, pl.ds(window(w)[0], 256)],
+                preferred_element_type=jnp.float32,
+            )
+            scale = scales[rows, :]
+            total = acc[w] * jnp.concatenate([scale, scale], axis=1) + added
+            acc[w] = total
+            picked = jnp.where(
+                inside(w, 0), total[:TREE], jnp.where(inside(w, 1), total[TREE:], 0.0)
+            )
+            head = picked[:, :128]
+            if w % 4:
+                head = head + carried
+            carried = picked[:, 128:]
+            sums[j, :, pl.ds(window(w)[0], 128)] = head.astype(jnp.bfloat16)
+            if w % 4 == 3:
+                sums[j, :, pl.ds(window(w)[0] + 128, 128)] = carried.astype(jnp.bfloat16)
+        row = jnp.full((TREE, 128), LOWEST, jnp.float32)
+        for head in range(H):
+            rows = pl.ds(TREE * head, TREE)
+            row = jnp.where(lanes == head, tops[rows, :], row)
+            row = jnp.where(lanes == 64 + head, dens[rows, :], row)
+        stats[j] = row
+        return carry
+
+    first = 0
+    for last in pause + (pages + 1,):
+        lax.fori_loop(first, last, step, 0)
+        first = last
+        if last <= pages:
+            yield
 
 
 PAIR_ORDER = (
@@ -393,6 +623,10 @@
     [f"{kind}{i}{s}" for kind, n in (("P", 16), ("T", 4), ("L", 4), ("R", 4)) for i in range(n) for s in "ns"]
     + [f"{kind}{s}" for kind in ("t0", "t1", "l", "r") for s in "ns"]
 )
+
+
+PAUSES = (3, 6, 9, 12, 14)
+ADVANCES = (0, 6, 10, 14, 18, 22)
 
 
 def split_stats(stats):
@@ -422,9 +656,9 @@
     return jnp.where(lanes < H, top, pltpu.roll(jnp.where(lanes < H, total, 0.0), 64, 1))
 
 
-def reduce_steps(spot, num, stats, out, spread, bufs, ssem, rsem):
+def reduce_steps(spot, tables, sums, stats, out, spread, bufs, ssem, rsem):
     pair_n, pair_s, work_n, work_s, thru_n, thru_s, left_n, left_s, right_n, right_s = bufs[:10]
-    fin_n, fin_s, two_n, two_s = bufs[10:]
+    fin_n, fin_s, two_n, two_s, out_n, out_s = bufs[10:]
     sent = {}
     send = sender(sent, ssem, rsem, REDUCE)
 
@@ -441,8 +675,10 @@
     other = (1 - spot.core) * 16
     mine = spot.core * 16
     for i, (a, b) in enumerate(PAIR_ORDER):
-        c = other + spot.chip(b, a)
-        put(f"P{i}", num.at[c], stats.at[c], pair_n.at[i], pair_s.at[i], spot.sibling)
+        found = tables[9, other + spot.chip(b, a)]
+        out_n[i] = sums[found]
+        out_s[i] = stats[found]
+        put(f"P{i}", out_n.at[i], out_s.at[i], pair_n.at[i], pair_s.at[i], spot.sibling)
     yield
 
     def store(dst_n, dst_s, parts):
@@ -453,9 +689,9 @@
     place = {pair: i for i, pair in enumerate(PAIR_ORDER)}
     for i, (a, b) in enumerate(PAIR_ORDER):
         took(f"P{i}")
-        c = mine + spot.chip(a, b)
+        found = tables[9, mine + spot.chip(a, b)]
         store(
-            work_n.at[i], work_s.at[i], [(num[c], stats[c]), (pair_n[i], pair_s[i])]
+            work_n.at[i], work_s.at[i], [(sums[found], stats[found]), (pair_n[i], pair_s[i])]
         )
         if a == 2:
             put(
@@ -531,30 +767,9 @@
         sent[event].wait_send()
 
 
-def reduce_and_gather(num, stats, spread, shards, collective_id):
+def attend_and_reduce(tables, gathered, cache, projected, marks, spread, shards, collective_id):
     count = len(shards)
-
-    def kernel(num_ref, stats_ref, spread_ref, *refs):
-        ins = refs[:count]
-        out = refs[count]
-        outs = refs[count + 1 : 2 * count + 1]
-        scratch = refs[2 * count + 1 :]
-        spot = Spot()
-        greet_plane(spot)
-        ssem, rsem = scratch[:2]
-        steps = [
-            reduce_steps(
-                spot,
-                num_ref,
-                stats_ref,
-                out,
-                lambda: spread_ref[...],
-                scratch[5:],
-                lambda e: ssem.at[e],
-                lambda e: rsem.at[e],
-            )
-        ]
-        run_all(steps + gather_all(spot, ins, outs, *scratch[2:5]))
+    pages = cache.shape[2] // PAGE
 
     def block(n):
         return [
@@ -562,31 +777,69 @@
             pltpu.VMEM((n, TREE, 128), jnp.float32),
         ]
 
+    parts = [
+        [pltpu.SemaphoreType.DMA((len(REDUCE),))] * 2,
+        gather_sems(count),
+        attend_scratch(pages),
+        block(16) + block(16) + block(4) + block(4) + block(4) + block(4) + block(3) + block(16),
+    ]
+
+    def kernel(tables_ref, query_ref, cache_ref, proj_ref, marks_ref, spread_ref, *refs):
+        ins = refs[:count]
+        out = refs[count]
+        outs = refs[count + 1 : 2 * count + 1]
+        left = list(refs[2 * count + 1 :])
+        scratch = []
+        for part in parts:
+            scratch.append(left[: len(part)])
+            left = left[len(part) :]
+        (ssem, rsem), gather_scratch, attend_bufs, reduce_bufs = scratch
+        spot = Spot()
+        work = attend_steps(
+            tables_ref, query_ref, cache_ref, proj_ref, marks_ref, attend_bufs, PAUSES
+        )
+        next(work)
+        greet_plane(spot)
+        gathers = gather_all(spot, ins, outs, *gather_scratch)
+
+        def advance():
+            for one in gathers:
+                next(one, None)
+
+        advance()
+        for _ in work:
+            advance()
+        for i, _ in enumerate(
+            reduce_steps(
+                spot,
+                tables_ref,
+                attend_bufs[-2],
+                attend_bufs[-1],
+                out,
+                lambda: spread_ref[...],
+                reduce_bufs,
+                lambda e: ssem.at[e],
+                lambda e: rsem.at[e],
+            )
+        ):
+            if i in ADVANCES:
+                advance()
+        run_all(gathers)
+
     return pl.pallas_call(
         kernel,
         out_shape=[jax.ShapeDtypeStruct((TREE, WIDTH), jnp.bfloat16)]
         + [jax.ShapeDtypeStruct((BLK,) + s.shape, s.dtype) for s in shards],
-        in_specs=[VMEM, VMEM, VMEM] + [ANY] * count,
+        in_specs=[pl.BlockSpec(memory_space=pltpu.SMEM), ANY, ANY, VMEM, VMEM, VMEM] + [VMEM] * count,
         out_specs=[VMEM] + [ANY] * count,
-        scratch_shapes=[
-            pltpu.SemaphoreType.DMA((len(REDUCE),)),
-            pltpu.SemaphoreType.DMA((len(REDUCE),)),
-        ]
-        + gather_sems(count)
-        + block(16)
-        + block(16)
-        + block(4)
-        + block(4)
-        + block(4)
-        + block(4)
-        + block(3),
+        scratch_shapes=[ref for part in parts for ref in part],
         compiler_params=pltpu.CompilerParams(
             collective_id=collective_id,
             has_side_effects=True,
-            vmem_limit_bytes=48 * 1024 * 1024,
+            vmem_limit_bytes=52 * 1024 * 1024,
         ),
-        name="reduce_and_gather",
-    )(num, stats, spread, *shards)
+        name="attend_and_reduce",
+    )(tables, gathered, cache, projected, marks, spread, *shards)
 
 
 def greet_column(at):
@@ -643,17 +896,6 @@
     )(block)
 
 
-def ancestors(parent_row):
-    nodes = jnp.arange(TREE, dtype=jnp.int32)
-    step = (parent_row[:, None] == nodes[None, :]).astype(jnp.float32)
-    current = jnp.eye(TREE, dtype=jnp.float32)
-    marks = current
-    for _ in range(DEPTH - 1):
-        current = jnp.dot(current, step)
-        marks = jnp.maximum(marks, current)
-    return marks
-
-
 def on_device(
     tree_input,
     cache,
@@ -668,81 +910,40 @@
     w_draft,
     w_patch,
 ):
-    myself = lax.axis_index("blk")
     width = WIDTH
     pool_pages = cache.shape[2] // PAGE
-    patch = lax.all_gather(w_patch.T, "req", axis=0, tiled=True)
-    normed = rms_rows(tree_input)
-    (qkv,) = all_gather([w_qkv.T], 1, "gather_qkv")
+    draft_mine = lax.dynamic_index_in_dim(
+        w_draft.transpose(0, 2, 1), lax.axis_index("req"), 0, keepdims=False
+    )
+    qkv, patch, normed, tables, pages, marks, picker = prepare(
+        w_qkv.T, w_patch.T, tree_input, page_table, lengths, accept_leaf, parents, pool_pages
+    )
     projected = dot_t(normed, qkv.reshape(3 * width, width)).astype(jnp.bfloat16)
-
-    page_row = page_table[0]
-    length_row = lengths[0]
-    leaf_row = accept_leaf[0]
-    requests = length_row.shape[0]
-    total_pages = page_row.shape[0]
-    npages = (length_row + DEPTH + PAGE - 1) // PAGE
-    before = jnp.arange(requests)[:, None] >= jnp.arange(requests)[None, :]
-    page_ends = jnp.sum(jnp.where(before, npages[None, :], 0), axis=1)
-    offsets = page_ends - npages
-    local_ids = myself * pool_pages + jnp.arange(pool_pages, dtype=jnp.int32)
-    located = page_row[None, :] == local_ids[:, None]
-    where_at = jnp.sum(
-        jnp.where(located, jnp.arange(total_pages, dtype=jnp.int32)[None, :], 0), axis=1
-    )
-    owner = jnp.sum((page_ends[None, :] <= where_at[:, None]).astype(jnp.int32), axis=1)
-    owner_hot = owner[:, None] == jnp.arange(requests, dtype=jnp.int32)[None, :]
-    safe_owner = jnp.minimum(owner, requests - 1)
-    level_marks = jnp.asarray(LEVEL_START[1:-1], jnp.int32)
-    accepted = 1 + jnp.sum((leaf_row[:, None] >= level_marks[None, :]).astype(jnp.int32), axis=1)
-
-    def of_owner(row):
-        return jnp.sum(jnp.where(owner_hot, row[None, :], 0), axis=1)
-
-    def with_tree(row, last):
-        return jnp.concatenate([row, jnp.reshape(jnp.asarray(last, jnp.int32), (1,))])
-
-    owners = with_tree(safe_owner, myself)
-    tables = jnp.stack(
-        [
-            owners % 2 * 16 + owners // 2,
-            with_tree((where_at - of_owner(offsets)) * PAGE, 0),
-            with_tree(of_owner(length_row), 0),
-            with_tree(of_owner(accepted), 0),
-            owners,
-        ]
-    )
-    marks = ancestors(parents[0])
-    my_leaf = jnp.sum(jnp.where(jnp.arange(requests) == myself, leaf_row, 0))
-    nodes = jnp.arange(TREE, dtype=jnp.int32)
-    chosen = jnp.sum(jnp.where(nodes[:, None] == my_leaf, marks, 0.0), axis=0)
-    ranks = jnp.sum(jnp.where(nodes[:, None] <= nodes[None, :], chosen[:, None], 0.0), axis=0) - 1
-    picker = jnp.where(
-        (chosen[None, :] > 0.5) & (ranks[None, :] == jnp.arange(8, dtype=jnp.float32)[:, None]),
-        1.0,
-        0.0,
-    ).astype(jnp.bfloat16)
     send_rows = jnp.dot(
-        picker, projected[:, width:], preferred_element_type=jnp.float32
+        picker[:8], projected[:, width:], preferred_element_type=jnp.float32
     ).astype(jnp.bfloat16)
     (gathered,) = all_gather(
         [jnp.concatenate([projected[:, :width], send_rows[:, :width], send_rows[:, width:]])],
         2,
         "gather_query",
     )
-    num, stats, cache_new = attend(tables, gathered, cache, projected, marks)
+    cache_new = append(pages, gathered, cache)
     spread = (
         jnp.arange(128, dtype=jnp.int32)[:, None]
         == jnp.arange(width, dtype=jnp.int32)[None, :] // HD
     ).astype(jnp.bfloat16)
-    draft_mine = lax.dynamic_index_in_dim(
-        w_draft.transpose(0, 2, 1), lax.axis_index("req"), 0, keepdims=False
-    )
-    attended, full_out, full_up, full_down, full_draft = reduce_and_gather(
-        num, stats, spread, [w_out.T, w_up.T, w_down, draft_mine], 3
-    )
-    full_out, full_up, full_down, full_draft = (
-        w.reshape(width, width) for w in (full_out, full_up, full_down, full_draft)
+    attended, full_out, full_up, full_down, full_draft = attend_and_reduce(
+        tables,
+        gathered,
+        cache,
+        projected,
+        marks,
+        spread,
+        [w_out.T, w_up.T, w_down, draft_mine],
+        3,
+    )
+    full_out, full_up, full_down, full_draft, patch = (
+        w.reshape(width, width) for w in (full_out, full_up, full_down, full_draft, patch)
     )
     proj = dot_t(attended, full_out).astype(jnp.bfloat16)
     mid = (tree_input.astype(jnp.float32) + proj.astype(jnp.float32)).astype(jnp.bfloat16)

time: 259 us -> 189 us (0.73)
  Pallas kernels: 209 us -> 154 us
  between operations: 14.3 us -> 0.93 us
  local copies, waits for them, and re-layouts: 3.93 us -> 7.35 us
  other arithmetic: 6.41 us -> 3.16 us
  matrix products: 24.1 us -> 20.9 us
    pallas_call x2 -> x1, Pallas kernels: 58.1 us -> 25.3 us  [all_gather(): pl.pallas_call(kernel, out_shape=[jax.ShapeDtypeStruct((BLK,) + s.shape,...]
    pallas_call x2 -> x3, Pallas kernels: 129 us -> 111 us  [the longest x1 64.2 us: attend_and_reduce(): pl.pallas_call(kernel, out_shape=[jax.ShapeDtypeStruct((TREE, WIDTH), jnp...]
    pallas_call x2, Pallas kernels: 22.1 us -> 18.4 us  [over_column(): pl.pallas_call(column_kernel(exchange), out_shape=jax.ShapeDtypeStruct(sh...]
    unnamed x21 -> x27, local copies, waits for them, and re-layouts: 3.87 us -> 7.32 us
    dot_general x5 -> x1, matrix products: 3.56 us -> 0.14 us  [on_device(): jnp.dot(picker[:8], projected[:, width:], preferred_element_type=jnp.floa...]
  transfers between devices with their start and end apart: 1 -> 0, of which waited for: 0 -> 0; matrix products, arithmetic and copies ran while one was open for 10% -> 0% of each run, Pallas kernels for 77% -> 0%
where the time goes in v3:
time: 189 us; the launch traced here: 187 us
  Pallas kernels  154 us (81%)
  matrix products  20.9 us (11%)
  local copies, waits for them, and re-layouts  7.35 us (4%)
  other arithmetic  3.16 us (2%)
    pallas_call x1, Pallas kernels, attend_and_reduce(): pl.pallas_call(kernel, out_shape=[jax.ShapeDtypeStruct((TREE, WIDTH), jnp...  64.2 us
    pallas_call x1, Pallas kernels, prepare(): pl.pallas_call(kernel, out_shape=[jax.ShapeDtypeStruct((BLK,) + shard.sha...  38 us
    pallas_call x1, Pallas kernels, all_gather(): pl.pallas_call(kernel, out_shape=[jax.ShapeDtypeStruct((BLK,) + s.shape,...  25.3 us
    pallas_call x2, Pallas kernels, over_column(): pl.pallas_call(column_kernel(exchange), out_shape=jax.ShapeDtypeStruct(sh...  18.4 us
    dot_general x4, matrix products, dot_t(): lax.dot_general(left, right, (((1,), (1,)), ((), ())), preferred_element_...  15.4 us
    pallas_call x1, Pallas kernels, append(): pl.pallas_call(append_kernel, out_shape=jax.ShapeDtypeStruct(cache.shape,...  8.32 us
    unnamed x27, local copies, waits for them, and re-layouts  7.32 us
    dot_general x1, matrix products, on_device(): feedforward = jnp.dot(hidden, full_down, preferred_element_type=jnp.float32)  5.34 us

profile of v3, /device:TPU:2, one launch (start us, length us, event | category | flops | bytes accessed | tf_op | source)
XLA Modules:
  0.0 186.7 jit_solution(10784725847922823227)
XLA Ops:
  0.6 0.0 copy-start
  0.6 38.0 %prepare.1 = (bf16[32,120,1280]{2,1,0:T(8,128)(2,1)}, bf16[4,320,1280]{2,1,0:T(8,128)(2,1)}, bf16[48,1280]{1,0:T(8,128)(2,1)}, s32[10,128]{1,0:T(8,128)}, s32[4,...) custom-call(bf16[120,1280]{1,0:T(8,128)(2,1)} %bitcast.40, bf16[320,1280]{1,0:T(8,128)(2,1)} %bitcast.38, ...), custom_call_target="tpu_custom_call" | custom-call | tf_op jit(solution)/shard_map/prepare/pallas_call | solution.py:392
  38.7 6.8 %convolution_convert_fusion.proj_ref = bf16[48,3840]{1,0:T(8,128)(2,1)S(1)} fusion(bf16[48,1280]{1,0:T(8,128)(2,1)} %get-tuple-element.16, bf16[3840,1280]{1,0:T(8,128)(2,1)} %bitcast.32), kind=kOutput, calls=%fused_computation | convolution fusion | flops 472043520 | bytes 10321920 | tf_op jit(solution)/shard_map/dot_general | solution.py:33
  45.5 0.0 copy-done.12
  45.6 0.1 convolution_convert_fusion.1
  45.7 0.0 copy-start.3
  45.7 0.0 copy-start.4
  45.7 0.0 copy-start.5
  45.8 0.7 pad_maximum_fusion.refs_0_
  46.5 25.3 %gather_query.1.query_ref.rows_ref = bf16[32,64,1280]{2,1,0:T(8,128)(2,1)} custom-call(bf16[64,1280]{1,0:T(8,128)(2,1)} %pad_maximum_fusion.refs_0_), custom_call_target="tpu_custom_call" | custom-call | tf_op jit(solution)/shard_map/gather_query/pallas_call | solution.py:273
  71.9 0.1 fusion.6.spread_ref
  72.0 64.2 %attend_and_reduce.1 = (bf16[48,1280]{1,0:T(8,128)(2,1)S(1)}, bf16[32,40,1280]{2,1,0:T(8,128)(2,1)}, bf16[32,40,1280]{2,1,0:T(8,128)(2,1)}, bf16[32,40,1280]{2,1,0:T(8,128)(2,1)}, bf16[32,40,1280]{2,1,0:T(8,128)(2,1)}) custom-call(s32[10,128]{1,0:T(8,128)S(1)} %copy-done.7, bf16[32,64,1280]{2,1,0:T(8,128)(2,1)} %gather_query.1.query_ref.rows_ref, ...), custom_call_target="tpu_custom_call" | custom-call | tf_op jit(solution)/shard_map/attend_and_reduce/pallas_call | solution.py:829
  136.2 3.1 %multiply_reduce_fusion.1 = (f32[48]{0:T(128)S(1)}, f32[48,1280]{1,0:T(8,128)S(1)}) fusion(bf16[48,1280]{1,0:T(8,128)(2,1)S(1)} %get-tuple-element.20, bf16[1280,1280]{1,0:T(8,128)(2,1)} %bitcast.36, bf16[48,1280]{1,0:T(8,128)(2,1)S(1)} %copy-done.11), kind=kOutput, calls=%fused_computation.28 | convolution fusion | flops 157777872 | bytes 3768512 | tf_op jit(solution)/shard_map/dot_general | solution.py:33
  139.4 5.3 %fusion.block = bf16[48,1280]{1,0:T(8,128)(2,1)} fusion(f32[48,1280]{1,0:T(8,128)S(1)} %get-tuple-element.30, bf16[1280,1280]{1,0:T(8,128)(2,1)} %bitcast.34, bf16[1280,1280]{1,0:T(8,128)(2,1)} %bitcast.33, f32[48]{0:T(128)S(1)} %add_rsqrt_fusion.1), kind=kOutput, calls=%fused_computation.4 | convolution fusion | flops 315371520 | bytes 6922432 | tf_op jit(solution)/shard_map/dot_general | solution.py:951
  144.7 9.1 %gather_rows.1 = bf16[4,48,1280]{2,1,0:T(8,128)(2,1)} custom-call(bf16[48,1280]{1,0:T(8,128)(2,1)} %fusion.block), custom_call_target="tpu_custom_call" | custom-call | tf_op jit(solution)/shard_map/gather_rows/pallas_call | solution.py:882
  153.9 1.2 multiply_reduce_fusion
  155.1 1.2 multiply_convert_fusion.1
  156.3 3.4 %fusion.5 = bf16[192,1280]{1,0:T(8,128)(2,1)S(1)} fusion(bf16[4,48,1280]{2,1,0:T(8,128)(2,1)} %gather_rows.1, bf16[192,1280]{1,0:T(8,128)(2,1)S(1)} %bitcast.39, bf16[1280,1280]{1,0:T(8,128)(2,1)} %bitcast.41), kind=kOutput, calls=%fused_computation.11 | convolution fusion | flops 631357440 | bytes 4751360 | tf_op jit(solution)/shard_map/dot_general | solution.py:33
  159.8 2.0 %convolution_convert_fusion.2 = bf16[192,1280]{1,0:T(8,128)(2,1)} fusion(bf16[192,1280]{1,0:T(8,128)(2,1)S(1)} %fusion.5, bf16[1280,1280]{1,0:T(8,128)(2,1)S(1)} %bitcast.35), kind=kOutput, calls=%fused_computation.2 | convolution fusion | flops 629391360 | bytes 4259840 | tf_op jit(solution)/shard_map/dot_general | solution.py:33
  161.8 9.3 %return_rows.1 = bf16[4,48,1280]{2,1,0:T(8,128)(2,1)} custom-call(bf16[4,48,1280]{2,1,0:T(8,128)(2,1)} %bitcast.37), custom_call_target="tpu_custom_call" | custom-call | tf_op jit(solution)/shard_map/return_rows/pallas_call | solution.py:882
  171.1 2.5 %copy-done.1 = bf16[32,64,1280]{2,1,0:T(8,128)(2,1)S(1)} copy-done((bf16[32,64,1280]{2,1,0:T(8,128)(2,1)S(1)}, bf16[32,64,1280]{2,1,0:T(8,128)(2,1)}, u32[]{:S(2)}) %copy-start.1) | copy-done | bytes 5242904
  173.6 4.0 %copy-done.2 = bf16[1,2,2048,1280]{3,2,1,0:T(8,128)(2,1)S(1)} copy-done((bf16[1,2,2048,1280]{3,2,1,0:T(8,128)(2,1)S(1)}, bf16[1,2,2048,1280]{3,2,1,0:T(8,128)(2,1)}, u32[]{:S(2)}) %copy-start.2) | copy-done | bytes 10485784
  177.6 8.3 %append.1 = bf16[1,2,2048,1280]{3,2,1,0:T(8,128)(2,1)} custom-call(s32[4,128]{1,0:T(4,128)S(1)} %copy-done.8, bf16[32,64,1280]{2,1,0:T(8,128)(2,1)S(1)} %copy-done.1, bf16[1,2,2048,1280]{3,2,1,0:T(8,128)(2,1)S(1)} %copy-done.2), custom_call_target="tpu_custom_call" | custom-call | tf_op jit(solution)/shard_map/append/pallas_call | solution.py:473
  185.9 0.8 copy.16
  (25 shorter events, 0.1 us)
Async XLA Ops:
  0.6 71.2 %copy-start = (bf16[4,1280,40]{1,2,0:T(8,128)(2,1)S(1)}, bf16[4,1280,40]{1,2,0:T(8,128)(2,1)}, u32[]{:S(2)}) copy-start(bf16[4,1280,40]{1,2,0:T(8,128)(2,1)} %param.22) | copy-start | bytes 1228804
  38.7 6.9 %copy-start.12 = (bf16[16,48]{1,0:T(8,128)(2,1)S(1)}, bf16[16,48]{1,0:T(8,128)(2,1)}, u32[]{:S(2)}) copy-start(bf16[16,48]{1,0:T(8,128)(2,1)} %get-tuple-element.18) | copy-start | bytes 4612
  45.7 26.2 %copy-start.3 = (bf16[1280,40]{0,1:T(8,128)(2,1)S(1)}, bf16[1280,40]{0,1:T(8,128)(2,1)}, u32[]{:S(2)}) copy-start(bf16[1280,40]{0,1:T(8,128)(2,1)} %param.19) | copy-start | bytes 307204
  45.7 26.2 %copy-start.4 = (bf16[1280,40]{0,1:T(8,128)(2,1)S(1)}, bf16[1280,40]{0,1:T(8,128)(2,1)}, u32[]{:S(2)}) copy-start(bf16[1280,40]{0,1:T(8,128)(2,1)} %param.20) | copy-start | bytes 307204
  45.7 26.2 %copy-start.5 = (bf16[40,1280]{1,0:T(8,128)(2,1)S(1)}, bf16[40,1280]{1,0:T(8,128)(2,1)}, u32[]{:S(2)}) copy-start(bf16[40,1280]{1,0:T(8,128)(2,1)} %refs_2_.1) | copy-start | bytes 307204
  45.8 26.2 %copy-start.6 = (f32[48,48]{1,0:T(8,128)S(1)}, f32[48,48]{1,0:T(8,128)}, u32[]{:S(2)}) copy-start(f32[48,48]{1,0:T(8,128)} %get-tuple-element.19.marks_ref) | copy-start | bytes 27652
  45.8 26.2 %copy-start.7 = (s32[10,128]{1,0:T(8,128)S(1)}, s32[10,128]{1,0:T(8,128)}, u32[]{:S(2)}) copy-start(s32[10,128]{1,0:T(8,128)} %get-tuple-element.15.tables_ref) | copy-start | bytes 15364
  72.0 64.3 %copy-start.11 = (bf16[48,1280]{1,0:T(8,128)(2,1)S(1)}, bf16[48,1280]{1,0:T(8,128)(2,1)}, u32[]{:S(2)}) copy-start(bf16[48,1280]{1,0:T(8,128)(2,1)} %x_ref.1) | copy-start | bytes 368644
  156.3 3.5 %copy-start.9 = (bf16[4,320,1280]{2,1,0:T(8,128)(2,1)S(1)}, bf16[4,320,1280]{2,1,0:T(8,128)(2,1)}, u32[]{:S(2)}) copy-start(bf16[4,320,1280]{2,1,0:T(8,128)(2,1)} %get-tuple-element.25) | copy-start | bytes 9830404
  159.8 11.3 %copy-start.8 = (s32[4,128]{1,0:T(4,128)S(1)}, s32[4,128]{1,0:T(4,128)}, u32[]{:S(2)}) copy-start(s32[4,128]{1,0:T(4,128)} %get-tuple-element.26.tables) | copy-start | bytes 6148
  171.1 2.5 %copy-start.1 = (bf16[32,64,1280]{2,1,0:T(8,128)(2,1)S(1)}, bf16[32,64,1280]{2,1,0:T(8,128)(2,1)}, u32[]{:S(2)}) copy-start(bf16[32,64,1280]{2,1,0:T(8,128)(2,1)} %gather_query.1.query_ref.rows_ref) | copy-start | bytes 15728644
  173.6 4.0 %copy-start.2 = (bf16[1,2,2048,1280]{3,2,1,0:T(8,128)(2,1)S(1)}, bf16[1,2,2048,1280]{3,2,1,0:T(8,128)(2,1)}, u32[]{:S(2)}) copy-start(bf16[1,2,2048,1280]{3,2,1,0:T(8,128)(2,1)} %cache_ref.3) | copy-start | bytes 31457284
  177.6 8.3 %copy-start.10 = (bf16[4,48,1280]{2,1,0:T(8,128)(2,1)S(1)}, bf16[4,48,1280]{2,1,0:T(8,128)(2,1)}, u32[]{:S(2)}) copy-start(bf16[4,48,1280]{2,1,0:T(8,128)(2,1)} %return_rows.1) | copy-start | bytes 1474564

commit v4 on v3

--- a/solution.py
+++ b/solution.py
@@ -184,20 +184,27 @@
     return cut
 
 
-def gather_all(spot, ins, outs, ssem, rsem, lsem):
+def gather_all(spot, ins, outs, ssem, rsem, lsem, cuts=None):
     count = len(GATHER)
-    return [
-        gather_steps(
-            spot,
-            ins[i],
-            lambda slot, i=i: outs[i].at[slot],
-            lambda e, i=i: ssem.at[i * count + e],
-            lambda e, i=i: rsem.at[i * count + e],
-            lsem.at[i],
-            row_halves(ins[i].shape[0]),
-        )
-        for i in range(len(ins))
-    ]
+    steps = []
+    for i, (shard, out) in enumerate(zip(ins, outs)):
+        first = 0
+        for rows in (cuts or {}).get(i, (shard.shape[0],)):
+            piece = pl.ds(first, rows)
+            at = len(steps) * count
+            steps.append(
+                gather_steps(
+                    spot,
+                    shard.at[piece],
+                    lambda slot, out=out, piece=piece: out.at[slot, piece],
+                    lambda e, at=at: ssem.at[at + e],
+                    lambda e, at=at: rsem.at[at + e],
+                    lsem.at[len(steps)],
+                    row_halves(rows),
+                )
+            )
+            first += rows
+    return steps
 
 
 def gather_sems(arrays):
@@ -259,26 +266,31 @@
 
 
 ANY = pl.BlockSpec(memory_space=pl.ANY)
+HBM = pl.BlockSpec(memory_space=pltpu.HBM)
 VMEM = pl.BlockSpec(memory_space=pltpu.VMEM)
 
 
-def all_gather(shards, collective_id, name):
+def all_gather(shards, cuts, collective_id, name):
     count = len(shards)
 
     def kernel(*refs):
         spot = Spot()
         greet_plane(spot)
-        run_all(gather_all(spot, refs[:count], refs[count : 2 * count], *refs[2 * count :]))
+        run_all(gather_all(spot, refs[:count], refs[count : 2 * count], *refs[2 * count :], cuts))
 
     return pl.pallas_call(
         kernel,
         out_shape=[jax.ShapeDtypeStruct((BLK,) + s.shape, s.dtype) for s in shards],
         in_specs=[VMEM] * count,
         out_specs=[ANY] * count,
-        scratch_shapes=gather_sems(count),
+        scratch_shapes=gather_sems(count + sum(len(rows) - 1 for rows in cuts.values())),
         compiler_params=pltpu.CompilerParams(collective_id=collective_id, has_side_effects=True),
         name=name,
     )(*shards)
+
+
+QKV_CUTS = (48, 48, 24)
+QUERY_CUTS = (32, 32)
 
 
 def iota(shape, dim):
@@ -370,10 +382,11 @@
     ):
         spot = Spot()
         greet_plane(spot, True)
-        steps = gather_all(spot, [shard_ref], [full_ref], *scratch[:3])
+        steps = gather_all(spot, [shard_ref], [full_ref], *scratch[:3], {0: QKV_CUTS})
         steps.append(column_steps(spot, patch_ref, full_patch_ref, *scratch[3:]))
-        for one in steps:
-            next(one)
+        for _ in range(3):
+            for one in steps:
+                next(one)
         normed_ref[...] = rms_rows(x_ref[...])
         leaf = jnp.sum(
             jnp.where(iota(leaf_ref.shape, 1) == spot.me, leaf_ref[...], 0), axis=1, keepdims=True
@@ -402,7 +415,7 @@
         ],
         in_specs=[VMEM] * 7,
         out_specs=[ANY, ANY] + [VMEM] * 5,
-        scratch_shapes=gather_sems(1)
+        scratch_shapes=gather_sems(len(QKV_CUTS))
         + [
             pltpu.SemaphoreType.DMA((len(COLUMN),)),
             pltpu.SemaphoreType.DMA((len(COLUMN),)),
@@ -417,8 +430,15 @@
     return 128 * (5 * (w // 4) + w % 4), 32 * (w % 4)
 
 
-def append_kernel(tables, rows_ref, cache_ref, new_ref, kept, rows, load, save, more):
+def draft_kernel(
+    tables, fresh_ref, cache_ref, layer_ref, draft_ref, patch_ref, head_ref, new_ref,
+    kept, rows, draft, patch, load, save, more, wide,
+):
     pages = kept.shape[0]
+    weights = [
+        pltpu.make_async_copy(draft_ref, draft, wide.at[0]),
+        pltpu.make_async_copy(patch_ref, patch, wide.at[1]),
+    ]
 
     def page_of(ref, p, i):
         return ref.at[0, i, pl.ds(p * PAGE, PAGE)]
@@ -438,6 +458,8 @@
     for p in range(pages):
         for copy in loads(p):
             copy.start()
+    for copy in weights:
+        copy.start()
     for p in range(pages):
         for copy in loads(p):
             copy.wait()
@@ -446,7 +468,7 @@
 
         @pl.when((row0 < PAGE) & (row0 + count > 0))
         def _():
-            fetch = pltpu.make_async_copy(rows_ref.at[tables[0, p], pl.ds(TREE, 16)], rows, more)
+            fetch = pltpu.make_async_copy(fresh_ref.at[tables[0, p], pl.ds(TREE, 16)], rows, more)
             fetch.start()
             fetch.wait()
             ahead = lax.broadcasted_iota(jnp.int32, (PAGE, 8), 0) - row0
@@ -463,28 +485,41 @@
 
         for copy in saves(p):
             copy.start()
+    weights[0].wait()
+    layer = layer_ref[...]
+    grown = dot_t(rms_rows(layer), draft[...])
+    branch = (grown / (1.0 + jnp.exp(-grown))).astype(jnp.bfloat16)
+    drafted = (layer.astype(jnp.float32) + branch.astype(jnp.float32)).astype(jnp.bfloat16)
+    weights[1].wait()
+    head_ref[...] = dot_t(drafted, patch[...]).astype(jnp.bfloat16)
     for p in range(pages):
         for copy in saves(p):
             copy.wait()
 
 
-def append(tables, gathered, cache):
+def draft_and_append(tables, gathered, cache, layer, draft, patch):
     pages = cache.shape[2] // PAGE
     return pl.pallas_call(
-        append_kernel,
-        out_shape=jax.ShapeDtypeStruct(cache.shape, cache.dtype),
-        in_specs=[pl.BlockSpec(memory_space=pltpu.SMEM), ANY, ANY],
-        out_specs=ANY,
+        draft_kernel,
+        out_shape=[
+            jax.ShapeDtypeStruct(layer.shape, layer.dtype),
+            jax.ShapeDtypeStruct(cache.shape, cache.dtype),
+        ],
+        in_specs=[pl.BlockSpec(memory_space=pltpu.SMEM), HBM, HBM, VMEM, HBM, HBM],
+        out_specs=[VMEM, HBM],
         scratch_shapes=[
             pltpu.VMEM((pages, 2, PAGE, WIDTH), jnp.bfloat16),
             pltpu.VMEM((16, WIDTH), jnp.bfloat16),
+            pltpu.VMEM(draft.shape, draft.dtype),
+            pltpu.VMEM(patch.shape, patch.dtype),
             pltpu.SemaphoreType.DMA((2 * pages,)),
             pltpu.SemaphoreType.DMA((2 * pages,)),
             pltpu.SemaphoreType.DMA,
+            pltpu.SemaphoreType.DMA((2,)),
         ],
-        compiler_params=pltpu.CompilerParams(vmem_limit_bytes=32 * 1024 * 1024),
-        name="append",
-    )(tables, gathered, cache)
+        compiler_params=pltpu.CompilerParams(vmem_limit_bytes=60 * 1024 * 1024),
+        name="draft_and_append",
+    )(tables, gathered, cache, layer, draft, patch)
 
 
 PAIR = 2 * TREE
@@ -842,37 +877,48 @@
     )(tables, gathered, cache, projected, marks, spread, *shards)
 
 
-def greet_column(at):
-    barrier = pltpu.get_barrier_semaphore()
-    for d in (1, 2, 3):
-        pl.semaphore_signal(
-            barrier, inc=1, device_id={"req": (at + d) % 4}, device_id_type=MESH
-        )
-    pl.semaphore_wait(barrier, 3)
+RETURN = numbered(["TA", "TB", "L", "R", "OA", "OB"])
 
 
 def column_kernel(exchange):
-    def kernel(block, out, ssem, rsem, lsem):
+    def kernel(block, out, thru, ssem, rsem, lsem):
         at = lax.axis_index("req")
-        greet_column(at)
-        copies = []
-        for d in (2, 1, 3):
-            to = (at + d) % 4
+        above, far, below = (at + 1) % 4, (at + 2) % 4, (at + 3) % 4
+        barrier = pltpu.get_barrier_semaphore()
+        for who in (above, below):
+            pl.semaphore_signal(barrier, inc=1, device_id={"req": who}, device_id_type=MESH)
+        pl.semaphore_wait(barrier, 2)
+        sent = {}
+        upper, lower = pl.ds(0, 32), pl.ds(32, TREE - 32)
+
+        def put(event, src, dst, who):
             copy = pltpu.make_async_remote_copy(
-                src_ref=block.at[to] if exchange else block,
-                dst_ref=out.at[at],
-                send_sem=ssem.at[d - 1],
-                recv_sem=rsem.at[d - 1],
-                device_id={"req": to},
+                src_ref=src,
+                dst_ref=dst,
+                send_sem=ssem.at[RETURN[event]],
+                recv_sem=rsem.at[RETURN[event]],
+                device_id={"req": who},
                 device_id_type=MESH,
             )
             copy.start()
-            copies.append(copy)
+            sent[event] = copy
+
+        if exchange:
+            put("TA", block.at[far, upper], thru.at[upper], above)
+            put("TB", block.at[far, lower], thru.at[lower], below)
+        put("L", block.at[above] if exchange else block, out.at[at], above)
+        put("R", block.at[below] if exchange else block, out.at[at], below)
         local = pltpu.make_async_copy(block.at[at] if exchange else block, out.at[at], lsem)
         local.start()
+        sent["TA" if exchange else "L"].wait_recv()
+        put("OA", thru.at[upper] if exchange else out.at[below, upper], out.at[below, upper], above)
+        sent["TB" if exchange else "R"].wait_recv()
+        put("OB", thru.at[lower] if exchange else out.at[above, lower], out.at[above, lower], below)
         local.wait()
-        for copy in copies:
-            copy.wait()
+        for event in ("L", "R", "OA", "OB") if exchange else ("OA", "OB"):
+            sent[event].wait_recv()
+        for copy in sent.values():
+            copy.wait_send()
 
     return kernel
 
@@ -885,8 +931,9 @@
         in_specs=[VMEM],
         out_specs=VMEM,
         scratch_shapes=[
-            pltpu.SemaphoreType.DMA((3,)),
-            pltpu.SemaphoreType.DMA((3,)),
+            pltpu.VMEM(block.shape[-2:], block.dtype),
+            pltpu.SemaphoreType.DMA((len(RETURN),)),
+            pltpu.SemaphoreType.DMA((len(RETURN),)),
             pltpu.SemaphoreType.DMA,
         ],
         compiler_params=pltpu.CompilerParams(
@@ -922,28 +969,29 @@
     send_rows = jnp.dot(
         picker[:8], projected[:, width:], preferred_element_type=jnp.float32
     ).astype(jnp.bfloat16)
-    (gathered,) = all_gather(
-        [jnp.concatenate([projected[:, :width], send_rows[:, :width], send_rows[:, width:]])],
+    pack = jnp.concatenate([projected[:, :width], send_rows[:, :width], send_rows[:, width:]])
+    gathered, *full_early = all_gather(
+        [pack, w_out.T, ],
+        {0: QUERY_CUTS},
         2,
         "gather_query",
     )
-    cache_new = append(pages, gathered, cache)
     spread = (
         jnp.arange(128, dtype=jnp.int32)[:, None]
         == jnp.arange(width, dtype=jnp.int32)[None, :] // HD
     ).astype(jnp.bfloat16)
-    attended, full_out, full_up, full_down, full_draft = attend_and_reduce(
+    attended, *full_late = attend_and_reduce(
         tables,
         gathered,
         cache,
         projected,
         marks,
         spread,
-        [w_out.T, w_up.T, w_down, draft_mine],
+        [w_up.T, w_down, draft_mine],
         3,
     )
     full_out, full_up, full_down, full_draft, patch = (
-        w.reshape(width, width) for w in (full_out, full_up, full_down, full_draft, patch)
+        w.reshape(width, width) for w in (*full_early, *full_late, patch)
     )
     proj = dot_t(attended, full_out).astype(jnp.bfloat16)
     mid = (tree_input.astype(jnp.float32) + proj.astype(jnp.float32)).astype(jnp.bfloat16)
@@ -951,9 +999,7 @@
     feedforward = jnp.dot(hidden, full_down, preferred_element_type=jnp.float32)
     layer_out = (mid.astype(jnp.float32) + feedforward).astype(jnp.bfloat16)
     rows = over_column(layer_out, False, 4, "gather_rows").reshape(4 * TREE, width)
-    branch = jax.nn.silu(dot_t(rms_rows(rows), full_draft)).astype(jnp.bfloat16)
-    drafted = (rows.astype(jnp.float32) + branch.astype(jnp.float32)).astype(jnp.bfloat16)
-    head = dot_t(drafted, patch).astype(jnp.bfloat16)
+    head, cache_new = draft_and_append(pages, gathered, cache, rows, full_draft, patch)
     drafts = over_column(head.reshape(4, TREE, width), True, 5, "return_rows")
     return (layer_out, drafts, cache_new)
 

time: 189 us -> 177 us (0.937)
  matrix products: 20.9 us -> 13.6 us
  local copies, waits for them, and re-layouts: 7.35 us -> 2.9 us
  Pallas kernels: 154 us -> 158 us
  other arithmetic: 3.16 us -> 0.75 us
    pallas_call x1, Pallas kernels: 64.2 us -> 51.2 us  [attend_and_reduce(): pl.pallas_call(kernel, out_shape=[jax.ShapeDtypeStruct((TREE, WIDTH), jnp...]
    dot_general x4 -> x2, matrix products: 15.4 us -> 8.1 us  [dot_t(): lax.dot_general(left, right, (((1,), (1,)), ((), ())), preferred_element_...]
    pallas_call x1, Pallas kernels: 25.3 us -> 31.5 us  [all_gather(): pl.pallas_call(kernel, out_shape=[jax.ShapeDtypeStruct((BLK,) + s.shape,...]
    pallas_call x1, Pallas kernels: 8.32 us -> 13.5 us  [draft_and_append(): pl.pallas_call(draft_kernel, out_shape=[jax.ShapeDtypeStruct(layer.shape,...]
    pallas_call x2, Pallas kernels: 18.4 us -> 23.5 us  [over_column(): pl.pallas_call(column_kernel(exchange), out_shape=jax.ShapeDtypeStruct(sh...]
    unnamed x27 -> x17, local copies, waits for them, and re-layouts: 7.32 us -> 2.88 us
where the time goes in v4:
time: 177 us; the launch traced here: 176 us
  Pallas kernels  158 us (89%)
  matrix products  13.6 us (8%)
  local copies, waits for them, and re-layouts  2.9 us (2%)
    pallas_call x1, Pallas kernels, attend_and_reduce(): pl.pallas_call(kernel, out_shape=[jax.ShapeDtypeStruct((TREE, WIDTH), jnp...  51.2 us
    pallas_call x1, Pallas kernels, prepare(): pl.pallas_call(kernel, out_shape=[jax.ShapeDtypeStruct((BLK,) + shard.sha...  38.1 us
    pallas_call x1, Pallas kernels, all_gather(): pl.pallas_call(kernel, out_shape=[jax.ShapeDtypeStruct((BLK,) + s.shape,...  31.5 us
    pallas_call x2, Pallas kernels, over_column(): pl.pallas_call(column_kernel(exchange), out_shape=jax.ShapeDtypeStruct(sh...  23.5 us
    pallas_call x1, Pallas kernels, draft_and_append(): pl.pallas_call(draft_kernel, out_shape=[jax.ShapeDtypeStruct(layer.shape,...  13.5 us
    dot_general x2, matrix products, dot_t(): lax.dot_general(left, right, (((1,), (1,)), ((), ())), preferred_element_...  8.1 us
    dot_general x1, matrix products, on_device(): feedforward = jnp.dot(hidden, full_down, preferred_element_type=jnp.float32)  5.34 us

profile of v4, /device:TPU:2, one launch (start us, length us, event | category | flops | bytes accessed | tf_op | source)
XLA Modules:
  0.0 175.9 jit_solution(8160294290260163525)
XLA Ops:
  0.6 0.0 copy-start
  0.7 1.0 copy-done
  1.6 0.1 fusion.5.spread_ref
  1.7 38.1 %prepare.1 = (bf16[32,120,1280]{2,1,0:T(8,128)(2,1)}, bf16[4,320,1280]{2,1,0:T(8,128)(2,1)}, bf16[48,1280]{1,0:T(8,128)(2,1)}, s32[10,128]{1,0:T(8,128)}, s32[4,...) custom-call(bf16[120,1280]{1,0:T(8,128)(2,1)} %bitcast.32, bf16[320,1280]{1,0:T(8,128)(2,1)} %bitcast.30, ...), custom_call_target="tpu_custom_call" | custom-call | tf_op jit(solution)/shard_map/prepare/pallas_call | solution.py:405
  39.8 0.0 copy-start.7
  39.8 0.0 copy-start.1
  39.8 0.0 copy-start.2
  39.9 0.0 copy-start.3
  39.9 0.0 copy-start.4
  39.9 6.9 %convolution_convert_fusion.proj_ref = bf16[48,3840]{1,0:T(8,128)(2,1)S(1)} fusion(bf16[48,1280]{1,0:T(8,128)(2,1)} %get-tuple-element.19, bf16[3840,1280]{1,0:T(8,128)(2,1)} %bitcast.23), kind=kOutput, calls=%fused_computation | convolution fusion | flops 472043520 | bytes 10321920 | tf_op jit(solution)/shard_map/dot_general | solution.py:33
  46.8 0.0 copy-done.7
  46.8 0.1 convolution_convert_fusion.1
  47.0 0.7 pad_maximum_fusion.refs_0_
  47.7 31.5 %gather_query.1 = (bf16[32,64,1280]{2,1,0:T(8,128)(2,1)}, bf16[32,40,1280]{2,1,0:T(8,128)(2,1)}) custom-call(bf16[64,1280]{1,0:T(8,128)(2,1)} %pad_maximum_fusion.refs_0_, bf16[40,1280]{1,0:T(8,128)(2,1)} %bitcast.33), custom_call_target="tpu_custom_call" | custom-call | tf_op jit(solution)/shard_map/gather_query/pallas_call | solution.py:281
  79.2 0.0 copy-done.1
  79.2 0.0 copy-done.2
  79.2 0.0 copy-start.6
  79.2 51.2 %attend_and_reduce.1 = (bf16[48,1280]{1,0:T(8,128)(2,1)S(1)}, bf16[32,40,1280]{2,1,0:T(8,128)(2,1)}, bf16[32,40,1280]{2,1,0:T(8,128)(2,1)}, bf16[32,40,1280]{2,1,0:T(8,128)(2,1)}) custom-call(s32[10,128]{1,0:T(8,128)S(1)} %copy-done.4, bf16[32,64,1280]{2,1,0:T(8,128)(2,1)} %get-tuple-element.22.query_ref.fresh_ref, bf16[1,2,2048,1280]{3,2,1,0:T(8,128)(2,1)} %cache_ref.3, ...), custom_call_target="tpu_custom_call" | custom-call | tf_op jit(solution)/shard_map/attend_and_reduce/pallas_call | solution.py:864
  130.4 1.2 multiply_reduce_fusion
  131.7 5.3 %fusion.block = bf16[48,1280]{1,0:T(8,128)(2,1)} fusion(f32[48,1280]{1,0:T(8,128)S(1)} %get-tuple-element.36, bf16[1280,1280]{1,0:T(8,128)(2,1)} %bitcast.25, bf16[1280,1280]{1,0:T(8,128)(2,1)} %bitcast.24, f32[48]{0:T(128)S(1)} %add_rsqrt_fusion), kind=kOutput, calls=%fused_computation.3 | convolution fusion | flops 315371520 | bytes 6922432 | tf_op jit(solution)/shard_map/dot_general | solution.py:999
  137.0 11.0 %gather_rows.1 = bf16[4,48,1280]{2,1,0:T(8,128)(2,1)} custom-call(bf16[48,1280]{1,0:T(8,128)(2,1)} %fusion.block), custom_call_target="tpu_custom_call" | custom-call | tf_op jit(solution)/shard_map/gather_rows/pallas_call | solution.py:928
  148.0 13.5 %draft_and_append.1 = (bf16[192,1280]{1,0:T(8,128)(2,1)}, bf16[1,2,2048,1280]{3,2,1,0:T(8,128)(2,1)}) custom-call(s32[4,128]{1,0:T(4,128)} %get-tuple-element.28.tables, bf16[32,64,1280]{2,1,0:T(8,128)(2,1)} %get-tuple-element.22.query_ref.fresh_ref, bf16[1,2,2048,1280]{3,2,1,0:T(8,128)(2,1)} %cache_ref.3, bf16[192,1280]{1,0:T(8,128)(2,1)} %bitcast.29, ...), custom_call_target="tpu_custom_call" | custom-call | tf_op jit(solution)/shard_map/draft_and_append/pallas_call | solution.py:502
  161.5 12.6 %return_rows.1 = bf16[4,48,1280]{2,1,0:T(8,128)(2,1)} custom-call(bf16[4,48,1280]{2,1,0:T(8,128)(2,1)} %bitcast.31), custom_call_target="tpu_custom_call" | custom-call | tf_op jit(solution)/shard_map/return_rows/pallas_call | solution.py:928
  174.1 1.8 %copy.16 = bf16[4,48,1280]{2,1,0:T(8,128)(2,1)} copy(bf16[4,48,1280]{2,1,0:T(8,128)(2,1)} %return_rows.1) | data formatting | bytes 983040
  (10 shorter events, 0.0 us)
Async XLA Ops:
  0.6 1.0 copy-start
  39.8 7.0 %copy-start.7 = (bf16[16,48]{1,0:T(8,128)(2,1)S(1)}, bf16[16,48]{1,0:T(8,128)(2,1)}, u32[]{:S(2)}) copy-start(bf16[16,48]{1,0:T(8,128)(2,1)} %get-tuple-element.21) | copy-start | bytes 4612
  39.8 39.4 %copy-start.1 = (bf16[1280,40]{0,1:T(8,128)(2,1)S(1)}, bf16[1280,40]{0,1:T(8,128)(2,1)}, u32[]{:S(2)}) copy-start(bf16[1280,40]{0,1:T(8,128)(2,1)} %param.20) | copy-start | bytes 307204
  39.8 39.4 %copy-start.2 = (bf16[40,1280]{1,0:T(8,128)(2,1)S(1)}, bf16[40,1280]{1,0:T(8,128)(2,1)}, u32[]{:S(2)}) copy-start(bf16[40,1280]{1,0:T(8,128)(2,1)} %refs_1_.1) | copy-start | bytes 307204
  39.9 39.4 %copy-start.3 = (f32[48,48]{1,0:T(8,128)S(1)}, f32[48,48]{1,0:T(8,128)}, u32[]{:S(2)}) copy-start(f32[48,48]{1,0:T(8,128)} %get-tuple-element.23.marks_ref) | copy-start | bytes 27652
  39.9 39.4 %copy-start.4 = (s32[10,128]{1,0:T(8,128)S(1)}, s32[10,128]{1,0:T(8,128)}, u32[]{:S(2)}) copy-start(s32[10,128]{1,0:T(8,128)} %get-tuple-element.18.tables_ref) | copy-start | bytes 15364
  79.2 51.2 %copy-start.5 = (bf16[32,40,1280]{2,1,0:T(8,128)(2,1)S(1)}, bf16[32,40,1280]{2,1,0:T(8,128)(2,1)}, u32[]{:S(2)}) copy-start(bf16[32,40,1280]{2,1,0:T(8,128)(2,1)} %get-tuple-element.25) | copy-start | bytes 9830404
  79.2 51.2 %copy-start.6 = (bf16[48,1280]{1,0:T(8,128)(2,1)S(1)}, bf16[48,1280]{1,0:T(8,128)(2,1)}, u32[]{:S(2)}) copy-start(bf16[48,1280]{1,0:T(8,128)(2,1)} %x_ref.1) | copy-start | bytes 368644

commit v5 on v4

--- a/solution.py
+++ b/solution.py
@@ -94,7 +94,7 @@
     return put
 
 
-def gather_steps(spot, shard, view, ssem, rsem, lsem, cut):
+def gather_steps(spot, shard, view, ssem, rsem, lsem, cut, ready=None):
     sent = {}
     send = sender(sent, ssem, rsem, GATHER)
 
@@ -103,6 +103,24 @@
         if half is not None:
             src, dst = cut(src, half), cut(dst, half)
         send(event, src, dst, who)
+
+    left_over = list(range(16))
+
+    def done(*slots):
+        if ready is not None:
+            for slot in slots:
+                ready(slot)
+
+    def from_sibling(*events):
+        for k in events:
+            left_over.remove(k)
+            sent[f"S{k}"].wait_recv()
+            a, b = ROWSLOT[k % 4][0], (0, -1, 1, 2)[k // 4]
+            done(1 - spot.core + 2 * spot.chip(b, a))
+
+    def early(*events):
+        if ready is not None:
+            from_sibling(*events)
 
     right, left = spot.at(1, 0), spot.at(-1, 0)
     up, down = spot.at(0, 1), spot.at(0, -1)
@@ -124,6 +142,8 @@
         put(f"D{k}", view(slot), slot, up)
         put(f"U{k}", view(slot), slot, down)
         put(f"S{k}", view(slot), slot, spot.sibling)
+        done(slot)
+        early(k - 1)
         yield
 
     def column(k):
@@ -136,8 +156,10 @@
         sent[f"U{k}"].wait_recv()
         put(f"PB{k}", view(slot), slot, down, 1)
         put(f"S{8 + k}", view(slot), slot, spot.sibling)
+        done(spot.at(a, -1), slot)
 
     column(0)
+    early(2)
     yield
     sent["OA"].wait_recv()
     sent["OB"].wait_recv()
@@ -145,18 +167,22 @@
     put("D3", view(slot), slot, up)
     put("U3", view(slot), slot, down)
     put("S3", view(slot), slot, spot.sibling)
+    done(slot)
+    early(4, 8)
     yield
     for k in (1, 2, 3):
         column(k)
+        early(*((3,), (5, 9), (6, 10))[k - 1])
         yield
     for k in range(4):
         slot = spot.at(ROWSLOT[k][0], 2)
         sent[f"PA{k}"].wait_recv()
         sent[f"PB{k}"].wait_recv()
         put(f"S{12 + k}", view(slot), slot, spot.sibling)
+        done(slot)
+        early(*((7, 11) if k == 0 else (11 + k,)))
         yield
-    for k in range(16):
-        sent[f"S{k}"].wait_recv()
+    from_sibling(*list(left_over))
     local.wait()
     for event in GATHER:
         sent[event].wait_send()
@@ -175,8 +201,8 @@
         steps = alive
 
 
-def row_halves(rows):
-    first = ((rows // 2) + 7) // 8 * 8
+def row_halves(rows, tile):
+    first = ((rows // 2) + tile - 1) // tile * tile
 
     def cut(ref, half):
         return ref.at[pl.ds(0, first)] if half == 0 else ref.at[pl.ds(first, rows - first)]
@@ -184,7 +210,7 @@
     return cut
 
 
-def gather_all(spot, ins, outs, ssem, rsem, lsem, cuts=None):
+def gather_all(spot, ins, outs, ssem, rsem, lsem, cuts=None, ready=None):
     count = len(GATHER)
     steps = []
     for i, (shard, out) in enumerate(zip(ins, outs)):
@@ -200,7 +226,19 @@
                     lambda e, at=at: ssem.at[at + e],
                     lambda e, at=at: rsem.at[at + e],
                     lsem.at[len(steps)],
-                    row_halves(rows),
+                    row_halves(rows, 16 if ready else 8),
+                    (lambda slot: None) if ready else None,
+                )
+                if ready is None or first + rows < shard.shape[0]
+                else gather_steps(
+                    spot,
+                    shard.at[piece],
+                    lambda slot, out=out, piece=piece: out.at[slot, piece],
+                    lambda e, at=at: ssem.at[at + e],
+                    lambda e, at=at: rsem.at[at + e],
+                    lsem.at[len(steps)],
+                    row_halves(rows, 16),
+                    ready,
                 )
             )
             first += rows
@@ -377,22 +415,28 @@
 def prepare(shard, patch, tree_input, page_row, length_row, leaf_row, parent_row, pool_pages):
     def kernel(
         shard_ref, patch_ref, x_ref, page_ref, length_ref, leaf_ref, parent_ref,
-        full_ref, full_patch_ref, normed_ref, steps_ref, pages_ref, marks_ref, picker_ref,
-        *scratch,
+        full_patch_ref, projected_ref, pack_ref, steps_ref, pages_ref, marks_ref,
+        full_ref, normed, parts, joined, *scratch,
     ):
         spot = Spot()
+        columns = shard_ref.shape[0]
         greet_plane(spot, True)
-        steps = gather_all(spot, [shard_ref], [full_ref], *scratch[:3], {0: QKV_CUTS})
+
+        def project(slot):
+            parts[slot, :, pl.ds(0, columns)] = dot_t(normed[...], full_ref[slot])
+
+        steps = gather_all(
+            spot, [shard_ref], [full_ref], *scratch[:3], {0: QKV_CUTS}, project
+        )
         steps.append(column_steps(spot, patch_ref, full_patch_ref, *scratch[3:]))
-        for _ in range(3):
-            for one in steps:
-                next(one)
-        normed_ref[...] = rms_rows(x_ref[...])
+        for one in steps:
+            next(one)
+        normed[...] = rms_rows(x_ref[...])
+        parts[spot.me, :, pl.ds(0, columns)] = dot_t(normed[...], shard_ref[...])
         leaf = jnp.sum(
             jnp.where(iota(leaf_ref.shape, 1) == spot.me, leaf_ref[...], 0), axis=1, keepdims=True
         )
         marks_ref[...], picker = tree_marks(parent_ref[...], leaf)
-        picker_ref[...] = picker.astype(jnp.bfloat16)
         in_order, as_they_lie = page_tables(
             page_ref[...], length_ref[...], leaf_ref[...], spot.me, pool_pages
         )
@@ -401,27 +445,46 @@
         for k, row in enumerate(as_they_lie):
             pages_ref[pl.ds(k, 1), :] = row
         run_all(steps)
+        for slot in range(BLK):
+            joined[:, pl.ds(columns * slot, columns)] = parts[slot, :, pl.ds(0, columns)]
+        projected_ref[...] = joined[...].astype(jnp.bfloat16)
+        pack_ref[pl.ds(0, TREE), :] = projected_ref[:, pl.ds(0, WIDTH)]
+        picked = jnp.dot(
+            picker.astype(jnp.bfloat16),
+            projected_ref[:, pl.ds(WIDTH, 2 * WIDTH)],
+            preferred_element_type=jnp.float32,
+        )
+        pack_ref[pl.ds(TREE, 16), :] = jnp.concatenate(
+            [picked[:8, :WIDTH], picked[:8, WIDTH:]], axis=0
+        ).astype(jnp.bfloat16)
 
     return pl.pallas_call(
         kernel,
         out_shape=[
-            jax.ShapeDtypeStruct((BLK,) + shard.shape, shard.dtype),
             jax.ShapeDtypeStruct((4,) + patch.shape, patch.dtype),
-            jax.ShapeDtypeStruct(tree_input.shape, jnp.bfloat16),
+            jax.ShapeDtypeStruct((TREE, 3 * WIDTH), jnp.bfloat16),
+            jax.ShapeDtypeStruct((TREE + 16, WIDTH), jnp.bfloat16),
             jax.ShapeDtypeStruct((10, 128), jnp.int32),
             jax.ShapeDtypeStruct((4, 128), jnp.int32),
             jax.ShapeDtypeStruct((TREE, TREE), jnp.float32),
-            jax.ShapeDtypeStruct((16, TREE), jnp.bfloat16),
         ],
         in_specs=[VMEM] * 7,
-        out_specs=[ANY, ANY] + [VMEM] * 5,
-        scratch_shapes=gather_sems(len(QKV_CUTS))
+        out_specs=[ANY] + [VMEM] * 5,
+        scratch_shapes=[
+            pltpu.VMEM((BLK,) + shard.shape, shard.dtype),
+            pltpu.VMEM(tree_input.shape, jnp.bfloat16),
+            pltpu.VMEM((BLK, TREE, 128), jnp.float32),
+            pltpu.VMEM((TREE, 3 * WIDTH), jnp.float32),
+        ]
+        + gather_sems(len(QKV_CUTS))
         + [
             pltpu.SemaphoreType.DMA((len(COLUMN),)),
             pltpu.SemaphoreType.DMA((len(COLUMN),)),
             pltpu.SemaphoreType.DMA,
         ],
-        compiler_params=pltpu.CompilerParams(collective_id=1, has_side_effects=True),
+        compiler_params=pltpu.CompilerParams(
+            collective_id=1, has_side_effects=True
+        ),
         name="prepare",
     )(shard, patch, tree_input, page_row, length_row, leaf_row, parent_row)
 
@@ -871,7 +934,6 @@
         compiler_params=pltpu.CompilerParams(
             collective_id=collective_id,
             has_side_effects=True,
-            vmem_limit_bytes=52 * 1024 * 1024,
         ),
         name="attend_and_reduce",
     )(tables, gathered, cache, projected, marks, spread, *shards)
@@ -962,14 +1024,9 @@
     draft_mine = lax.dynamic_index_in_dim(
         w_draft.transpose(0, 2, 1), lax.axis_index("req"), 0, keepdims=False
     )
-    qkv, patch, normed, tables, pages, marks, picker = prepare(
+    patch, projected, pack, tables, pages, marks = prepare(
         w_qkv.T, w_patch.T, tree_input, page_table, lengths, accept_leaf, parents, pool_pages
     )
-    projected = dot_t(normed, qkv.reshape(3 * width, width)).astype(jnp.bfloat16)
-    send_rows = jnp.dot(
-        picker[:8], projected[:, width:], preferred_element_type=jnp.float32
-    ).astype(jnp.bfloat16)
-    pack = jnp.concatenate([projected[:, :width], send_rows[:, :width], send_rows[:, width:]])
     gathered, *full_early = all_gather(
         [pack, w_out.T, ],
         {0: QUERY_CUTS},

time: 177 us -> 176 us (level)
  matrix products: 13.6 us -> 8.54 us
  Pallas kernels: 158 us -> 161 us
    dot_general x2 -> x1, matrix products: 8.1 us -> 3.2 us  [dot_t(): lax.dot_general(left, right, (((1,), (1,)), ((), ())), preferred_element_...]
    pallas_call x1, Pallas kernels: 38.1 us -> 40.6 us  [prepare(): pl.pallas_call(kernel, out_shape=[jax.ShapeDtypeStruct((4,) + patch.shape...]
where the time goes in v5:
time: 176 us; the launch traced here: 175 us
  Pallas kernels  161 us (91%)
  matrix products  8.54 us (5%)
  local copies, waits for them, and re-layouts  3.48 us (2%)
    pallas_call x1, Pallas kernels, attend_and_reduce(): pl.pallas_call(kernel, out_shape=[jax.ShapeDtypeStruct((TREE, WIDTH), jnp...  52.9 us
    pallas_call x1, Pallas kernels, prepare(): pl.pallas_call(kernel, out_shape=[jax.ShapeDtypeStruct((4,) + patch.shape...  40.6 us
    pallas_call x1, Pallas kernels, all_gather(): pl.pallas_call(kernel, out_shape=[jax.ShapeDtypeStruct((BLK,) + s.shape,...  30.7 us
    pallas_call x2, Pallas kernels, over_column(): pl.pallas_call(column_kernel(exchange), out_shape=jax.ShapeDtypeStruct(sh...  23.3 us
    pallas_call x1, Pallas kernels, draft_and_append(): pl.pallas_call(draft_kernel, out_shape=[jax.ShapeDtypeStruct(layer.shape,...  13.5 us
    dot_general x1, matrix products, on_device(): feedforward = jnp.dot(hidden, full_down, preferred_element_type=jnp.float32)  5.34 us

profile of v5, /device:TPU:2, one launch (start us, length us, event | category | flops | bytes accessed | tf_op | source)
XLA Modules:
  0.0 174.6 jit_solution(1572679282467461554)
XLA Ops:
  0.6 0.0 copy-start
  0.7 1.0 copy-done
  1.6 0.6 dynamic-slice_bitcast_fusion.refs_2_
  2.3 0.8 fusion.5.spread_ref
  3.1 40.6 %prepare.1 = (bf16[4,320,1280]{2,1,0:T(8,128)(2,1)}, bf16[48,3840]{1,0:T(8,128)(2,1)}, bf16[64,1280]{1,0:T(8,128)(2,1)}, s32[10,128]{1,0:T(8,128)}, s32[4,128]{1,0:T(4,128)}, /*index=5*/f32[48,48]{1,0:T(8,128)}) custom-call(bf16[120,1280]{1,0:T(8,128)(2,1)} %bitcast.27, bf16[320,1280]{1,0:T(8,128)(2,1)} %bitcast.25, bf16[48,1280]{1,0:T(8,128)(2,1)} %x_ref.1, ...), custom_call_target="tpu_custom_call" | custom-call | tf_op jit(solution)/shard_map/prepare/pallas_call | solution.py:461
  43.7 30.7 %gather_query.1 = (bf16[32,64,1280]{2,1,0:T(8,128)(2,1)}, bf16[32,40,1280]{2,1,0:T(8,128)(2,1)}) custom-call(bf16[64,1280]{1,0:T(8,128)(2,1)} %get-tuple-element.18.refs_0_, bf16[40,1280]{1,0:T(8,128)(2,1)} %bitcast.28), custom_call_target="tpu_custom_call" | custom-call | tf_op jit(solution)/shard_map/gather_query/pallas_call | solution.py:319
  74.4 0.0 copy-start.1
  74.4 52.9 %attend_and_reduce.1 = (bf16[48,1280]{1,0:T(8,128)(2,1)}, bf16[32,40,1280]{2,1,0:T(8,128)(2,1)}, bf16[32,40,1280]{2,1,0:T(8,128)(2,1)}, bf16[32,40,1280]{2,1,0:T(8,128)(2,1)}) custom-call(s32[10,128]{1,0:T(8,128)} %get-tuple-element.17.tables_ref, bf16[32,64,1280]{2,1,0:T(8,128)(2,1)} %get-tuple-element.19.query_ref.fresh_ref, ...), custom_call_target="tpu_custom_call" | custom-call | tf_op jit(solution)/shard_map/attend_and_reduce/pallas_call | solution.py:927
  127.3 0.0 copy-done.1
  127.4 3.2 %multiply_reduce_fusion = (f32[48]{0:T(128)S(1)}, f32[48,1280]{1,0:T(8,128)S(1)}) fusion(bf16[48,1280]{1,0:T(8,128)(2,1)} %get-tuple-element.22, bf16[1280,1280]{1,0:T(8,128)(2,1)} %bitcast.21, bf16[48,1280]{1,0:T(8,128)(2,1)S(1)} %copy-done.1), kind=kOutput, calls=%fused_computation.19 | convolution fusion | flops 157777872 | bytes 3768512 | tf_op jit(solution)/shard_map/dot_general | solution.py:33
  130.6 5.3 %fusion.block = bf16[48,1280]{1,0:T(8,128)(2,1)} fusion(f32[48,1280]{1,0:T(8,128)S(1)} %get-tuple-element.32, bf16[1280,1280]{1,0:T(8,128)(2,1)} %bitcast.20, bf16[1280,1280]{1,0:T(8,128)(2,1)} %bitcast.19, f32[48]{0:T(128)S(1)} %add_rsqrt_fusion), kind=kOutput, calls=%fused_computation.1 | convolution fusion | flops 315371520 | bytes 6922432 | tf_op jit(solution)/shard_map/dot_general | solution.py:1056
  135.9 11.1 %gather_rows.1 = bf16[4,48,1280]{2,1,0:T(8,128)(2,1)} custom-call(bf16[48,1280]{1,0:T(8,128)(2,1)} %fusion.block), custom_call_target="tpu_custom_call" | custom-call | tf_op jit(solution)/shard_map/gather_rows/pallas_call | solution.py:990
  147.0 13.5 %draft_and_append.1 = (bf16[192,1280]{1,0:T(8,128)(2,1)}, bf16[1,2,2048,1280]{3,2,1,0:T(8,128)(2,1)}) custom-call(s32[4,128]{1,0:T(4,128)} %get-tuple-element.26.tables, bf16[32,64,1280]{2,1,0:T(8,128)(2,1)} %get-tuple-element.19.query_ref.fresh_ref, bf16[1,2,2048,1280]{3,2,1,0:T(8,128)(2,1)} %cache_ref.3, bf16[192,1280]{1,0:T(8,128)(2,1)} %bitcast.24, ...), custom_call_target="tpu_custom_call" | custom-call | tf_op jit(solution)/shard_map/draft_and_append/pallas_call | solution.py:565
  160.5 12.2 %return_rows.1 = bf16[4,48,1280]{2,1,0:T(8,128)(2,1)} custom-call(bf16[4,48,1280]{2,1,0:T(8,128)(2,1)} %bitcast.26), custom_call_target="tpu_custom_call" | custom-call | tf_op jit(solution)/shard_map/return_rows/pallas_call | solution.py:990
  172.7 1.8 %copy.16 = bf16[4,48,1280]{2,1,0:T(8,128)(2,1)} copy(bf16[4,48,1280]{2,1,0:T(8,128)(2,1)} %return_rows.1) | data formatting | bytes 983040
  (2 shorter events, 0.0 us)
Async XLA Ops:
  0.6 1.0 copy-start
  74.4 53.0 %copy-start.1 = (bf16[48,1280]{1,0:T(8,128)(2,1)S(1)}, bf16[48,1280]{1,0:T(8,128)(2,1)}, u32[]{:S(2)}) copy-start(bf16[48,1280]{1,0:T(8,128)(2,1)} %x_ref.1) | copy-start | bytes 368644

commit v6 on v5

--- a/solution.py
+++ b/solution.py
@@ -724,7 +724,7 @@
 
 
 PAUSES = (3, 6, 9, 12, 14)
-ADVANCES = (0, 6, 10, 14, 18, 22)
+ADVANCES = (8, 12, 16, 18, 20, 22)
 
 
 def split_stats(stats):

time: 176 us -> 176 us (level)
  no operation moved by 1% of the time
where the time goes in v6:
time: 176 us; the launch traced here: 174 us
  Pallas kernels  161 us (91%)
  matrix products  8.54 us (5%)
  local copies, waits for them, and re-layouts  3.48 us (2%)
    pallas_call x1, Pallas kernels, attend_and_reduce(): pl.pallas_call(kernel, out_shape=[jax.ShapeDtypeStruct((TREE, WIDTH), jnp...  52.9 us
    pallas_call x1, Pallas kernels, prepare(): pl.pallas_call(kernel, out_shape=[jax.ShapeDtypeStruct((4,) + patch.shape...  40.6 us
    pallas_call x1, Pallas kernels, all_gather(): pl.pallas_call(kernel, out_shape=[jax.ShapeDtypeStruct((BLK,) + s.shape,...  30.7 us
    pallas_call x2, Pallas kernels, over_column(): pl.pallas_call(column_kernel(exchange), out_shape=jax.ShapeDtypeStruct(sh...  21.8 us
    pallas_call x1, Pallas kernels, draft_and_append(): pl.pallas_call(draft_kernel, out_shape=[jax.ShapeDtypeStruct(layer.shape,...  14.5 us
    dot_general x1, matrix products, on_device(): feedforward = jnp.dot(hidden, full_down, preferred_element_type=jnp.float32)  5.34 us

profile of v6, /device:TPU:2, one launch (start us, length us, event | category | flops | bytes accessed | tf_op | source)
XLA Modules:
  0.0 174.1 jit_solution(9907310621666036358)
XLA Ops:
  0.6 0.0 copy-start
  0.7 1.0 copy-done
  1.6 0.6 dynamic-slice_bitcast_fusion.refs_2_
  2.3 0.8 fusion.5.spread_ref
  3.1 40.6 %prepare.1 = (bf16[4,320,1280]{2,1,0:T(8,128)(2,1)}, bf16[48,3840]{1,0:T(8,128)(2,1)}, bf16[64,1280]{1,0:T(8,128)(2,1)}, s32[10,128]{1,0:T(8,128)}, s32[4,128]{1,0:T(4,128)}, /*index=5*/f32[48,48]{1,0:T(8,128)}) custom-call(bf16[120,1280]{1,0:T(8,128)(2,1)} %bitcast.27, bf16[320,1280]{1,0:T(8,128)(2,1)} %bitcast.25, bf16[48,1280]{1,0:T(8,128)(2,1)} %x_ref.1, ...), custom_call_target="tpu_custom_call" | custom-call | tf_op jit(solution)/shard_map/prepare/pallas_call | solution.py:461
  43.7 30.7 %gather_query.1 = (bf16[32,64,1280]{2,1,0:T(8,128)(2,1)}, bf16[32,40,1280]{2,1,0:T(8,128)(2,1)}) custom-call(bf16[64,1280]{1,0:T(8,128)(2,1)} %get-tuple-element.18.refs_0_, bf16[40,1280]{1,0:T(8,128)(2,1)} %bitcast.28), custom_call_target="tpu_custom_call" | custom-call | tf_op jit(solution)/shard_map/gather_query/pallas_call | solution.py:319
  74.4 0.0 copy-start.1
  74.4 52.9 %attend_and_reduce.1 = (bf16[48,1280]{1,0:T(8,128)(2,1)}, bf16[32,40,1280]{2,1,0:T(8,128)(2,1)}, bf16[32,40,1280]{2,1,0:T(8,128)(2,1)}, bf16[32,40,1280]{2,1,0:T(8,128)(2,1)}) custom-call(s32[10,128]{1,0:T(8,128)} %get-tuple-element.17.tables_ref, bf16[32,64,1280]{2,1,0:T(8,128)(2,1)} %get-tuple-element.19.query_ref.fresh_ref, ...), custom_call_target="tpu_custom_call" | custom-call | tf_op jit(solution)/shard_map/attend_and_reduce/pallas_call | solution.py:927
  127.3 0.0 copy-done.1
  127.4 3.2 %multiply_reduce_fusion = (f32[48]{0:T(128)S(1)}, f32[48,1280]{1,0:T(8,128)S(1)}) fusion(bf16[48,1280]{1,0:T(8,128)(2,1)} %get-tuple-element.22, bf16[1280,1280]{1,0:T(8,128)(2,1)} %bitcast.21, bf16[48,1280]{1,0:T(8,128)(2,1)S(1)} %copy-done.1), kind=kOutput, calls=%fused_computation.19 | convolution fusion | flops 157777872 | bytes 3768512 | tf_op jit(solution)/shard_map/dot_general | solution.py:33
  130.6 5.3 %fusion.block = bf16[48,1280]{1,0:T(8,128)(2,1)} fusion(f32[48,1280]{1,0:T(8,128)S(1)} %get-tuple-element.32, bf16[1280,1280]{1,0:T(8,128)(2,1)} %bitcast.20, bf16[1280,1280]{1,0:T(8,128)(2,1)} %bitcast.19, f32[48]{0:T(128)S(1)} %add_rsqrt_fusion), kind=kOutput, calls=%fused_computation.1 | convolution fusion | flops 315371520 | bytes 6922432 | tf_op jit(solution)/shard_map/dot_general | solution.py:1056
  135.9 11.0 %gather_rows.1 = bf16[4,48,1280]{2,1,0:T(8,128)(2,1)} custom-call(bf16[48,1280]{1,0:T(8,128)(2,1)} %fusion.block), custom_call_target="tpu_custom_call" | custom-call | tf_op jit(solution)/shard_map/gather_rows/pallas_call | solution.py:990
  146.9 14.5 %draft_and_append.1 = (bf16[192,1280]{1,0:T(8,128)(2,1)}, bf16[1,2,2048,1280]{3,2,1,0:T(8,128)(2,1)}) custom-call(s32[4,128]{1,0:T(4,128)} %get-tuple-element.26.tables, bf16[32,64,1280]{2,1,0:T(8,128)(2,1)} %get-tuple-element.19.query_ref.fresh_ref, bf16[1,2,2048,1280]{3,2,1,0:T(8,128)(2,1)} %cache_ref.3, bf16[192,1280]{1,0:T(8,128)(2,1)} %bitcast.24, ...), custom_call_target="tpu_custom_call" | custom-call | tf_op jit(solution)/shard_map/draft_and_append/pallas_call | solution.py:565
  161.4 10.9 %return_rows.1 = bf16[4,48,1280]{2,1,0:T(8,128)(2,1)} custom-call(bf16[4,48,1280]{2,1,0:T(8,128)(2,1)} %bitcast.26), custom_call_target="tpu_custom_call" | custom-call | tf_op jit(solution)/shard_map/return_rows/pallas_call | solution.py:990
  172.3 1.8 %copy.16 = bf16[4,48,1280]{2,1,0:T(8,128)(2,1)} copy(bf16[4,48,1280]{2,1,0:T(8,128)(2,1)} %return_rows.1) | data formatting | bytes 983040
  (2 shorter events, 0.0 us)
Async XLA Ops:
  0.6 1.0 copy-start
  74.4 53.0 %copy-start.1 = (bf16[48,1280]{1,0:T(8,128)(2,1)S(1)}, bf16[48,1280]{1,0:T(8,128)(2,1)}, u32[]{:S(2)}) copy-start(bf16[48,1280]{1,0:T(8,128)(2,1)} %x_ref.1) | copy-start | bytes 368644
